TPU v7x, 256 devices: a whole 4x4x8 slice. The times are simulated.
256 devices in a mesh: wide: 128 (over x, y, z_lo, core), head: 2 (over z_hi).
Axes of the slice: x: 4, y: 4, z: 8 (z_hi: 2, z_lo: 4; z = z_hi * 4 + z_lo), core: 2. Of those that a mesh axis runs over, the one named last changes fastest.
Arguments:
- branch_query: bfloat16 [512, 8192], P('wide', 'head'), may hold values from -6 to 6
- key_new: bfloat16 [512, 1024], P('wide', 'head'), may hold values from -6 to 6
- value_new: bfloat16 [512, 1024], P('wide', 'head'), may hold values from -6 to 6
- pool_pages: bfloat16 [2, 8192, 16, 1024], P(None, 'wide', None, 'head'), may hold values from -6 to 6
- page_table: int32 [512, 16], P('wide'), may hold values from 0 to 63, as said below
- tail_length: int32 [512], P('wide'), may hold values from 1 to 256
- parent_row: int32 [512], P('wide'), may hold values from 0 to 511, as said below
- residual: bfloat16 [512, 8192], P(('wide', 'head')), may hold values from -6 to 6
- norm_gain: float32 [8192], replicated, may hold values from 0.5 to 1.5
- gate_blocks: bfloat16 [128, 32, 128, 128], P('wide'), may hold values from -0.09375 to 0.09375
- up_blocks: bfloat16 [128, 32, 128, 128], P('wide'), may hold values from -0.09375 to 0.09375
- gate_up_keep: int32 [128, 32], P('wide'), may hold values from 0 to 63, as said below
- gate_scale: float32 [128, 32], P('wide'), may hold values from 0.5 to 2
- up_scale: float32 [128, 32], P('wide'), may hold values from 0.5 to 2
- down_blocks: bfloat16 [128, 32, 128, 128], P('wide'), may hold values from -0.0625 to 0.0625
- down_keep: int32 [128, 32], P('wide'), may hold values from 0 to 63, as said below
- down_scale: float32 [128, 32], P('wide'), may hold values from 0.5 to 2
Outputs:
- layer_out: bfloat16 [512, 8192], P(('wide', 'head'))
Inputs may be any that keep to these rules, and one draw needn't show every extreme that they name: parent_row never falls with the branch index, and parent_row[b] <= b and parent_row[b] > b - 4. `page_table`: the entries of the 4 rows held by one index of wide name each of that index's 64 pages once. `gate_up_keep`: each row names 32 different blocks. `down_keep`: each row names 32 different blocks.
All inputs are finite; a program needn't handle non-finite values.
Results may differ from a plain program's by a relative error of at most 0.017.
Values may be sent and summed in bfloat16 or wider, within the bound.
A program may use at most 64 MiB of HBM per device.

v0:
```python
import math

import jax
import jax.numpy as jnp
from jax import lax
from jax.sharding import PartitionSpec as P

HD = 128
BLK = 128


def shifted(block, axis, distance):
    devices = range(lax.axis_size(axis))
    route = [(i - distance, i) for i in devices if i - distance in devices]
    return lax.ppermute(block, axis, route)


def attend(branch_query, key_new, value_new, child_tails, child_length):
    row_count = branch_query.shape[0]
    groups = key_new.shape[1] // HD
    per_group = branch_query.shape[1] // (groups * HD)
    tail_size = child_tails.shape[2]
    queries = branch_query.reshape(row_count, groups, per_group, HD)
    tail_keys = child_tails[0].reshape(row_count, tail_size, groups, HD)
    tail_values = child_tails[1].reshape(row_count, tail_size, groups, HD)
    own_keys = key_new.reshape(row_count, groups, HD)
    own_values = value_new.reshape(row_count, groups, HD)
    factor = 1.0 / math.sqrt(HD)
    tail_scores = (
        jnp.einsum("rgjd,rtgd->rgjt", queries, tail_keys, preferred_element_type=jnp.float32)
        * factor
    )
    own_scores = (
        jnp.einsum("rgjd,rgd->rgj", queries, own_keys, preferred_element_type=jnp.float32) * factor
    )
    live_mask = (jnp.arange(tail_size, dtype=jnp.float32)[None, :] < child_length[:, None])[
        :, None, None, :
    ]
    top_score = jnp.maximum(jnp.max(jnp.where(live_mask, tail_scores, -1e30), axis=-1), own_scores)
    tail_exp = jnp.where(live_mask, jnp.exp(tail_scores - top_score[..., None]), 0.0)
    own_exp = jnp.exp(own_scores - top_score)
    totals = jnp.sum(tail_exp, axis=-1) + own_exp
    tail_weights = (tail_exp / totals[..., None]).astype(jnp.bfloat16)
    own_weights = (own_exp / totals).astype(jnp.bfloat16)
    mixture = jnp.einsum(
        "rgjt,rtgd->rgjd", tail_weights, tail_values, preferred_element_type=jnp.float32
    )
    mixture = mixture + own_weights[..., None].astype(jnp.float32) * own_values[
        :, :, None, :
    ].astype(jnp.float32)
    return mixture.reshape(row_count, -1).astype(jnp.bfloat16)


def ffn_terms(
    rows_in, gate_blocks, up_blocks, gate_up_keep, gate_scale, up_scale, down_blocks, down_scale
):
    row_count = rows_in.shape[0]
    blocks = rows_in.reshape(row_count, -1, BLK)
    picked = blocks[:, gate_up_keep]
    gate_part = jnp.einsum(
        "rckd,ckdf->rckf", picked, gate_blocks, preferred_element_type=jnp.float32
    )
    up_part = jnp.einsum("rckd,ckdf->rckf", picked, up_blocks, preferred_element_type=jnp.float32)
    gate_sum = jnp.sum(gate_part * gate_scale[None, :, :, None], axis=2)
    up_sum = jnp.sum(up_part * up_scale[None, :, :, None], axis=2)
    hidden = (jax.nn.silu(gate_sum) * up_sum).astype(jnp.bfloat16)
    contrib = (
        jnp.einsum("rcf,ckfe->rcke", hidden, down_blocks, preferred_element_type=jnp.float32)
        * down_scale[None, :, :, None]
    )
    return contrib.reshape(row_count, -1, BLK)


def feed_forward(
    rows_in,
    gate_blocks,
    up_blocks,
    gate_up_keep,
    gate_scale,
    up_scale,
    down_blocks,
    down_keep,
    down_scale,
):
    row_count = rows_in.shape[0]
    contrib = ffn_terms(
        rows_in, gate_blocks, up_blocks, gate_up_keep, gate_scale, up_scale, down_blocks, down_scale
    )
    placed = jnp.zeros((row_count, rows_in.shape[1] // BLK, BLK), jnp.float32)
    placed = placed.at[:, down_keep.reshape(-1)].add(contrib)
    return placed.reshape(row_count, -1)


def per_device(
    branch_query,
    key_new,
    value_new,
    pool_pages,
    page_table,
    tail_length,
    parent_row,
    residual,
    norm_gain,
    gate_blocks,
    up_blocks,
    gate_up_keep,
    gate_scale,
    up_scale,
    down_blocks,
    down_keep,
    down_scale,
):
    row_count = branch_query.shape[0]
    tail_size = page_table.shape[1] * pool_pages.shape[2]
    own_tails = pool_pages[:, page_table].reshape(2, row_count, tail_size, pool_pages.shape[3])
    own_length = tail_length.astype(jnp.bfloat16)
    prior_tails, prior_length = shifted((own_tails, own_length), "wide", 1)
    both_tails = jnp.concatenate([prior_tails, own_tails], axis=1)
    both_length = jnp.concatenate([prior_length, own_length]).astype(jnp.float32)
    local_parent = parent_row - (lax.axis_index("wide") - 1) * row_count
    child_tails = both_tails[:, local_parent]
    child_length = both_length[local_parent]
    attention = attend(branch_query, key_new, value_new, child_tails, child_length)
    head_rows = lax.all_to_all(attention, "head", split_axis=0, concat_axis=1, tiled=True)
    middle = residual.astype(jnp.float32) + head_rows.astype(jnp.float32)
    normed = (
        middle * lax.rsqrt(jnp.mean(middle * middle, axis=-1, keepdims=True) + 1e-05) * norm_gain
    ).astype(jnp.bfloat16)
    gathered = lax.all_gather(normed, "wide", axis=0, tiled=True)
    ffn_share = lax.psum_scatter(
        feed_forward(
            gathered,
            gate_blocks,
            up_blocks,
            gate_up_keep,
            gate_scale,
            up_scale,
            down_blocks,
            down_keep,
            down_scale,
        ),
        "wide",
        scatter_dimension=0,
        tiled=True,
    )
    return (middle + ffn_share).astype(jnp.bfloat16)


def solution(mesh):
    placed = (
        P("wide", "head"),
        P("wide", "head"),
        P("wide", "head"),
        P(None, "wide", None, "head"),
        P("wide", None),
        P("wide"),
        P("wide"),
        P(("wide", "head"), None),
        P(),
        P("wide", None, None, None),
        P("wide", None, None, None),
        P("wide", None),
        P("wide", None),
        P("wide", None),
        P("wide", None, None, None),
        P("wide", None),
        P("wide", None),
    )
    return jax.shard_map(
        per_device, mesh=mesh, in_specs=placed, out_specs=P(("wide", "head"), None), check_vma=False
    )
```

profile of v0, /device:TPU:1, one launch (start us, length us, event | category | flops | bytes accessed | tf_op | source)
XLA Modules:
  0.0 1659.0 jit_solution(4971448282090236320)
XLA Ops:
  6.5 0.0 copy-start
  6.5 0.0 all-gather.3.cloned.1.call-start
  6.5 0.8 compare_select_fusion
  7.4 0.1 reshape.169
  7.5 0.7 copy-done
  8.2 0.0 copy-start.4
  8.2 2.0 gather_fusion.1
  10.2 3.1 copy.39
  13.3 4.9 collective-permute-start.1
  18.3 0.0 copy-done.10
  18.3 1.9 collective-permute-start
  20.2 0.0 copy-done.6
  20.2 0.0 copy-done.7
  20.3 0.0 copy-done.11
  20.3 0.0 copy-done.4
  20.3 0.1 fusion.21
  20.4 21.1 %collective-permute-done = bf16[4]{0:T(256)(128)(2,1)S(1)} collective-permute-done((bf16[4]{0:T(256)(128)(2,1)S(1)}, bf16[4]{0:T(256)(128)(2,1)S(1)}, u32[]{:S(2)}, u32[]{:S(2)}) %collective-permute-start) | collective-permute-done | bytes 40 | tf_op jit(solution)/shard_map/ppermute | solution.py:15
  41.5 0.1 maximum_convert_fusion
  41.6 0.6 gather_fusion
  42.2 0.1 iota_compare_fusion
  42.3 0.0 collective-permute-done.1
  42.3 4.5 pad_maximum_fusion
  46.8 2.9 gather_fusion.2
  49.7 1.2 fusion.33
  50.9 1.5 copy.40
  52.4 0.3 select_reduce_fusion
  52.8 0.2 bitcast_reduce_fusion
  53.0 0.5 copy.42
  53.5 0.4 fusion.5
  54.0 13.8 all_to_all.10
  67.8 0.0 copy-done.3
  67.8 0.2 multiply_reduce_fusion
  68.0 0.0 copy-done.5
  68.0 0.7 fusion.24
  68.7 0.0 all-gather.3.cloned.1.call-update
  68.7 0.2 all-reduce.3.cloned.1.call-start
  69.0 0.0 copy-done.12
  69.0 0.0 copy-done.13
  69.0 202.0 %all-gather.3.cloned.1.call-done = bf16[128,2,8192]{2,1,0:T(2,128)(2,1)} async-done(((bf16[1,2,8192]{2,1,0:T(2,128)(2,1)}), bf16[128,2,8192]{2,1,0:T(2,128)(2,1)}) %all-gather.3.cloned.1.call-update) | async-done | bytes 4194320 | tf_op jit(solution)/shard_map/all_gather | solution.py:129
  271.0 7.8 reshape.150
  278.8 6.9 copy.44
  285.7 3.2 gather_fusion.3
  288.9 0.0 copy-start.9
  288.9 0.0 copy-done.14
  288.9 0.0 copy-start.2
  288.9 0.0 copy-start.8
  288.9 2.1 fusion.1
  291.0 0.0 copy-done.15
  291.0 0.0 copy-done.9
  291.0 0.7 fusion.2
  291.8 0.0 copy-done.2
  291.8 0.0 copy-done.8
  291.8 2.7 fusion
  294.4 4.3 broadcast_in_dim.48
  298.7 10.2 scatter_fusion
  308.9 9.0 copy.45
  317.9 0.0 all-reduce.3.cloned.1.call-update
  317.9 0.6 copy-done.16
  318.5 0.6 dynamic-slice
  319.8 1323.4 %all-reduce.3.cloned.1.call-done = f32[256,8192]{0,1:T(8,128)} async-done(((f32[256,8192]{0,1:T(8,128)}), f32[256,8192]{0,1:T(8,128)}) %all-reduce.3.cloned.1.call-update) | async-done | bytes 8388624
  1643.2 5.4 constant_dynamic-slice_fusion
  1648.6 2.8 copy.46
  1651.5 0.7 add_convert_fusion
  1652.1 0.0 copy-done.1
  (26 shorter events, 0.2 us)
Async XLA Ops:
  6.5 1.6 copy-start
  6.5 264.5 %all-gather.3.cloned.1.call-start = ((), (), s32[]{:S(2)}) async-start(), calls=%async_computation.1 | async-start | bytes 4227072 | tf_op jit(solution)/shard_map/all_gather | solution.py:129
  8.1 10.1 copy-start.10
  8.1 12.1 copy-start.6
  8.1 12.1 copy-start.7
  8.1 12.1 copy-start.11
  8.2 12.1 copy-start.4
  13.3 29.0 %collective-permute-start.1 = (bf16[2,4,256,512]{3,2,1,0:T(8,128)(2,1)}, bf16[2,4,256,512]{3,2,1,0:T(8,128)(2,1)}, u32[]{:S(2)}, u32[]{:S(2)}) collective-permute-start(bf16[2,4,256,512]{3,2,1,0:T(8,128)(2,1)} %bitcast.2), channel_id=1, source_target_pairs={{0,2},{2,4},{4,6},{6,8},{8,10},{10,12},{12,14},{14,16},{16,18},{18... | collective-permute-start | bytes 6291464 | tf_op jit(solution)/shard_map/ppermute | solution.py:15
  18.3 23.3 %collective-permute-start = (bf16[4]{0:T(256)(128)(2,1)S(1)}, bf16[4]{0:T(256)(128)(2,1)S(1)}, u32[]{:S(2)}, u32[]{:S(2)}) collective-permute-start(bf16[4]{0:T(256)(128)(2,1)S(1)} %convert_element_type.63), channel_id=1, source_target_pairs={{0,2},{2,4},{4,6},{6,8},{8,10},{10,12},{12,14},{14,16},{16,18},{18... | collective-permute-start | bytes 32 | tf_op jit(solution)/shard_map/ppermute | solution.py:15
  50.9 16.9 %copy-start.3 = (bf16[2,8192]{1,0:T(2,128)(2,1)S(1)}, bf16[2,8192]{1,0:T(2,128)(2,1)}, u32[]{:S(2)}) copy-start(bf16[2,8192]{1,0:T(2,128)(2,1)} %param.24) | copy-start | bytes 98308
  50.9 17.1 %copy-start.5 = (f32[8192]{0:T(1024)S(1)}, f32[8192]{0:T(1024)}, u32[]{:S(2)}) copy-start(f32[8192]{0:T(1024)} %param.25) | copy-start | bytes 98308
  50.9 18.1 %copy-start.12 = (s32[1,32]{1,0:T(1,128)S(1)}, s32[1,32]{1,0:T(1,128)}, u32[]{:S(2)}) copy-start(s32[1,32]{1,0:T(1,128)} %param.28) | copy-start | bytes 388
  50.9 18.1 %copy-start.13 = (s32[1,32]{1,0:T(1,128)S(1)}, s32[1,32]{1,0:T(1,128)}, u32[]{:S(2)}) copy-start(s32[1,32]{1,0:T(1,128)} %param.32) | copy-start | bytes 388
  68.7 1574.4 %all-reduce.3.cloned.1.call-start = ((), (), s32[]{:S(2)}) async-start(), calls=%async_computation.2 | async-start | bytes 16777216
  285.7 3.2 copy-start.14
  285.7 5.3 copy-start.15
  288.9 2.1 copy-start.9
  288.9 2.9 copy-start.2
  288.9 2.8 copy-start.8
  317.9 0.7 copy-start.16
  1643.2 9.0 copy-start.1
Sparse Core Ops, SparseCore 0:
  68.9 202.1 all-gather.2
  318.0 1325.1 all-reduce.2
where the time goes:
time: 1660 us
  waiting for transfers between devices  1550 us (93%)
  local copies, waits for them, and re-layouts  53.3 us (3%)
  other arithmetic  17.5 us (1%)
    unnamed x3, waiting for transfers between devices  1320 us
    all_gather x1, waiting for transfers between devices, per_device(): gathered = lax.all_gather(normed, 'wide', axis=0, tiled=True)  202 us
  transfers between devices with their start and end apart: 4, of which 3 were waited for; matrix products, arithmetic and copies ran while one was open for 0% of the time, Pallas kernels for 0%

commit v1 on v0

--- a/solution.py
+++ b/solution.py
@@ -51,44 +51,18 @@
     return mixture.reshape(row_count, -1).astype(jnp.bfloat16)
 
 
-def ffn_terms(
-    rows_in, gate_blocks, up_blocks, gate_up_keep, gate_scale, up_scale, down_blocks, down_scale
-):
-    row_count = rows_in.shape[0]
-    blocks = rows_in.reshape(row_count, -1, BLK)
-    picked = blocks[:, gate_up_keep]
+def ffn_terms(picked, gate_blocks, up_blocks, gate_scale, up_scale, down_blocks, down_scale):
     gate_part = jnp.einsum(
-        "rckd,ckdf->rckf", picked, gate_blocks, preferred_element_type=jnp.float32
+        "rkd,kdf->rkf", picked, gate_blocks[0], preferred_element_type=jnp.float32
     )
-    up_part = jnp.einsum("rckd,ckdf->rckf", picked, up_blocks, preferred_element_type=jnp.float32)
-    gate_sum = jnp.sum(gate_part * gate_scale[None, :, :, None], axis=2)
-    up_sum = jnp.sum(up_part * up_scale[None, :, :, None], axis=2)
+    up_part = jnp.einsum("rkd,kdf->rkf", picked, up_blocks[0], preferred_element_type=jnp.float32)
+    gate_sum = jnp.sum(gate_part * gate_scale[0][None, :, None], axis=1)
+    up_sum = jnp.sum(up_part * up_scale[0][None, :, None], axis=1)
     hidden = (jax.nn.silu(gate_sum) * up_sum).astype(jnp.bfloat16)
-    contrib = (
-        jnp.einsum("rcf,ckfe->rcke", hidden, down_blocks, preferred_element_type=jnp.float32)
-        * down_scale[None, :, :, None]
+    return (
+        jnp.einsum("rf,kfe->rke", hidden, down_blocks[0], preferred_element_type=jnp.float32)
+        * down_scale[0][None, :, None]
     )
-    return contrib.reshape(row_count, -1, BLK)
-
-
-def feed_forward(
-    rows_in,
-    gate_blocks,
-    up_blocks,
-    gate_up_keep,
-    gate_scale,
-    up_scale,
-    down_blocks,
-    down_keep,
-    down_scale,
-):
-    row_count = rows_in.shape[0]
-    contrib = ffn_terms(
-        rows_in, gate_blocks, up_blocks, gate_up_keep, gate_scale, up_scale, down_blocks, down_scale
-    )
-    placed = jnp.zeros((row_count, rows_in.shape[1] // BLK, BLK), jnp.float32)
-    placed = placed.at[:, down_keep.reshape(-1)].add(contrib)
-    return placed.reshape(row_count, -1)
 
 
 def per_device(
@@ -126,23 +100,29 @@
     normed = (
         middle * lax.rsqrt(jnp.mean(middle * middle, axis=-1, keepdims=True) + 1e-05) * norm_gain
     ).astype(jnp.bfloat16)
-    gathered = lax.all_gather(normed, "wide", axis=0, tiled=True)
-    ffn_share = lax.psum_scatter(
-        feed_forward(
-            gathered,
-            gate_blocks,
-            up_blocks,
-            gate_up_keep,
-            gate_scale,
-            up_scale,
-            down_blocks,
-            down_keep,
-            down_scale,
-        ),
-        "wide",
-        scatter_dimension=0,
-        tiled=True,
+    keep_lists = lax.all_gather(
+        jnp.concatenate([gate_up_keep, down_keep], axis=1), "wide", axis=0, tiled=True
     )
+    keep = gate_up_keep.shape[1]
+    in_keep, out_keep = keep_lists[:, :keep], keep_lists[:, keep:]
+    feature_blocks = normed.shape[1] // BLK
+    normed_blocks = normed.reshape(normed.shape[0], feature_blocks, BLK)
+    outgoing = jnp.swapaxes(normed_blocks[:, in_keep], 0, 1)
+    picked = lax.all_to_all(outgoing, "wide", split_axis=0, concat_axis=0, tiled=True)
+    picked = picked.reshape(-1, keep, BLK)
+    contrib = ffn_terms(
+        picked, gate_blocks, up_blocks, gate_scale, up_scale, down_blocks, down_scale
+    ).astype(jnp.bfloat16)
+    contrib = contrib.reshape(-1, normed.shape[0], keep, BLK)
+    arrived = lax.all_to_all(contrib, "wide", split_axis=0, concat_axis=0, tiled=True)
+    senders = arrived.shape[0]
+    placement = (
+        out_keep.reshape(senders * keep, 1) == jnp.arange(feature_blocks, dtype=jnp.int32)[None, :]
+    ).astype(jnp.bfloat16)
+    flat = jnp.swapaxes(arrived, 0, 1).reshape(normed.shape[0], senders * keep, BLK)
+    ffn_share = jnp.einsum(
+        "rsd,sb->rbd", flat, placement, preferred_element_type=jnp.float32
+    ).reshape(normed.shape[0], -1)
     return (middle + ffn_share).astype(jnp.bfloat16)
 
 

time: 1660 us -> 396 us (0.24)
  waiting for transfers between devices: 1550 us -> 58.4 us
  blocking collectives: 13.8 us -> 249 us
    unnamed x3 -> x0, waiting for transfers between devices: 1320 us -> none
    all_gather x1 -> x0, waiting for transfers between devices: 202 us -> none  [per_device(): gathered = lax.all_gather(normed, 'wide', axis=0, tiled=True)]
    all_gather x0 -> x1, blocking collectives: none -> 191 us  [per_device(): lax.all_gather(jnp.concatenate([gate_up_keep, down_keep], axis=1), 'wide'...]
    all_to_all x0 -> x2, waiting for transfers between devices: none -> 58.4 us  [the longest x1 51.7 us: per_device(): lax.all_to_all(contrib, 'wide', split_axis=0, concat_axis=0, tiled=True)]
    all_to_all x1, blocking collectives: 13.8 us -> 58.3 us  [per_device(): lax.all_to_all(outgoing, 'wide', split_axis=0, concat_axis=0, tiled=True)]
    gather x1 -> x2, local copies, waits for them, and re-layouts: 3.16 us -> 28.8 us  [per_device(): outgoing = jnp.swapaxes(normed_blocks[:, in_keep], 0, 1)]
    ppermute x2, waiting for transfers between devices: 21.1 us -> 0.01 us  [shifted(): return lax.ppermute(block, axis, route)]
  transfers between devices with their start and end apart: 4 -> 4, of which waited for: 3 -> 2; matrix products, arithmetic and copies ran while one was open for 0% -> 0% of each run, Pallas kernels for 0% -> 0%
where the time goes in v1:
time: 396 us
  blocking collectives  249 us (63%)
  waiting for transfers between devices  58.4 us (15%)
  local copies, waits for them, and re-layouts  55.5 us (14%)
  starting transfers between devices  20.7 us (5%)
  other arithmetic  6.95 us (2%)
  matrix products  4.63 us (1%)
    all_gather x1, blocking collectives, per_device(): lax.all_gather(jnp.concatenate([gate_up_keep, down_keep], axis=1), 'wide'...  191 us
    all_to_all x1, blocking collectives, per_device(): lax.all_to_all(outgoing, 'wide', split_axis=0, concat_axis=0, tiled=True)  58.3 us
    all_to_all x1, waiting for transfers between devices, per_device(): lax.all_to_all(contrib, 'wide', split_axis=0, concat_axis=0, tiled=True)  51.7 us
    gather x2, local copies, waits for them, and re-layouts, per_device(): outgoing = jnp.swapaxes(normed_blocks[:, in_keep], 0, 1)  28.8 us
  transfers between devices with their start and end apart: 4, of which 2 were waited for; matrix products, arithmetic and copies ran while one was open for 0% of the time, Pallas kernels for 0%

profile of v1, /device:TPU:1, one launch (start us, length us, event | category | flops | bytes accessed | tf_op | source)
XLA Modules:
  0.0 395.7 jit_solution(13125555480860348929)
XLA Ops:
  0.0 0.0 copy-start
  0.0 0.8 compare_select_fusion.1
  0.8 0.1 reshape.96
  0.9 0.7 copy-done
  1.6 2.0 gather_fusion.1
  3.6 0.0 copy-start.12
  3.6 0.0 copy-start.13
  3.7 0.0 copy-start.3
  3.7 3.2 copy.29
  6.8 4.9 %collective-permute-start.1 = (bf16[2,4,256,512]{3,2,1,0:T(8,128)(2,1)}, bf16[2,4,256,512]{3,2,1,0:T(8,128)(2,1)}, u32[]{:S(2)}, u32[]{:S(2)}) collective-permute-start(bf16[2,4,256,512]{3,2,1,0:T(8,128)(2,1)} %bitcast.2), channel_id=1, source_target_pairs={{0,2},{2,4},{4,6},{6,8},{8,10},{10,12},{12,14},{14,16},{16,18},{18... | collective-permute-start | bytes 6291464 | tf_op jit(solution)/shard_map/ppermute | solution.py:15
  11.8 0.0 copy-done.10
  11.8 1.9 collective-permute-start
  13.7 0.0 copy-done.5
  13.8 0.0 copy-done.6
  13.8 0.0 copy-done.11
  13.8 0.0 copy-done.12
  13.8 0.1 add_bitcast_fusion
  13.9 191.1 %all-gather = s32[128,1,64]{2,1,0:T(1,128)S(1)} all-gather(s32[1,1,64]{2,1,0:T(1,128)S(1)} %add_bitcast_fusion), channel_id=1, replica_groups=mesh['wide'=128,'head'=2] {'wide'}, dimensions={0}, use_global_device_ids=true | all-gather | bytes 33024 | tf_op jit(solution)/shard_map/all_gather | solution.py:103
  204.9 0.1 fusion.26
  205.0 0.1 reshape.112
  205.1 0.0 copy-done.13
  205.1 0.0 copy-done.3
  205.2 0.1 fusion.15
  205.3 0.0 collective-permute-done
  205.3 0.1 maximum_convert_fusion
  205.4 0.6 gather_fusion
  206.0 0.1 iota_compare_fusion.1
  206.1 0.0 collective-permute-done.1
  206.1 4.5 %pad_maximum_fusion = bf16[2,8,256,512]{3,2,1,0:T(8,128)(2,1)} fusion(bf16[2,4,256,512]{3,2,1,0:T(8,128)(2,1)} %bitcast.2, bf16[2,4,256,512]{3,2,1,0:T(8,128)(2,1)} %collective-permute-done.1), kind=kLoop, calls=%fused_computation.4 | loop fusion | flops 2097152 | bytes 8388608 | tf_op jit(solution)/shard_map/concatenate | solution.py:92
  210.6 4.2 %gather_fusion.2 = bf16[4,2,256,512]{3,2,1,0:T(8,128)(2,1)} fusion(bf16[2,8,256,512]{3,2,1,0:T(8,128)(2,1)} %pad_maximum_fusion, s32[1024]{0:T(1024)S(1)} %pad_clamp_fusion.1), kind=kCustom, calls=%fused_computation.2 | custom fusion | bytes 4194320 | tf_op jit(solution)/shard_map/gather | solution.py:95
  214.8 2.7 fusion.25
  217.5 1.3 copy.32
  218.8 1.5 copy.30
  220.3 0.0 copy-start.2
  220.3 0.0 copy-start.4
  220.3 0.3 select_reduce_fusion
  220.7 0.2 bitcast_reduce_fusion
  220.9 1.6 fusion
  222.5 0.6 convert_element_type.68
  223.2 6.4 %all-to-all-start = ((bf16[2,2,4096]{2,1,0:T(2,128)(2,1)}), bf16[2,2,4096]{2,1,0:T(2,128)(2,1)S(1)}, u32[]{:S(2)}, u32[]{:S(2)}) async-start(bf16[2,2,4096]{2,1,0:T(2,128)(2,1)} %convert_element_type.68), calls=%async_computation | async-start | bytes 65536 | tf_op jit(solution)/shard_map/all_to_all | solution.py:98
  229.6 6.7 %all-to-all-done = bf16[2,2,4096]{2,1,0:T(2,128)(2,1)S(1)} async-done(((bf16[2,2,4096]{2,1,0:T(2,128)(2,1)}), bf16[2,2,4096]{2,1,0:T(2,128)(2,1)S(1)}, u32[]{:S(2)}, u32[]{:S(2)}) %all-to-all-start) | async-done | bytes 32800 | tf_op jit(solution)/shard_map/all_to_all | solution.py:98
  236.3 0.0 copy-done.2
  236.3 0.2 multiply_reduce_fusion.2
  236.5 0.0 copy-done.4
  236.5 0.1 fusion.18
  236.6 26.9 %gather_fusion.3 = bf16[4096,2,128]{2,1,0:T(2,128)(2,1)} fusion(bf16[2,64,128]{2,0,1:T(2,128)(2,1)S(1)} %fusion.18, s32[4096]{0:T(1024)S(1)} %broadcast_clamp_fusion), kind=kCustom, calls=%fused_computation.3 | custom fusion | bytes 4210688 | tf_op jit(solution)/shard_map/gather | solution.py:110
  263.5 1.9 copy.35
  265.4 0.7 copy.36
  266.1 58.3 %all_to_all.20 = bf16[128,2,32,128]{3,2,1,0:T(8,128)(2,1)S(1)} all-to-all(bf16[128,2,32,128]{3,2,1,0:T(8,128)(2,1)S(1)} %copy.36), channel_id=1, replica_groups=mesh['wide'=128,'head'=2] {'wide'}, dimensions={0} | all-to-all | bytes 4194304 | tf_op jit(solution)/shard_map/all_to_all | solution.py:111
  324.4 2.2 copy.37
  326.6 0.0 copy-start.9
  326.7 0.0 copy-start.15
  326.7 0.7 multiply_reduce_fusion
  327.4 0.5 copy-done.9
  327.9 0.7 multiply_reduce_fusion.1
  328.6 0.5 copy-done.1
  329.1 0.7 multiply_convert_fusion
  329.8 3.7 copy.38
  333.5 7.4 %all-to-all-start.2 = ((bf16[128,2,32,128]{3,1,2,0:T(2,128)(2,1)}), bf16[128,2,32,128]{3,1,2,0:T(2,128)(2,1)}, u32[]{:S(2)}, u32[]{:S(2)}) async-start(bf16[128,2,32,128]{3,1,2,0:T(2,128)(2,1)} %copy.38), calls=%async_computation.2 | async-start | bytes 4194304 | tf_op jit(solution)/shard_map/all_to_all | solution.py:117
  340.9 0.1 eq.15
  341.0 51.7 %all-to-all-done.2 = bf16[128,2,32,128]{3,1,2,0:T(2,128)(2,1)} async-done(((bf16[128,2,32,128]{3,1,2,0:T(2,128)(2,1)}), bf16[128,2,32,128]{3,1,2,0:T(2,128)(2,1)}, u32[]{:S(2)}, u32[]{:S(2)}) %all-to-all-start.2) | async-done | bytes 2097184 | tf_op jit(solution)/shard_map/all_to_all | solution.py:117
  392.7 1.9 copy.39
  394.6 0.4 convolution_bitcast_fusion
  395.0 0.7 fusion.9
  (23 shorter events, 0.1 us)
Async XLA Ops:
  0.0 1.6 copy-start
  3.6 8.2 %copy-start.10 = (s32[4]{0:T(128)S(1)}, s32[4]{0:T(128)}, u32[]{:S(2)}) copy-start(s32[4]{0:T(128)} %param.22) | copy-start | bytes 52
  3.6 10.1 %copy-start.5 = (bf16[4,512]{1,0:T(4,128)(2,1)S(1)}, bf16[4,512]{1,0:T(4,128)(2,1)}, u32[]{:S(2)}) copy-start(bf16[4,512]{1,0:T(4,128)(2,1)} %param.18) | copy-start | bytes 12292
  3.6 10.1 %copy-start.6 = (bf16[4,512]{1,0:T(4,128)(2,1)S(1)}, bf16[4,512]{1,0:T(4,128)(2,1)}, u32[]{:S(2)}) copy-start(bf16[4,512]{1,0:T(4,128)(2,1)} %param.19) | copy-start | bytes 12292
  3.6 10.2 %copy-start.11 = (s32[1,32]{1,0:T(1,128)S(1)}, s32[1,32]{1,0:T(1,128)}, u32[]{:S(2)}) copy-start(s32[1,32]{1,0:T(1,128)} %param.32) | copy-start | bytes 388
  3.6 10.2 %copy-start.12 = (s32[1,32]{1,0:T(1,128)S(1)}, s32[1,32]{1,0:T(1,128)}, u32[]{:S(2)}) copy-start(s32[1,32]{1,0:T(1,128)} %param.28) | copy-start | bytes 388
  3.6 201.5 %copy-start.13 = (s32[4]{0:T(128)S(1)}, s32[4]{0:T(128)}, u32[]{:S(2)}) copy-start(s32[4]{0:T(128)} %param.23) | copy-start | bytes 52
  3.7 201.5 %copy-start.3 = (bf16[4,4096]{1,0:T(4,128)(2,1)S(1)}, bf16[4,4096]{1,0:T(4,128)(2,1)}, u32[]{:S(2)}) copy-start(bf16[4,4096]{1,0:T(4,128)(2,1)} %param.17) | copy-start | bytes 98308
  6.8 199.2 %collective-permute-start.1 = (bf16[2,4,256,512]{3,2,1,0:T(8,128)(2,1)}, bf16[2,4,256,512]{3,2,1,0:T(8,128)(2,1)}, u32[]{:S(2)}, u32[]{:S(2)}) collective-permute-start(bf16[2,4,256,512]{3,2,1,0:T(8,128)(2,1)} %bitcast.2), channel_id=1, source_target_pairs={{0,2},{2,4},{4,6},{6,8},{8,10},{10,12},{12,14},{14,16},{16,18},{18... | collective-permute-start | bytes 6291464 | tf_op jit(solution)/shard_map/ppermute | solution.py:15
  11.8 193.5 %collective-permute-start = (bf16[4]{0:T(256)(128)(2,1)S(1)}, bf16[4]{0:T(256)(128)(2,1)S(1)}, u32[]{:S(2)}, u32[]{:S(2)}) collective-permute-start(bf16[4]{0:T(256)(128)(2,1)S(1)} %convert_element_type.60), channel_id=1, source_target_pairs={{0,2},{2,4},{4,6},{6,8},{8,10},{10,12},{12,14},{14,16},{16,18},{18... | collective-permute-start | bytes 32 | tf_op jit(solution)/shard_map/ppermute | solution.py:15
  220.3 16.0 %copy-start.2 = (bf16[2,8192]{1,0:T(2,128)(2,1)S(1)}, bf16[2,8192]{1,0:T(2,128)(2,1)}, u32[]{:S(2)}) copy-start(bf16[2,8192]{1,0:T(2,128)(2,1)} %param.24) | copy-start | bytes 98308
  220.3 16.2 %copy-start.4 = (f32[8192]{0:T(1024)S(1)}, f32[8192]{0:T(1024)}, u32[]{:S(2)}) copy-start(f32[8192]{0:T(1024)} %param.25) | copy-start | bytes 98308
  223.2 13.1 %all-to-all-start = ((bf16[2,2,4096]{2,1,0:T(2,128)(2,1)}), bf16[2,2,4096]{2,1,0:T(2,128)(2,1)S(1)}, u32[]{:S(2)}, u32[]{:S(2)}) async-start(bf16[2,2,4096]{2,1,0:T(2,128)(2,1)} %convert_element_type.68), calls=%async_computation | async-start | bytes 65536 | tf_op jit(solution)/shard_map/all_to_all | solution.py:98
  324.4 2.2 copy-start.8
  324.4 2.2 copy-start.14
  326.6 1.2 copy-start.9
  326.7 1.2 copy-start.15
  327.9 1.2 copy-start.1
  327.9 1.2 copy-start.7
  333.5 59.2 %all-to-all-start.2 = ((bf16[128,2,32,128]{3,1,2,0:T(2,128)(2,1)}), bf16[128,2,32,128]{3,1,2,0:T(2,128)(2,1)}, u32[]{:S(2)}, u32[]{:S(2)}) async-start(bf16[128,2,32,128]{3,1,2,0:T(2,128)(2,1)} %copy.38), calls=%async_computation.2 | async-start | bytes 4194304 | tf_op jit(solution)/shard_map/all_to_all | solution.py:117

commit v2 on v1

--- a/solution.py
+++ b/solution.py
@@ -100,16 +100,27 @@
     normed = (
         middle * lax.rsqrt(jnp.mean(middle * middle, axis=-1, keepdims=True) + 1e-05) * norm_gain
     ).astype(jnp.bfloat16)
-    keep_lists = lax.all_gather(
-        jnp.concatenate([gate_up_keep, down_keep], axis=1), "wide", axis=0, tiled=True
+    peers = lax.axis_size("wide")
+    own_lists = jnp.concatenate([gate_up_keep, down_keep], axis=1)
+    keep_lists = lax.all_to_all(
+        jnp.broadcast_to(own_lists, (peers, own_lists.shape[1])),
+        "wide",
+        split_axis=0,
+        concat_axis=0,
+        tiled=True,
     )
     keep = gate_up_keep.shape[1]
     in_keep, out_keep = keep_lists[:, :keep], keep_lists[:, keep:]
     feature_blocks = normed.shape[1] // BLK
+    blocks = jnp.arange(feature_blocks, dtype=jnp.int32)
+    choose = (in_keep.reshape(peers * keep, 1) == blocks[None, :]).astype(jnp.bfloat16)
     normed_blocks = normed.reshape(normed.shape[0], feature_blocks, BLK)
-    outgoing = jnp.swapaxes(normed_blocks[:, in_keep], 0, 1)
+    outgoing = jnp.einsum(
+        "sb,rbd->srd", choose, normed_blocks, preferred_element_type=jnp.float32
+    ).astype(jnp.bfloat16)
+    outgoing = outgoing.reshape(peers, keep, normed.shape[0], BLK)
     picked = lax.all_to_all(outgoing, "wide", split_axis=0, concat_axis=0, tiled=True)
-    picked = picked.reshape(-1, keep, BLK)
+    picked = jnp.swapaxes(picked, 1, 2).reshape(-1, keep, BLK)
     contrib = ffn_terms(
         picked, gate_blocks, up_blocks, gate_scale, up_scale, down_blocks, down_scale
     ).astype(jnp.bfloat16)

time: 396 us -> 207 us (0.52)
  blocking collectives: 249 us -> 66.1 us
  local copies, waits for them, and re-layouts: 55.5 us -> 27.9 us
  starting transfers between devices: 20.7 us -> 33 us
  waiting for transfers between devices: 58.4 us -> 67.6 us
    all_gather x1 -> x0, blocking collectives: 191 us -> none  [per_device(): lax.all_gather(jnp.concatenate([gate_up_keep, down_keep], axis=1), 'wide'...]
    gather x2 -> x0, local copies, waits for them, and re-layouts: 28.8 us -> none  [per_device(): outgoing = jnp.swapaxes(normed_blocks[:, in_keep], 0, 1)]
    all_to_all x0 -> x1, starting transfers between devices: none -> 11.5 us  [per_device(): lax.all_to_all(jnp.broadcast_to(own_lists, (peers, own_lists.shape[1])),...]
    ppermute x2, waiting for transfers between devices: 0.01 us -> 9.38 us  [shifted(): return lax.ppermute(block, axis, route)]
    all_to_all x1, blocking collectives: 58.3 us -> 66.1 us  [per_device(): lax.all_to_all(outgoing, 'wide', split_axis=0, concat_axis=0, tiled=True)]
  transfers between devices with their start and end apart: 4 -> 5, of which waited for: 2 -> 3; matrix products, arithmetic and copies ran while one was open for 0% -> 9% of each run, Pallas kernels for 0% -> 0%
where the time goes in v2:
time: 207 us; the launch traced here: 206 us
  waiting for transfers between devices  67.6 us (33%)
  blocking collectives  66.1 us (32%)
  starting transfers between devices  33 us (16%)
  local copies, waits for them, and re-layouts  27.9 us (13%)
  other arithmetic  6.85 us (3%)
  matrix products  4.17 us (2%)
    all_to_all x1, blocking collectives, per_device(): lax.all_to_all(outgoing, 'wide', split_axis=0, concat_axis=0, tiled=True)  66.1 us
    all_to_all x1, waiting for transfers between devices, per_device(): lax.all_to_all(contrib, 'wide', split_axis=0, concat_axis=0, tiled=True)  51.7 us
    all_to_all x1, starting transfers between devices, per_device(): lax.all_to_all(jnp.broadcast_to(own_lists, (peers, own_lists.shape[1])),...  11.5 us
    ppermute x2, waiting for transfers between devices, shifted(): return lax.ppermute(block, axis, route)  9.38 us
    all_to_all x1, starting transfers between devices, per_device(): lax.all_to_all(contrib, 'wide', split_axis=0, concat_axis=0, tiled=True)  7.44 us
    all_to_all x1, starting transfers between devices, per_device(): lax.all_to_all(attention, 'head', split_axis=0, concat_axis=1, tiled=True)  7.28 us
    ppermute x2, starting transfers between devices, shifted(): return lax.ppermute(block, axis, route)  6.85 us
    all_to_all x1, waiting for transfers between devices, per_device(): lax.all_to_all(attention, 'head', split_axis=0, concat_axis=1, tiled=True)  6.54 us
  transfers between devices with their start and end apart: 5, of which 3 were waited for; matrix products, arithmetic and copies ran while one was open for 9% of the time, Pallas kernels for 0%

profile of v2, /device:TPU:1, one launch (start us, length us, event | category | flops | bytes accessed | tf_op | source)
XLA Modules:
  0.0 206.0 jit_solution(13224205020840541013)
XLA Ops:
  0.0 0.0 copy-start
  0.0 0.8 compare_select_fusion
  0.8 0.1 reshape.108
  0.9 0.7 copy-done
  1.6 2.0 gather_fusion.1
  3.6 0.0 copy-start.6
  3.6 0.0 copy-start.13
  3.6 0.0 copy-start.3
  3.7 3.2 %copy.29 = bf16[64,2,16,512]{3,2,0,1:T(8,128)(2,1)} copy(bf16[64,2,16,512]{3,2,1,0:T(8,128)(2,1)} %gather_fusion.1) | data formatting | bytes 4194304 | tf_op jit(solution)/shard_map/gather | solution.py:89
  6.9 4.9 %collective-permute-start.1 = (bf16[2,4,256,512]{3,2,1,0:T(8,128)(2,1)}, bf16[2,4,256,512]{3,2,1,0:T(8,128)(2,1)}, u32[]{:S(2)}, u32[]{:S(2)}) collective-permute-start(bf16[2,4,256,512]{3,2,1,0:T(8,128)(2,1)} %bitcast.2), channel_id=1, source_target_pairs={{0,2},{2,4},{4,6},{6,8},{8,10},{10,12},{12,14},{14,16},{16,18},{18... | collective-permute-start | bytes 6291464 | tf_op jit(solution)/shard_map/ppermute | solution.py:15
  11.8 0.0 copy-done.10
  11.8 1.9 collective-permute-start
  13.7 0.0 copy-done.11
  13.7 0.0 copy-done.12
  13.8 0.1 add_bitcast_fusion
  13.8 0.7 broadcast_in_dim.45
  14.5 11.5 %all-to-all-start.1 = ((s32[128,1,64]{2,1,0:T(1,128)}), s32[128,1,64]{2,1,0:T(1,128)S(1)}, u32[]{:S(2)}, u32[]{:S(2)}) async-start(s32[128,1,64]{2,1,0:T(1,128)} %broadcast_in_dim.45), calls=%async_computation.1 | async-start | bytes 131072 | tf_op jit(solution)/shard_map/all_to_all | solution.py:105
  26.0 0.0 copy-done.5
  26.0 0.0 copy-done.6
  26.0 0.0 copy-done.13
  26.1 0.0 copy-done.3
  26.1 0.1 fusion.20
  26.2 9.4 %collective-permute-done = bf16[4]{0:T(256)(128)(2,1)S(1)} collective-permute-done((bf16[4]{0:T(256)(128)(2,1)S(1)}, bf16[4]{0:T(256)(128)(2,1)S(1)}, u32[]{:S(2)}, u32[]{:S(2)}) %collective-permute-start) | collective-permute-done | bytes 40 | tf_op jit(solution)/shard_map/ppermute | solution.py:15
  35.6 0.1 maximum_convert_fusion
  35.7 0.6 gather_fusion
  36.3 0.1 iota_compare_fusion.2
  36.4 0.0 collective-permute-done.1
  36.4 4.5 %pad_maximum_fusion = bf16[2,8,256,512]{3,2,1,0:T(8,128)(2,1)} fusion(bf16[2,4,256,512]{3,2,1,0:T(8,128)(2,1)} %bitcast.2, bf16[2,4,256,512]{3,2,1,0:T(8,128)(2,1)} %collective-permute-done.1), kind=kLoop, calls=%fused_computation.4 | loop fusion | flops 2097152 | bytes 8388608 | tf_op jit(solution)/shard_map/concatenate | solution.py:92
  40.9 4.2 %gather_fusion.2 = bf16[4,2,256,512]{3,2,1,0:T(8,128)(2,1)} fusion(bf16[2,8,256,512]{3,2,1,0:T(8,128)(2,1)} %pad_maximum_fusion, s32[1024]{0:T(1024)S(1)} %pad_clamp_fusion.1), kind=kCustom, calls=%fused_computation.2 | custom fusion | bytes 4194320 | tf_op jit(solution)/shard_map/gather | solution.py:95
  45.1 3.0 %fusion.30 = (bf16[1,4,256,512]{3,2,0,1:T(8,128)(2,1)}, bf16[1,4,256,512]{3,2,0,1:T(8,128)(2,1)}) fusion(bf16[2,4,256,512]{3,2,0,1:T(8,128)(2,1)} %bitcast.78), kind=kLoop, calls=%fused_computation.60 | loop fusion | bytes 4194304 | tf_op jit(solution)/shard_map/slice | solution.py:24
  48.1 1.5 copy.30
  49.6 0.3 select_reduce_fusion
  49.9 0.2 bitcast_reduce_fusion
  50.1 0.0 copy-start.2
  50.2 0.0 copy-start.4
  50.2 1.5 copy.32
  51.7 0.4 fusion
  52.1 0.6 convert_element_type.72
  52.7 0.0 all-to-all-done.1
  52.7 7.3 %all-to-all-start = ((bf16[2,2,4096]{2,1,0:T(2,128)(2,1)}), bf16[2,2,4096]{2,1,0:T(2,128)(2,1)S(1)}, u32[]{:S(2)}, u32[]{:S(2)}) async-start(bf16[2,2,4096]{2,1,0:T(2,128)(2,1)} %convert_element_type.72), calls=%async_computation | async-start | bytes 65536 | tf_op jit(solution)/shard_map/all_to_all | solution.py:98
  60.0 0.1 fusion.31
  60.1 0.1 eq.34
  60.2 6.5 %all-to-all-done = bf16[2,2,4096]{2,1,0:T(2,128)(2,1)S(1)} async-done(((bf16[2,2,4096]{2,1,0:T(2,128)(2,1)}), bf16[2,2,4096]{2,1,0:T(2,128)(2,1)S(1)}, u32[]{:S(2)}, u32[]{:S(2)}) %all-to-all-start) | async-done | bytes 32800 | tf_op jit(solution)/shard_map/all_to_all | solution.py:98
  66.8 0.2 multiply_reduce_fusion.2
  67.0 0.0 copy-done.4
  67.0 0.1 fusion.23
  67.1 0.8 convolution_convert_fusion
  67.8 0.7 copy.35
  68.6 66.1 %all_to_all.29 = bf16[128,32,2,128]{3,1,2,0:T(8,128)(2,1)S(1)} all-to-all(bf16[128,32,2,128]{3,1,2,0:T(8,128)(2,1)S(1)} %copy.35), channel_id=1, replica_groups=mesh['wide'=128,'head'=2] {'wide'}, dimensions={0} | all-to-all | bytes 4194304 | tf_op jit(solution)/shard_map/all_to_all | solution.py:122
  134.7 2.2 %copy.36 = bf16[128,2,32,128]{3,1,0,2:T(2,128)(2,1)S(1)} copy(bf16[128,2,32,128]{3,2,1,0:T(8,128)(2,1)S(1)} %bitcast.82) | data formatting | bytes 4194304 | tf_op jit(solution)/shard_map/transpose | solution.py:123
  136.9 0.0 copy-start.9
  136.9 0.0 copy-start.15
  137.0 0.7 multiply_reduce_fusion
  137.7 0.5 copy-done.9
  138.2 0.7 multiply_reduce_fusion.1
  138.9 0.5 copy-done.1
  139.4 0.7 multiply_convert_fusion
  140.1 3.7 %copy.37 = bf16[128,2,32,128]{3,1,2,0:T(2,128)(2,1)} copy(bf16[128,2,32,128]{3,1,0,2:T(2,128)(2,1)S(1)} %bitcast.80) | data formatting | bytes 4194304 | tf_op jit(solution)/shard_map/reshape | solution.py:127
  143.8 7.4 %all-to-all-start.3 = ((bf16[128,2,32,128]{3,1,2,0:T(2,128)(2,1)}), bf16[128,2,32,128]{3,1,2,0:T(2,128)(2,1)}, u32[]{:S(2)}, u32[]{:S(2)}) async-start(bf16[128,2,32,128]{3,1,2,0:T(2,128)(2,1)} %copy.37), calls=%async_computation.3 | async-start | bytes 4194304 | tf_op jit(solution)/shard_map/all_to_all | solution.py:128
  151.2 0.1 eq.30
  151.3 51.7 %all-to-all-done.3 = bf16[128,2,32,128]{3,1,2,0:T(2,128)(2,1)} async-done(((bf16[128,2,32,128]{3,1,2,0:T(2,128)(2,1)}), bf16[128,2,32,128]{3,1,2,0:T(2,128)(2,1)}, u32[]{:S(2)}, u32[]{:S(2)}) %all-to-all-start.3) | async-done | bytes 2097184 | tf_op jit(solution)/shard_map/all_to_all | solution.py:128
  203.0 1.9 copy.38
  204.9 0.4 convolution_bitcast_fusion
  205.3 0.7 fusion.12
  (23 shorter events, 0.1 us)
Async XLA Ops:
  0.0 1.6 copy-start
  3.6 8.2 %copy-start.10 = (s32[4]{0:T(128)S(1)}, s32[4]{0:T(128)}, u32[]{:S(2)}) copy-start(s32[4]{0:T(128)} %param.22) | copy-start | bytes 52
  3.6 10.1 %copy-start.11 = (s32[1,32]{1,0:T(1,128)S(1)}, s32[1,32]{1,0:T(1,128)}, u32[]{:S(2)}) copy-start(s32[1,32]{1,0:T(1,128)} %param.32) | copy-start | bytes 388
  3.6 10.1 %copy-start.12 = (s32[1,32]{1,0:T(1,128)S(1)}, s32[1,32]{1,0:T(1,128)}, u32[]{:S(2)}) copy-start(s32[1,32]{1,0:T(1,128)} %param.28) | copy-start | bytes 388
  3.6 22.4 %copy-start.5 = (bf16[4,512]{1,0:T(4,128)(2,1)S(1)}, bf16[4,512]{1,0:T(4,128)(2,1)}, u32[]{:S(2)}) copy-start(bf16[4,512]{1,0:T(4,128)(2,1)} %param.18) | copy-start | bytes 12292
  3.6 22.4 %copy-start.6 = (bf16[4,512]{1,0:T(4,128)(2,1)S(1)}, bf16[4,512]{1,0:T(4,128)(2,1)}, u32[]{:S(2)}) copy-start(bf16[4,512]{1,0:T(4,128)(2,1)} %param.19) | copy-start | bytes 12292
  3.6 22.4 %copy-start.13 = (s32[4]{0:T(128)S(1)}, s32[4]{0:T(128)}, u32[]{:S(2)}) copy-start(s32[4]{0:T(128)} %param.23) | copy-start | bytes 52
  3.6 22.4 %copy-start.3 = (bf16[4,4096]{1,0:T(4,128)(2,1)S(1)}, bf16[4,4096]{1,0:T(4,128)(2,1)}, u32[]{:S(2)}) copy-start(bf16[4,4096]{1,0:T(4,128)(2,1)} %param.17) | copy-start | bytes 98308
  6.9 29.5 %collective-permute-start.1 = (bf16[2,4,256,512]{3,2,1,0:T(8,128)(2,1)}, bf16[2,4,256,512]{3,2,1,0:T(8,128)(2,1)}, u32[]{:S(2)}, u32[]{:S(2)}) collective-permute-start(bf16[2,4,256,512]{3,2,1,0:T(8,128)(2,1)} %bitcast.2), channel_id=1, source_target_pairs={{0,2},{2,4},{4,6},{6,8},{8,10},{10,12},{12,14},{14,16},{16,18},{18... | collective-permute-start | bytes 6291464 | tf_op jit(solution)/shard_map/ppermute | solution.py:15
  11.8 23.8 %collective-permute-start = (bf16[4]{0:T(256)(128)(2,1)S(1)}, bf16[4]{0:T(256)(128)(2,1)S(1)}, u32[]{:S(2)}, u32[]{:S(2)}) collective-permute-start(bf16[4]{0:T(256)(128)(2,1)S(1)} %convert_element_type.64), channel_id=1, source_target_pairs={{0,2},{2,4},{4,6},{6,8},{8,10},{10,12},{12,14},{14,16},{16,18},{18... | collective-permute-start | bytes 32 | tf_op jit(solution)/shard_map/ppermute | solution.py:15
  14.5 38.2 %all-to-all-start.1 = ((s32[128,1,64]{2,1,0:T(1,128)}), s32[128,1,64]{2,1,0:T(1,128)S(1)}, u32[]{:S(2)}, u32[]{:S(2)}) async-start(s32[128,1,64]{2,1,0:T(1,128)} %broadcast_in_dim.45), calls=%async_computation.1 | async-start | bytes 131072 | tf_op jit(solution)/shard_map/all_to_all | solution.py:105
  50.1 16.6 %copy-start.2 = (bf16[2,8192]{1,0:T(2,128)(2,1)S(1)}, bf16[2,8192]{1,0:T(2,128)(2,1)}, u32[]{:S(2)}) copy-start(bf16[2,8192]{1,0:T(2,128)(2,1)} %param.24) | copy-start | bytes 98308
  50.2 16.8 %copy-start.4 = (f32[8192]{0:T(1024)S(1)}, f32[8192]{0:T(1024)}, u32[]{:S(2)}) copy-start(f32[8192]{0:T(1024)} %param.25) | copy-start | bytes 98308
  52.7 14.0 %all-to-all-start = ((bf16[2,2,4096]{2,1,0:T(2,128)(2,1)}), bf16[2,2,4096]{2,1,0:T(2,128)(2,1)S(1)}, u32[]{:S(2)}, u32[]{:S(2)}) async-start(bf16[2,2,4096]{2,1,0:T(2,128)(2,1)} %convert_element_type.72), calls=%async_computation | async-start | bytes 65536 | tf_op jit(solution)/shard_map/all_to_all | solution.py:98
  134.7 2.2 %copy-start.8 = (bf16[1,32,128,128]{3,2,1,0:T(8,128)(2,1)S(1)}, bf16[1,32,128,128]{3,2,1,0:T(8,128)(2,1)}, u32[]{:S(2)}) copy-start(bf16[1,32,128,128]{3,2,1,0:T(8,128)(2,1)} %param.27) | copy-start | bytes 3145732
  134.7 2.2 %copy-start.14 = (f32[1,32]{1,0:T(1,128)S(1)}, f32[1,32]{1,0:T(1,128)}, u32[]{:S(2)}) copy-start(f32[1,32]{1,0:T(1,128)} %param.30) | copy-start | bytes 388
  136.9 1.2 copy-start.9
  136.9 1.2 copy-start.15
  138.2 1.2 copy-start.1
  138.2 1.2 copy-start.7
  143.8 59.2 %all-to-all-start.3 = ((bf16[128,2,32,128]{3,1,2,0:T(2,128)(2,1)}), bf16[128,2,32,128]{3,1,2,0:T(2,128)(2,1)}, u32[]{:S(2)}, u32[]{:S(2)}) async-start(bf16[128,2,32,128]{3,1,2,0:T(2,128)(2,1)} %copy.37), calls=%async_computation.3 | async-start | bytes 4194304 | tf_op jit(solution)/shard_map/all_to_all | solution.py:128

commit v3 on v2

--- a/solution.py
+++ b/solution.py
@@ -1,12 +1,58 @@
+import functools
 import math
 
 import jax
 import jax.numpy as jnp
 from jax import lax
+from jax.experimental import pallas as pl
+from jax.experimental.pallas import tpu as pltpu
 from jax.sharding import PartitionSpec as P
 
 HD = 128
 BLK = 128
+
+
+def exchange_kernel(axis, x_ref, y_ref, send_sem, recv_sem, local_sem):
+    me = lax.axis_index(axis)
+    n = x_ref.shape[0]
+    local = pltpu.make_async_copy(x_ref.at[me], y_ref.at[me], local_sem)
+    local.start()
+
+    def send(j, carry):
+        peer = lax.rem(me + j, n)
+        pltpu.make_async_remote_copy(
+            src_ref=x_ref.at[peer],
+            dst_ref=y_ref.at[me],
+            send_sem=send_sem,
+            recv_sem=recv_sem,
+            device_id={axis: peer},
+            device_id_type=pl.DeviceIdType.MESH,
+        ).start()
+        return carry
+
+    lax.fori_loop(1, n, send, 0)
+    every = pltpu.make_async_remote_copy(
+        src_ref=x_ref.at[pl.ds(0, n - 1)],
+        dst_ref=y_ref.at[pl.ds(0, n - 1)],
+        send_sem=send_sem,
+        recv_sem=recv_sem,
+        device_id={axis: me},
+        device_id_type=pl.DeviceIdType.MESH,
+    )
+    every.wait_send()
+    every.wait_recv()
+    local.wait()
+
+
+def exchange(x, axis):
+    return pl.pallas_call(
+        functools.partial(exchange_kernel, axis),
+        out_shape=jax.ShapeDtypeStruct(x.shape, x.dtype),
+        in_specs=[pl.BlockSpec(memory_space=pl.ANY)],
+        out_specs=pl.BlockSpec(memory_space=pl.ANY),
+        scratch_shapes=[pltpu.SemaphoreType.DMA, pltpu.SemaphoreType.DMA, pltpu.SemaphoreType.DMA],
+        compiler_params=pltpu.CompilerParams(has_side_effects=True),
+    )(x)
 
 
 def shifted(block, axis, distance):
@@ -119,13 +165,13 @@
         "sb,rbd->srd", choose, normed_blocks, preferred_element_type=jnp.float32
     ).astype(jnp.bfloat16)
     outgoing = outgoing.reshape(peers, keep, normed.shape[0], BLK)
-    picked = lax.all_to_all(outgoing, "wide", split_axis=0, concat_axis=0, tiled=True)
+    picked = exchange(outgoing, "wide")
     picked = jnp.swapaxes(picked, 1, 2).reshape(-1, keep, BLK)
     contrib = ffn_terms(
         picked, gate_blocks, up_blocks, gate_scale, up_scale, down_blocks, down_scale
     ).astype(jnp.bfloat16)
     contrib = contrib.reshape(-1, normed.shape[0], keep, BLK)
-    arrived = lax.all_to_all(contrib, "wide", split_axis=0, concat_axis=0, tiled=True)
+    arrived = exchange(contrib, "wide")
     senders = arrived.shape[0]
     placement = (
         out_keep.reshape(senders * keep, 1) == jnp.arange(feature_blocks, dtype=jnp.int32)[None, :]

time: 207 us -> 217 us (1.048)
  Pallas kernels: 0 us -> 119 us
  blocking collectives: 66.1 us -> 0 us
  waiting for transfers between devices: 67.6 us -> 15.9 us
  local copies, waits for them, and re-layouts: 27.9 us -> 43.4 us
  starting transfers between devices: 33 us -> 25.6 us
    pallas_call x0 -> x2, Pallas kernels: none -> 119 us  [exchange(): pl.pallas_call(functools.partial(exchange_kernel, axis), out_shape=jax.Sh...]
    all_to_all x1 -> x0, blocking collectives: 66.1 us -> none  [per_device(): lax.all_to_all(outgoing, 'wide', split_axis=0, concat_axis=0, tiled=True)]
    all_to_all x1 -> x0, waiting for transfers between devices: 51.7 us -> none  [per_device(): lax.all_to_all(contrib, 'wide', split_axis=0, concat_axis=0, tiled=True)]
    convert_element_type x0 -> x2, local copies, waits for them, and re-layouts: none -> 20.8 us  [the longest x1 18.1 us: per_device(): outgoing = jnp.einsum('sb,rbd->srd', choose, normed_blocks, preferred_ele...]
    all_to_all x1 -> x0, starting transfers between devices: 7.44 us -> none  [per_device(): lax.all_to_all(contrib, 'wide', split_axis=0, concat_axis=0, tiled=True)]
    reshape x2 -> x0, local copies, waits for them, and re-layouts: 4.41 us -> none  [the longest x1 3.68 us: per_device(): contrib = contrib.reshape(-1, normed.shape[0], keep, BLK)]
  transfers between devices with their start and end apart: 5 -> 4, of which waited for: 3 -> 2; matrix products, arithmetic and copies ran while one was open for 9% -> 8% of each run, Pallas kernels for 0% -> 0%
where the time goes in v3:
time: 217 us
  Pallas kernels  119 us (55%)
  local copies, waits for them, and re-layouts  43.4 us (20%)
  starting transfers between devices  25.6 us (12%)
  waiting for transfers between devices  15.9 us (7%)
  other arithmetic  6.86 us (3%)
  matrix products  5.31 us (2%)
    pallas_call x2, Pallas kernels, exchange(): pl.pallas_call(functools.partial(exchange_kernel, axis), out_shape=jax.Sh...  119 us
    convert_element_type x1, local copies, waits for them, and re-layouts, per_device(): outgoing = jnp.einsum('sb,rbd->srd', choose, normed_blocks, preferred_ele...  18.1 us
    all_to_all x1, starting transfers between devices, per_device(): lax.all_to_all(jnp.broadcast_to(own_lists, (peers, own_lists.shape[1])),...  11.5 us
    ppermute x2, waiting for transfers between devices, shifted(): return lax.ppermute(block, axis, route)  9.39 us
    all_to_all x1, starting transfers between devices, per_device(): lax.all_to_all(attention, 'head', split_axis=0, concat_axis=1, tiled=True)  7.28 us
    ppermute x2, starting transfers between devices, shifted(): return lax.ppermute(block, axis, route)  6.85 us
    all_to_all x1, waiting for transfers between devices, per_device(): lax.all_to_all(attention, 'head', split_axis=0, concat_axis=1, tiled=True)  6.46 us
    gather x2, local copies, waits for them, and re-layouts, per_device(): pool_pages[:, page_table]  5.19 us
  transfers between devices with their start and end apart: 4, of which 2 were waited for; matrix products, arithmetic and copies ran while one was open for 8% of the time, Pallas kernels for 0%

profile of v3, /device:TPU:1, one launch (start us, length us, event | category | flops | bytes accessed | tf_op | source)
XLA Modules:
  0.0 216.6 jit_solution(5513890147309208959)
XLA Ops:
  0.0 0.0 copy-start
  0.0 0.8 compare_select_fusion
  0.8 0.1 reshape.108
  0.9 0.7 copy-done
  1.6 2.0 gather_fusion.1
  3.6 0.0 copy-start.6
  3.6 0.0 copy-start.13
  3.7 0.0 copy-start.3
  3.7 3.2 %copy.32 = bf16[64,2,16,512]{3,2,0,1:T(8,128)(2,1)} copy(bf16[64,2,16,512]{3,2,1,0:T(8,128)(2,1)} %gather_fusion.1) | data formatting | bytes 4194304 | tf_op jit(solution)/shard_map/gather | solution.py:135
  6.8 4.9 %collective-permute-start.1 = (bf16[2,4,256,512]{3,2,1,0:T(8,128)(2,1)}, bf16[2,4,256,512]{3,2,1,0:T(8,128)(2,1)}, u32[]{:S(2)}, u32[]{:S(2)}) collective-permute-start(bf16[2,4,256,512]{3,2,1,0:T(8,128)(2,1)} %bitcast.2), channel_id=1, source_target_pairs={{0,2},{2,4},{4,6},{6,8},{8,10},{10,12},{12,14},{14,16},{16,18},{18... | collective-permute-start | bytes 6291464 | tf_op jit(solution)/shard_map/ppermute | solution.py:61
  11.8 0.0 copy-done.10
  11.8 1.9 collective-permute-start
  13.7 0.0 copy-done.11
  13.7 0.0 copy-done.12
  13.8 0.1 add_bitcast_fusion
  13.8 0.7 broadcast_in_dim.45
  14.5 11.5 %all-to-all-start.1 = ((s32[128,1,64]{2,1,0:T(1,128)}), s32[128,1,64]{2,1,0:T(1,128)S(1)}, u32[]{:S(2)}, u32[]{:S(2)}) async-start(s32[128,1,64]{2,1,0:T(1,128)} %broadcast_in_dim.45), calls=%async_computation.1 | async-start | bytes 131072 | tf_op jit(solution)/shard_map/all_to_all | solution.py:151
  26.1 0.1 fusion.22
  26.2 9.4 %collective-permute-done = bf16[4]{0:T(256)(128)(2,1)S(1)} collective-permute-done((bf16[4]{0:T(256)(128)(2,1)S(1)}, bf16[4]{0:T(256)(128)(2,1)S(1)}, u32[]{:S(2)}, u32[]{:S(2)}) %collective-permute-start) | collective-permute-done | bytes 40 | tf_op jit(solution)/shard_map/ppermute | solution.py:61
  35.6 0.1 maximum_convert_fusion
  35.7 0.6 gather_fusion
  36.3 0.1 iota_compare_fusion.2
  36.4 0.0 collective-permute-done.1
  36.4 4.5 %pad_maximum_fusion = bf16[2,8,256,512]{3,2,1,0:T(8,128)(2,1)} fusion(bf16[2,4,256,512]{3,2,1,0:T(8,128)(2,1)} %bitcast.2, bf16[2,4,256,512]{3,2,1,0:T(8,128)(2,1)} %collective-permute-done.1), kind=kLoop, calls=%fused_computation.4 | loop fusion | flops 2097152 | bytes 8388608 | tf_op jit(solution)/shard_map/concatenate | solution.py:138
  40.9 4.2 %gather_fusion.2 = bf16[4,2,256,512]{3,2,1,0:T(8,128)(2,1)} fusion(bf16[2,8,256,512]{3,2,1,0:T(8,128)(2,1)} %pad_maximum_fusion, s32[1024]{0:T(1024)S(1)} %pad_clamp_fusion.1), kind=kCustom, calls=%fused_computation.2 | custom fusion | bytes 4194320 | tf_op jit(solution)/shard_map/gather | solution.py:141
  45.1 3.0 %fusion.32 = (bf16[1,4,256,512]{3,2,0,1:T(8,128)(2,1)}, bf16[1,4,256,512]{3,2,0,1:T(8,128)(2,1)}) fusion(bf16[2,4,256,512]{3,2,0,1:T(8,128)(2,1)} %bitcast.76), kind=kLoop, calls=%fused_computation.62 | loop fusion | bytes 4194304 | tf_op jit(solution)/shard_map/slice | solution.py:70
  48.1 1.5 copy.33
  49.6 0.3 select_reduce_fusion
  49.9 0.2 bitcast_reduce_fusion
  50.2 0.0 copy-start.2
  50.2 0.0 copy-start.4
  50.2 1.5 copy.35
  51.7 0.4 fusion.2
  52.1 0.6 convert_element_type.72
  52.7 0.0 all-to-all-done.1
  52.7 7.3 %all-to-all-start = ((bf16[2,2,4096]{2,1,0:T(2,128)(2,1)}), bf16[2,2,4096]{2,1,0:T(2,128)(2,1)S(1)}, u32[]{:S(2)}, u32[]{:S(2)}) async-start(bf16[2,2,4096]{2,1,0:T(2,128)(2,1)} %convert_element_type.72), calls=%async_computation | async-start | bytes 65536 | tf_op jit(solution)/shard_map/all_to_all | solution.py:144
  60.0 0.1 fusion.33
  60.1 0.1 eq.34
  60.2 0.1 eq.30
  60.3 6.5 %all-to-all-done = bf16[2,2,4096]{2,1,0:T(2,128)(2,1)S(1)} async-done(((bf16[2,2,4096]{2,1,0:T(2,128)(2,1)}), bf16[2,2,4096]{2,1,0:T(2,128)(2,1)S(1)}, u32[]{:S(2)}, u32[]{:S(2)}) %all-to-all-start) | async-done | bytes 32800 | tf_op jit(solution)/shard_map/all_to_all | solution.py:144
  66.8 0.2 multiply_reduce_fusion.2
  67.0 0.1 fusion.25
  67.1 0.8 convolution_convert_fusion
  67.8 18.1 %copy.38 = bf16[4096,2,128]{2,1,0:T(2,128)(2,1)} copy(bf16[4096,2,128]{2,0,1:T(8,128)(2,1)S(1)} %convolution_convert_fusion) | data formatting | bytes 4194304 | tf_op jit(solution)/shard_map/convert_element_type | solution.py:166
  86.0 60.3 %shard_map.163 = bf16[128,32,2,128]{3,2,1,0:T(2,128)(2,1)} custom-call(bf16[128,32,2,128]{3,2,1,0:T(2,128)(2,1)} %bitcast.78), custom_call_target="tpu_custom_call" | custom-call | tf_op jit(solution)/shard_map/pallas_call | solution.py:48
  146.3 0.0 copy-start.8
  146.3 0.0 copy-start.14
  146.3 2.3 %copy.39 = bf16[128,2,32,128]{3,2,1,0:T(8,128)(2,1)S(1)} copy(bf16[128,2,32,128]{3,1,2,0:T(2,128)(2,1)} %bitcast.79) | data formatting | bytes 4194304 | tf_op jit(solution)/shard_map/transpose | solution.py:169
  148.6 0.0 copy-done.8
  148.6 0.0 copy-done.14
  148.6 0.0 copy-start.9
  148.6 0.0 copy-start.15
  148.6 1.3 multiply_reduce_fusion
  149.9 0.0 copy-start.1
  149.9 0.0 copy-start.7
  149.9 1.3 multiply_reduce_fusion.1
  151.2 0.0 copy-done.1
  151.2 0.0 copy-done.7
  151.2 0.7 multiply_convert_fusion
  151.9 2.7 %copy.42 = bf16[256,32,128]{2,1,0:T(8,128)(2,1)} copy(bf16[256,32,128]{2,0,1:T(8,128)(2,1)S(1)} %multiply_convert_fusion) | data formatting | bytes 4194304 | tf_op jit(solution)/shard_map/convert_element_type | solution.py:172
  154.6 58.8 %shard_map.164 = bf16[128,2,32,128]{3,2,1,0:T(8,128)(2,1)} custom-call(bf16[128,2,32,128]{3,2,1,0:T(8,128)(2,1)} %bitcast.80), custom_call_target="tpu_custom_call" | custom-call | tf_op jit(solution)/shard_map/pallas_call | solution.py:48
  213.5 2.0 copy.43
  215.4 0.4 convolution_bitcast_fusion
  215.9 0.7 fusion.14
  (22 shorter events, 0.1 us)
Async XLA Ops:
  0.0 1.6 copy-start
  3.6 8.2 %copy-start.10 = (s32[4]{0:T(128)S(1)}, s32[4]{0:T(128)}, u32[]{:S(2)}) copy-start(s32[4]{0:T(128)} %param.22) | copy-start | bytes 52
  3.6 10.1 %copy-start.11 = (s32[1,32]{1,0:T(1,128)S(1)}, s32[1,32]{1,0:T(1,128)}, u32[]{:S(2)}) copy-start(s32[1,32]{1,0:T(1,128)} %param.32) | copy-start | bytes 388
  3.6 10.1 %copy-start.12 = (s32[1,32]{1,0:T(1,128)S(1)}, s32[1,32]{1,0:T(1,128)}, u32[]{:S(2)}) copy-start(s32[1,32]{1,0:T(1,128)} %param.28) | copy-start | bytes 388
  3.6 22.3 %copy-start.5 = (bf16[4,512]{1,0:T(4,128)(2,1)S(1)}, bf16[4,512]{1,0:T(4,128)(2,1)}, u32[]{:S(2)}) copy-start(bf16[4,512]{1,0:T(4,128)(2,1)} %param.18) | copy-start | bytes 12292
  3.6 22.4 %copy-start.6 = (bf16[4,512]{1,0:T(4,128)(2,1)S(1)}, bf16[4,512]{1,0:T(4,128)(2,1)}, u32[]{:S(2)}) copy-start(bf16[4,512]{1,0:T(4,128)(2,1)} %param.19) | copy-start | bytes 12292
  3.6 22.4 %copy-start.13 = (s32[4]{0:T(128)S(1)}, s32[4]{0:T(128)}, u32[]{:S(2)}) copy-start(s32[4]{0:T(128)} %param.23) | copy-start | bytes 52
  3.7 22.4 %copy-start.3 = (bf16[4,4096]{1,0:T(4,128)(2,1)S(1)}, bf16[4,4096]{1,0:T(4,128)(2,1)}, u32[]{:S(2)}) copy-start(bf16[4,4096]{1,0:T(4,128)(2,1)} %param.17) | copy-start | bytes 98308
  6.8 29.5 %collective-permute-start.1 = (bf16[2,4,256,512]{3,2,1,0:T(8,128)(2,1)}, bf16[2,4,256,512]{3,2,1,0:T(8,128)(2,1)}, u32[]{:S(2)}, u32[]{:S(2)}) collective-permute-start(bf16[2,4,256,512]{3,2,1,0:T(8,128)(2,1)} %bitcast.2), channel_id=1, source_target_pairs={{0,2},{2,4},{4,6},{6,8},{8,10},{10,12},{12,14},{14,16},{16,18},{18... | collective-permute-start | bytes 6291464 | tf_op jit(solution)/shard_map/ppermute | solution.py:61
  11.8 23.8 %collective-permute-start = (bf16[4]{0:T(256)(128)(2,1)S(1)}, bf16[4]{0:T(256)(128)(2,1)S(1)}, u32[]{:S(2)}, u32[]{:S(2)}) collective-permute-start(bf16[4]{0:T(256)(128)(2,1)S(1)} %convert_element_type.64), channel_id=1, source_target_pairs={{0,2},{2,4},{4,6},{6,8},{8,10},{10,12},{12,14},{14,16},{16,18},{18... | collective-permute-start | bytes 32 | tf_op jit(solution)/shard_map/ppermute | solution.py:61
  14.5 38.3 %all-to-all-start.1 = ((s32[128,1,64]{2,1,0:T(1,128)}), s32[128,1,64]{2,1,0:T(1,128)S(1)}, u32[]{:S(2)}, u32[]{:S(2)}) async-start(s32[128,1,64]{2,1,0:T(1,128)} %broadcast_in_dim.45), calls=%async_computation.1 | async-start | bytes 131072 | tf_op jit(solution)/shard_map/all_to_all | solution.py:151
  50.2 16.6 %copy-start.2 = (bf16[2,8192]{1,0:T(2,128)(2,1)S(1)}, bf16[2,8192]{1,0:T(2,128)(2,1)}, u32[]{:S(2)}) copy-start(bf16[2,8192]{1,0:T(2,128)(2,1)} %param.24) | copy-start | bytes 98308
  50.2 16.8 %copy-start.4 = (f32[8192]{0:T(1024)S(1)}, f32[8192]{0:T(1024)}, u32[]{:S(2)}) copy-start(f32[8192]{0:T(1024)} %param.25) | copy-start | bytes 98308
  52.7 14.0 %all-to-all-start = ((bf16[2,2,4096]{2,1,0:T(2,128)(2,1)}), bf16[2,2,4096]{2,1,0:T(2,128)(2,1)S(1)}, u32[]{:S(2)}, u32[]{:S(2)}) async-start(bf16[2,2,4096]{2,1,0:T(2,128)(2,1)} %convert_element_type.72), calls=%async_computation | async-start | bytes 65536 | tf_op jit(solution)/shard_map/all_to_all | solution.py:144
  146.3 2.3 %copy-start.8 = (bf16[1,32,128,128]{3,2,1,0:T(8,128)(2,1)S(1)}, bf16[1,32,128,128]{3,2,1,0:T(8,128)(2,1)}, u32[]{:S(2)}) copy-start(bf16[1,32,128,128]{3,2,1,0:T(8,128)(2,1)} %param.27) | copy-start | bytes 3145732
  146.3 2.3 %copy-start.14 = (f32[1,32]{1,0:T(1,128)S(1)}, f32[1,32]{1,0:T(1,128)}, u32[]{:S(2)}) copy-start(f32[1,32]{1,0:T(1,128)} %param.30) | copy-start | bytes 388
  148.6 1.3 copy-start.9
  148.6 1.3 copy-start.15
  149.9 1.3 copy-start.1
  149.9 1.3 copy-start.7

commit v4 on v3

--- a/solution.py
+++ b/solution.py
@@ -10,10 +10,29 @@
 
 HD = 128
 BLK = 128
-
-
-def exchange_kernel(axis, x_ref, y_ref, send_sem, recv_sem, local_sem):
-    me = lax.axis_index(axis)
+Z_LANES = 4
+
+
+def copy_head(source_z, target_lane, source_core, lanes):
+    offset = (source_z - target_lane + 2 * lanes) % (2 * lanes)
+    upper = ((offset + 1) % (2 * lanes)) // lanes
+    tie = ((offset % lanes) // 2) * (1 - (offset % lanes) % 2)
+    return upper + tie * source_core * (1 - 2 * upper)
+
+
+def gather_route(me, here, peer, lanes):
+    source_z = (me // 2) % lanes + lanes * here
+    return copy_head(source_z, (peer // 2) % lanes, me % 2, lanes)
+
+
+def return_route(me, here, peer, lanes):
+    first = copy_head((peer // 2) % lanes, (me // 2) % lanes, peer % 2, lanes)
+    return (first + here) % 2
+
+
+def exchange_kernel(route, lanes, x_ref, y_ref, send_sem, recv_sem, local_sem):
+    me = lax.axis_index("wide")
+    here = lax.axis_index("head")
     n = x_ref.shape[0]
     local = pltpu.make_async_copy(x_ref.at[me], y_ref.at[me], local_sem)
     local.start()
@@ -25,7 +44,7 @@
             dst_ref=y_ref.at[me],
             send_sem=send_sem,
             recv_sem=recv_sem,
-            device_id={axis: peer},
+            device_id=(peer, route(me, here, peer, lanes)),
             device_id_type=pl.DeviceIdType.MESH,
         ).start()
         return carry
@@ -36,7 +55,7 @@
         dst_ref=y_ref.at[pl.ds(0, n - 1)],
         send_sem=send_sem,
         recv_sem=recv_sem,
-        device_id={axis: me},
+        device_id=(me, here),
         device_id_type=pl.DeviceIdType.MESH,
     )
     every.wait_send()
@@ -44,9 +63,9 @@
     local.wait()
 
 
-def exchange(x, axis):
+def exchange(x, route, lanes):
     return pl.pallas_call(
-        functools.partial(exchange_kernel, axis),
+        functools.partial(exchange_kernel, route, lanes),
         out_shape=jax.ShapeDtypeStruct(x.shape, x.dtype),
         in_specs=[pl.BlockSpec(memory_space=pl.ANY)],
         out_specs=pl.BlockSpec(memory_space=pl.ANY),
@@ -99,16 +118,16 @@
 
 def ffn_terms(picked, gate_blocks, up_blocks, gate_scale, up_scale, down_blocks, down_scale):
     gate_part = jnp.einsum(
-        "rkd,kdf->rkf", picked, gate_blocks[0], preferred_element_type=jnp.float32
-    )
-    up_part = jnp.einsum("rkd,kdf->rkf", picked, up_blocks[0], preferred_element_type=jnp.float32)
+        "skd,kdf->skf", picked, gate_blocks[0], preferred_element_type=jnp.float32
+    )
+    up_part = jnp.einsum("skd,kdf->skf", picked, up_blocks[0], preferred_element_type=jnp.float32)
     gate_sum = jnp.sum(gate_part * gate_scale[0][None, :, None], axis=1)
     up_sum = jnp.sum(up_part * up_scale[0][None, :, None], axis=1)
     hidden = (jax.nn.silu(gate_sum) * up_sum).astype(jnp.bfloat16)
     return (
-        jnp.einsum("rf,kfe->rke", hidden, down_blocks[0], preferred_element_type=jnp.float32)
+        jnp.einsum("sf,kfe->ske", hidden, down_blocks[0], preferred_element_type=jnp.float32)
         * down_scale[0][None, :, None]
-    )
+    ).astype(jnp.bfloat16)
 
 
 def per_device(
@@ -158,28 +177,35 @@
     keep = gate_up_keep.shape[1]
     in_keep, out_keep = keep_lists[:, :keep], keep_lists[:, keep:]
     feature_blocks = normed.shape[1] // BLK
+    rows = normed.shape[0]
     blocks = jnp.arange(feature_blocks, dtype=jnp.int32)
     choose = (in_keep.reshape(peers * keep, 1) == blocks[None, :]).astype(jnp.bfloat16)
-    normed_blocks = normed.reshape(normed.shape[0], feature_blocks, BLK)
-    outgoing = jnp.einsum(
-        "sb,rbd->srd", choose, normed_blocks, preferred_element_type=jnp.float32
+    by_block = jnp.swapaxes(normed.reshape(rows, feature_blocks, BLK), 0, 1)
+    outgoing = jnp.dot(
+        choose, by_block.reshape(feature_blocks, rows * BLK), preferred_element_type=jnp.float32
     ).astype(jnp.bfloat16)
-    outgoing = outgoing.reshape(peers, keep, normed.shape[0], BLK)
-    picked = exchange(outgoing, "wide")
-    picked = jnp.swapaxes(picked, 1, 2).reshape(-1, keep, BLK)
-    contrib = ffn_terms(
-        picked, gate_blocks, up_blocks, gate_scale, up_scale, down_blocks, down_scale
-    ).astype(jnp.bfloat16)
-    contrib = contrib.reshape(-1, normed.shape[0], keep, BLK)
-    arrived = exchange(contrib, "wide")
-    senders = arrived.shape[0]
-    placement = (
-        out_keep.reshape(senders * keep, 1) == jnp.arange(feature_blocks, dtype=jnp.int32)[None, :]
-    ).astype(jnp.bfloat16)
-    flat = jnp.swapaxes(arrived, 0, 1).reshape(normed.shape[0], senders * keep, BLK)
-    ffn_share = jnp.einsum(
-        "rsd,sb->rbd", flat, placement, preferred_element_type=jnp.float32
-    ).reshape(normed.shape[0], -1)
+    picked = exchange(outgoing.reshape(peers, keep, rows * BLK), gather_route, Z_LANES)
+    terms = [
+        ffn_terms(
+            picked[:, :, r * BLK : (r + 1) * BLK],
+            gate_blocks,
+            up_blocks,
+            gate_scale,
+            up_scale,
+            down_blocks,
+            down_scale,
+        )
+        for r in range(rows)
+    ]
+    arrived = exchange(jnp.concatenate(terms, axis=2), return_route, Z_LANES)
+    placement = (out_keep.reshape(peers * keep, 1) == blocks[None, :]).astype(jnp.bfloat16)
+    summed = lax.dot_general(
+        placement,
+        arrived.reshape(peers * keep, rows * BLK),
+        (((0,), (0,)), ((), ())),
+        preferred_element_type=jnp.float32,
+    )
+    ffn_share = jnp.swapaxes(summed.reshape(feature_blocks, rows, BLK), 0, 1).reshape(rows, -1)
     return (middle + ffn_share).astype(jnp.bfloat16)
 
 

time: 217 us -> 188 us (0.87)
  Pallas kernels: 119 us -> 86.8 us
  local copies, waits for them, and re-layouts: 43.4 us -> 34.5 us
  matrix products: 5.31 us -> 14.1 us
  other arithmetic: 6.86 us -> 11.3 us
    pallas_call x2, Pallas kernels: 119 us -> 86.8 us  [exchange(): pl.pallas_call(functools.partial(exchange_kernel, route, lanes), out_shap...]
    convert_element_type x2 -> x0, local copies, waits for them, and re-layouts: 20.8 us -> none  [the longest x1 18.1 us: per_device(): outgoing = jnp.einsum('sb,rbd->srd', choose, normed_blocks, preferred_ele...]
    dot_general x0 -> x3, local copies, waits for them, and re-layouts: none -> 10.4 us  [the longest x2 6.24 us: ffn_terms(): jnp.einsum('sf,kfe->ske', hidden, down_blocks[0], preferred_element_type=...]
    transpose x2 -> x0, local copies, waits for them, and re-layouts: 4.22 us -> none  [the longest x1 2.26 us: per_device(): picked = jnp.swapaxes(picked, 1, 2).reshape(-1, keep, BLK)]
    unnamed x0 -> x2, matrix products: none -> 3.54 us
    convert_element_type x0 -> x2, other arithmetic: none -> 2.89 us  [the longest x1 2.78 us: ffn_terms(): return (jnp.einsum('sf,kfe->ske', hidden, down_blocks[0], preferred_eleme...]
    dot_general x5 -> x6, matrix products: 4.43 us -> 7.25 us  [the longest x1 2.35 us: per_device(): lax.dot_general(placement, arrived.reshape(peers * keep, rows * BLK), (((...]
  transfers between devices with their start and end apart: 4 -> 4, of which waited for: 2 -> 2; matrix products, arithmetic and copies ran while one was open for 8% -> 13% of each run, Pallas kernels for 0% -> 0%
where the time goes in v4:
time: 188 us; the launch traced here: 187 us
  Pallas kernels  86.8 us (46%)
  local copies, waits for them, and re-layouts  34.5 us (18%)
  starting transfers between devices  25.7 us (14%)
  waiting for transfers between devices  14.2 us (8%)
  matrix products  14.1 us (8%)
  other arithmetic  11.3 us (6%)
    pallas_call x2, Pallas kernels, exchange(): pl.pallas_call(functools.partial(exchange_kernel, route, lanes), out_shap...  86.8 us
    all_to_all x1, starting transfers between devices, per_device(): lax.all_to_all(jnp.broadcast_to(own_lists, (peers, own_lists.shape[1])),...  11.5 us
    ppermute x2, waiting for transfers between devices, shifted(): return lax.ppermute(block, axis, route)  7.75 us
    all_to_all x1, starting transfers between devices, per_device(): lax.all_to_all(attention, 'head', split_axis=0, concat_axis=1, tiled=True)  7.28 us
    ppermute x2, starting transfers between devices, shifted(): return lax.ppermute(block, axis, route)  6.98 us
    all_to_all x1, waiting for transfers between devices, per_device(): lax.all_to_all(attention, 'head', split_axis=0, concat_axis=1, tiled=True)  6.46 us
    dot_general x2, local copies, waits for them, and re-layouts, ffn_terms(): jnp.einsum('sf,kfe->ske', hidden, down_blocks[0], preferred_element_type=...  6.24 us
    slice x2, local copies, waits for them, and re-layouts, attend(): tail_keys = child_tails[0].reshape(row_count, tail_size, groups, HD)  5.3 us
  transfers between devices with their start and end apart: 4, of which 2 were waited for; matrix products, arithmetic and copies ran while one was open for 13% of the time, Pallas kernels for 0%

profile of v4, /device:TPU:1, one launch (start us, length us, event | category | flops | bytes accessed | tf_op | source)
XLA Modules:
  0.0 186.9 jit_solution(16427205573965570835)
XLA Ops:
  0.0 0.0 copy-start
  0.0 0.8 compare_select_fusion
  0.8 0.1 reshape.106
  0.9 0.7 copy-done
  1.6 2.0 %gather_fusion.1 = bf16[64,2,16,512]{3,2,1,0:T(8,128)(2,1)} fusion(bf16[2,64,16,512]{3,2,1,0:T(8,128)(2,1)S(1)} %copy-done, s32[1024]{0:T(1024)S(1)} %pad_clamp_fusion), kind=kCustom, calls=%fused_computation.1 | custom fusion | bytes 4194560 | tf_op jit(solution)/shard_map/gather | solution.py:154
  3.7 0.0 copy-start.5
  3.7 3.2 %copy.40 = bf16[64,2,16,512]{3,2,0,1:T(8,128)(2,1)} copy(bf16[64,2,16,512]{3,2,1,0:T(8,128)(2,1)} %gather_fusion.1) | data formatting | bytes 4194304 | tf_op jit(solution)/shard_map/gather | solution.py:154
  6.8 5.1 %collective-permute-start.1 = (bf16[2,4,256,512]{3,2,1,0:T(8,128)(2,1)}, bf16[2,4,256,512]{3,2,1,0:T(8,128)(2,1)}, u32[]{:S(2)}, u32[]{:S(2)}) collective-permute-start(bf16[2,4,256,512]{3,2,1,0:T(8,128)(2,1)} %bitcast.2), channel_id=1, source_target_pairs={{0,2},{2,4},{4,6},{6,8},{8,10},{10,12},{12,14},{14,16},{16,18},{18... | collective-permute-start | bytes 6291464 | tf_op jit(solution)/shard_map/ppermute | solution.py:80
  11.9 0.0 copy-done.9
  11.9 1.9 %collective-permute-start = (bf16[4]{0:T(256)(128)(2,1)S(1)}, bf16[4]{0:T(256)(128)(2,1)S(1)}, u32[]{:S(2)}, u32[]{:S(2)}) collective-permute-start(bf16[4]{0:T(256)(128)(2,1)S(1)} %convert_element_type.70), channel_id=1, source_target_pairs={{0,2},{2,4},{4,6},{6,8},{8,10},{10,12},{12,14},{14,16},{16,18},{18... | collective-permute-start | bytes 32 | tf_op jit(solution)/shard_map/ppermute | solution.py:80
  13.8 0.0 copy-done.10
  13.9 0.1 add_bitcast_fusion
  13.9 0.7 broadcast_in_dim.45
  14.6 11.5 %all-to-all-start.1 = ((s32[128,1,64]{2,1,0:T(1,128)}), s32[128,1,64]{2,1,0:T(1,128)S(1)}, u32[]{:S(2)}, u32[]{:S(2)}) async-start(s32[128,1,64]{2,1,0:T(1,128)} %broadcast_in_dim.45), calls=%async_computation.1 | async-start | bytes 131072 | tf_op jit(solution)/shard_map/all_to_all | solution.py:170
  26.1 0.0 copy-done.5
  26.1 1.6 copy.49
  27.8 0.1 fusion.24
  28.0 7.7 %collective-permute-done = bf16[4]{0:T(256)(128)(2,1)S(1)} collective-permute-done((bf16[4]{0:T(256)(128)(2,1)S(1)}, bf16[4]{0:T(256)(128)(2,1)S(1)}, u32[]{:S(2)}, u32[]{:S(2)}) %collective-permute-start) | collective-permute-done | bytes 40 | tf_op jit(solution)/shard_map/ppermute | solution.py:80
  35.7 0.1 maximum_convert_fusion
  35.8 0.6 gather_fusion
  36.4 0.1 iota_compare_fusion.3
  36.5 0.0 collective-permute-done.1
  36.5 4.5 %pad_maximum_fusion = bf16[2,8,256,512]{3,2,1,0:T(8,128)(2,1)} fusion(bf16[2,4,256,512]{3,2,1,0:T(8,128)(2,1)} %bitcast.2, bf16[2,4,256,512]{3,2,1,0:T(8,128)(2,1)} %collective-permute-done.1), kind=kLoop, calls=%fused_computation.4 | loop fusion | flops 2097152 | bytes 8388608 | tf_op jit(solution)/shard_map/concatenate | solution.py:157
  41.0 4.2 %gather_fusion.2 = bf16[4,2,256,512]{3,2,1,0:T(8,128)(2,1)} fusion(bf16[2,8,256,512]{3,2,1,0:T(8,128)(2,1)} %pad_maximum_fusion, s32[1024]{0:T(1024)S(1)} %pad_clamp_fusion.1), kind=kCustom, calls=%fused_computation.2 | custom fusion | bytes 4194320 | tf_op jit(solution)/shard_map/gather | solution.py:160
  45.2 3.0 %fusion.37 = (bf16[1,4,256,512]{3,2,0,1:T(8,128)(2,1)}, bf16[1,4,256,512]{3,2,0,1:T(8,128)(2,1)}) fusion(bf16[2,4,256,512]{3,2,0,1:T(8,128)(2,1)} %bitcast.84), kind=kLoop, calls=%fused_computation.73 | loop fusion | bytes 4194304 | tf_op jit(solution)/shard_map/slice | solution.py:89
  48.2 2.3 %copy.41 = bf16[1,4,256,512]{2,3,1,0:T(8,128)(2,1)} copy(bf16[1,4,256,512]{3,2,0,1:T(8,128)(2,1)} %get-tuple-element.7) | data formatting | bytes 2097152 | tf_op jit(solution)/shard_map/slice | solution.py:89
  50.5 1.6 select_reduce_fusion
  52.1 0.2 bitcast_reduce_fusion
  52.3 0.0 copy-start.1
  52.3 0.0 copy-start.3
  52.3 2.3 %copy.43 = bf16[1,4,256,512]{2,3,1,0:T(8,128)(2,1)} copy(bf16[1,4,256,512]{3,2,0,1:T(8,128)(2,1)} %get-tuple-element.8) | data formatting | bytes 2097152 | tf_op jit(solution)/shard_map/slice | solution.py:90
  54.6 1.6 fusion
  56.3 0.6 convert_element_type.78
  56.9 0.0 all-to-all-done.1
  56.9 7.3 %all-to-all-start = ((bf16[2,2,4096]{2,1,0:T(2,128)(2,1)}), bf16[2,2,4096]{2,1,0:T(2,128)(2,1)S(1)}, u32[]{:S(2)}, u32[]{:S(2)}) async-start(bf16[2,2,4096]{2,1,0:T(2,128)(2,1)} %convert_element_type.78), calls=%async_computation | async-start | bytes 65536 | tf_op jit(solution)/shard_map/all_to_all | solution.py:163
  64.2 0.1 fusion.38
  64.3 0.1 eq.34
  64.3 0.1 eq.30
  64.4 6.5 %all-to-all-done = bf16[2,2,4096]{2,1,0:T(2,128)(2,1)S(1)} async-done(((bf16[2,2,4096]{2,1,0:T(2,128)(2,1)}), bf16[2,2,4096]{2,1,0:T(2,128)(2,1)S(1)}, u32[]{:S(2)}, u32[]{:S(2)}) %all-to-all-start) | async-done | bytes 32800 | tf_op jit(solution)/shard_map/all_to_all | solution.py:163
  70.9 0.2 multiply_reduce_fusion.4
  71.1 0.0 copy-done.3
  71.1 0.1 multiply_convert_fusion.4
  71.2 2.0 %convolution_convert_fusion = bf16[4096,256]{1,0:T(8,128)(2,1)} fusion(s32[4096]{0:T(1024)S(1)} %eq.34, bf16[8,8,2,128]{3,2,1,0:T(2,128)(2,1)S(1)} %bitcast.97), kind=kOutput, calls=%fused_computation.3 | convolution fusion | flops 135528448 | bytes 2146304 | tf_op jit(solution)/shard_map/dot_general | solution.py:184
  73.3 45.4 %shard_map.163 = bf16[128,32,256]{2,1,0:T(8,128)(2,1)} custom-call(bf16[128,32,256]{2,1,0:T(8,128)(2,1)} %bitcast.86), custom_call_target="tpu_custom_call" | custom-call | tf_op jit(solution)/shard_map/pallas_call | solution.py:67
  118.7 0.0 copy-start.7
  118.7 0.0 copy-start.13
  118.7 2.0 %fusion.36 = (bf16[128,32,128]{2,1,0:T(8,128)(2,1)S(1)}, bf16[128,32,128]{2,1,0:T(8,128)(2,1)S(1)}) fusion(bf16[128,32,256]{2,1,0:T(8,128)(2,1)} %shard_map.163), kind=kLoop, calls=%fused_computation.72 | loop fusion | bytes 4194304 | tf_op jit(solution)/shard_map/slice | solution.py:190
  120.7 0.7 multiply_reduce_fusion
  121.4 0.0 copy-start.8
  121.4 0.0 copy-start.14
  121.5 0.7 multiply_reduce_fusion.2
  122.2 0.5 copy-done.8
  122.7 0.7 multiply_reduce_fusion.1
  123.4 0.7 multiply_reduce_fusion.3
  124.1 1.8 fusion.21
  125.9 3.1 %copy.54 = f32[128,32,128]{2,1,0:T(8,128)} copy(f32[128,32,128]{0,2,1:T(8,128)} %bitcast.87) | data formatting | bytes 4194304 | tf_op jit(solution)/shard_map/sf,kfe->ske/dot_general | solution.py:128
  129.0 1.8 fusion.20
  130.8 3.1 %copy.50 = f32[128,32,128]{2,1,0:T(8,128)} copy(f32[128,32,128]{0,2,1:T(8,128)} %bitcast.85) | data formatting | bytes 4194304 | tf_op jit(solution)/shard_map/sf,kfe->ske/dot_general | solution.py:128
  133.9 2.8 %multiply_convert_fusion.1 = (bf16[128,32,128]{2,1,0:T(8,128)(2,1)S(1)}, bf16[128,32,128]{2,1,0:T(8,128)(2,1)S(1)}) fusion(f32[128,32,128]{2,1,0:T(8,128)} %copy.50, f32[32]{0:T(128)S(1)} %bitcast.102, f32[128,32,128]{2,1,0:T(8,128)} %copy.54), kind=kLoop, calls=%fused_computation.9 | loop fusion | flops 2097152 | bytes 6291584 | tf_op jit(solution)/shard_map/convert_element_type | solution.py:130
  136.7 1.7 pad_maximum_fusion.1.x_ref
  138.4 41.4 %shard_map.164 = bf16[128,32,256]{2,1,0:T(8,128)(2,1)} custom-call(bf16[128,32,256]{2,1,0:T(8,128)(2,1)} %pad_maximum_fusion.1.x_ref), custom_call_target="tpu_custom_call" | custom-call | tf_op jit(solution)/shard_map/pallas_call | solution.py:67
  179.7 4.1 %copy.55 = bf16[256,4096]{1,0:T(8,128)(2,1)} copy(bf16[256,4096]{0,1:T(8,128)(2,1)} %bitcast.89) | data formatting | bytes 4194304 | tf_op jit(solution)/shard_map/dot_general | solution.py:202
  183.9 2.4 %convolution_bitcast_fusion = f32[1,2,64,128]{3,2,1,0:T(8,128)S(1)} fusion(bf16[2,128,4096]{2,1,0:T(8,128)(2,1)} %bitcast.88, s32[4096]{0:T(1024)S(1)} %eq.30), kind=kOutput, calls=%fused_computation.15 | convolution fusion | flops 134479872 | bytes 2179072 | tf_op jit(solution)/shard_map/dot_general | solution.py:202
  186.2 0.7 fusion.15
  (26 shorter events, 0.1 us)
Async XLA Ops:
  0.0 1.6 copy-start
  3.6 8.3 %copy-start.9 = (s32[4]{0:T(128)S(1)}, s32[4]{0:T(128)}, u32[]{:S(2)}) copy-start(s32[4]{0:T(128)} %param.22) | copy-start | bytes 52
  3.6 10.2 %copy-start.10 = (s32[1,32]{1,0:T(1,128)S(1)}, s32[1,32]{1,0:T(1,128)}, u32[]{:S(2)}) copy-start(s32[1,32]{1,0:T(1,128)} %param.32) | copy-start | bytes 388
  3.6 10.2 %copy-start.11 = (s32[1,32]{1,0:T(1,128)S(1)}, s32[1,32]{1,0:T(1,128)}, u32[]{:S(2)}) copy-start(s32[1,32]{1,0:T(1,128)} %param.28) | copy-start | bytes 388
  3.6 22.5 %copy-start.4 = (bf16[4,512]{1,0:T(4,128)(2,1)S(1)}, bf16[4,512]{1,0:T(4,128)(2,1)}, u32[]{:S(2)}) copy-start(bf16[4,512]{1,0:T(4,128)(2,1)} %param.18) | copy-start | bytes 12292
  3.7 22.5 %copy-start.5 = (bf16[4,512]{1,0:T(4,128)(2,1)S(1)}, bf16[4,512]{1,0:T(4,128)(2,1)}, u32[]{:S(2)}) copy-start(bf16[4,512]{1,0:T(4,128)(2,1)} %param.19) | copy-start | bytes 12292
  6.8 20.9 %copy-start.12 = (s32[4]{0:T(128)S(1)}, s32[4]{0:T(128)}, u32[]{:S(2)}) copy-start(s32[4]{0:T(128)} %param.23) | copy-start | bytes 52
  6.8 21.0 %copy-start.2 = (bf16[4,4096]{1,0:T(4,128)(2,1)S(1)}, bf16[4,4096]{1,0:T(4,128)(2,1)}, u32[]{:S(2)}) copy-start(bf16[4,4096]{1,0:T(4,128)(2,1)} %param.17) | copy-start | bytes 98308
  6.8 29.7 %collective-permute-start.1 = (bf16[2,4,256,512]{3,2,1,0:T(8,128)(2,1)}, bf16[2,4,256,512]{3,2,1,0:T(8,128)(2,1)}, u32[]{:S(2)}, u32[]{:S(2)}) collective-permute-start(bf16[2,4,256,512]{3,2,1,0:T(8,128)(2,1)} %bitcast.2), channel_id=1, source_target_pairs={{0,2},{2,4},{4,6},{6,8},{8,10},{10,12},{12,14},{14,16},{16,18},{18... | collective-permute-start | bytes 6291464 | tf_op jit(solution)/shard_map/ppermute | solution.py:80
  11.9 23.8 %collective-permute-start = (bf16[4]{0:T(256)(128)(2,1)S(1)}, bf16[4]{0:T(256)(128)(2,1)S(1)}, u32[]{:S(2)}, u32[]{:S(2)}) collective-permute-start(bf16[4]{0:T(256)(128)(2,1)S(1)} %convert_element_type.70), channel_id=1, source_target_pairs={{0,2},{2,4},{4,6},{6,8},{8,10},{10,12},{12,14},{14,16},{16,18},{18... | collective-permute-start | bytes 32 | tf_op jit(solution)/shard_map/ppermute | solution.py:80
  14.6 42.3 %all-to-all-start.1 = ((s32[128,1,64]{2,1,0:T(1,128)}), s32[128,1,64]{2,1,0:T(1,128)S(1)}, u32[]{:S(2)}, u32[]{:S(2)}) async-start(s32[128,1,64]{2,1,0:T(1,128)} %broadcast_in_dim.45), calls=%async_computation.1 | async-start | bytes 131072 | tf_op jit(solution)/shard_map/all_to_all | solution.py:170
  52.3 18.6 %copy-start.1 = (bf16[2,8192]{1,0:T(2,128)(2,1)S(1)}, bf16[2,8192]{1,0:T(2,128)(2,1)}, u32[]{:S(2)}) copy-start(bf16[2,8192]{1,0:T(2,128)(2,1)} %param.24) | copy-start | bytes 98308
  52.3 18.8 %copy-start.3 = (f32[8192]{0:T(1024)S(1)}, f32[8192]{0:T(1024)}, u32[]{:S(2)}) copy-start(f32[8192]{0:T(1024)} %param.25) | copy-start | bytes 98308
  56.9 14.0 %all-to-all-start = ((bf16[2,2,4096]{2,1,0:T(2,128)(2,1)}), bf16[2,2,4096]{2,1,0:T(2,128)(2,1)S(1)}, u32[]{:S(2)}, u32[]{:S(2)}) async-start(bf16[2,2,4096]{2,1,0:T(2,128)(2,1)} %convert_element_type.78), calls=%async_computation | async-start | bytes 65536 | tf_op jit(solution)/shard_map/all_to_all | solution.py:163
  118.7 2.0 %copy-start.7 = (bf16[1,32,128,128]{3,2,1,0:T(8,128)(2,1)S(1)}, bf16[1,32,128,128]{3,2,1,0:T(8,128)(2,1)}, u32[]{:S(2)}) copy-start(bf16[1,32,128,128]{3,2,1,0:T(8,128)(2,1)} %param.27) | copy-start | bytes 3145732
  118.7 2.0 %copy-start.13 = (f32[1,32]{1,0:T(1,128)S(1)}, f32[1,32]{1,0:T(1,128)}, u32[]{:S(2)}) copy-start(f32[1,32]{1,0:T(1,128)} %param.30) | copy-start | bytes 388
  121.4 1.2 copy-start.8
  121.4 1.2 copy-start.14
  130.8 3.1 %copy-start.6 = (f32[1,32]{1,0:T(1,128)S(1)}, f32[1,32]{1,0:T(1,128)}, u32[]{:S(2)}) copy-start(f32[1,32]{1,0:T(1,128)} %param.33) | copy-start | bytes 388

commit v5 on v4

--- a/solution.py
+++ b/solution.py
@@ -118,11 +118,11 @@
 
 def ffn_terms(picked, gate_blocks, up_blocks, gate_scale, up_scale, down_blocks, down_scale):
     gate_part = jnp.einsum(
-        "skd,kdf->skf", picked, gate_blocks[0], preferred_element_type=jnp.float32
-    )
-    up_part = jnp.einsum("skd,kdf->skf", picked, up_blocks[0], preferred_element_type=jnp.float32)
-    gate_sum = jnp.sum(gate_part * gate_scale[0][None, :, None], axis=1)
-    up_sum = jnp.sum(up_part * up_scale[0][None, :, None], axis=1)
+        "skd,kdf->ksf", picked, gate_blocks[0], preferred_element_type=jnp.float32
+    )
+    up_part = jnp.einsum("skd,kdf->ksf", picked, up_blocks[0], preferred_element_type=jnp.float32)
+    gate_sum = jnp.sum(gate_part * gate_scale[0][:, None, None], axis=0)
+    up_sum = jnp.sum(up_part * up_scale[0][:, None, None], axis=0)
     hidden = (jax.nn.silu(gate_sum) * up_sum).astype(jnp.bfloat16)
     return (
         jnp.einsum("sf,kfe->ske", hidden, down_blocks[0], preferred_element_type=jnp.float32)
@@ -160,7 +160,16 @@
     child_tails = both_tails[:, local_parent]
     child_length = both_length[local_parent]
     attention = attend(branch_query, key_new, value_new, child_tails, child_length)
-    head_rows = lax.all_to_all(attention, "head", split_axis=0, concat_axis=1, tiled=True)
+    half = residual.shape[0]
+    here = lax.axis_index("head")
+    mine = lax.dynamic_slice_in_dim(attention, here * half, half, axis=0)
+    theirs = lax.dynamic_slice_in_dim(attention, (1 - here) * half, half, axis=0)
+    arrived_half = lax.ppermute(theirs, "head", [(0, 1), (1, 0)])
+    head_rows = jnp.where(
+        here == 0,
+        jnp.concatenate([mine, arrived_half], axis=1),
+        jnp.concatenate([arrived_half, mine], axis=1),
+    )
     middle = residual.astype(jnp.float32) + head_rows.astype(jnp.float32)
     normed = (
         middle * lax.rsqrt(jnp.mean(middle * middle, axis=-1, keepdims=True) + 1e-05) * norm_gain
@@ -198,12 +207,9 @@
         for r in range(rows)
     ]
     arrived = exchange(jnp.concatenate(terms, axis=2), return_route, Z_LANES)
-    placement = (out_keep.reshape(peers * keep, 1) == blocks[None, :]).astype(jnp.bfloat16)
-    summed = lax.dot_general(
-        placement,
-        arrived.reshape(peers * keep, rows * BLK),
-        (((0,), (0,)), ((), ())),
-        preferred_element_type=jnp.float32,
+    placement = (blocks[:, None] == out_keep.reshape(1, peers * keep)).astype(jnp.bfloat16)
+    summed = jnp.dot(
+        placement, arrived.reshape(peers * keep, rows * BLK), preferred_element_type=jnp.float32
     )
     ffn_share = jnp.swapaxes(summed.reshape(feature_blocks, rows, BLK), 0, 1).reshape(rows, -1)
     return (middle + ffn_share).astype(jnp.bfloat16)

time: 188 us -> 185 us (0.984)
  waiting for transfers between devices: 14.2 us -> 8.64 us
  Pallas kernels: 86.8 us -> 91.6 us
    all_to_all x1 -> x0, starting transfers between devices: 7.28 us -> none  [per_device(): lax.all_to_all(attention, 'head', split_axis=0, concat_axis=1, tiled=True)]
    all_to_all x1 -> x0, waiting for transfers between devices: 6.46 us -> none  [per_device(): lax.all_to_all(attention, 'head', split_axis=0, concat_axis=1, tiled=True)]
    ppermute x0 -> x1, starting transfers between devices: none -> 6.1 us  [per_device(): arrived_half = lax.ppermute(theirs, 'head', [(0, 1), (1, 0)])]
    pallas_call x2, Pallas kernels: 86.8 us -> 91.6 us  [exchange(): pl.pallas_call(functools.partial(exchange_kernel, route, lanes), out_shap...]
where the time goes in v5:
time: 185 us; the launch traced here: 184 us
  Pallas kernels  91.6 us (50%)
  local copies, waits for them, and re-layouts  33.9 us (18%)
  starting transfers between devices  24.5 us (13%)
  matrix products  14.1 us (8%)
  other arithmetic  11.2 us (6%)
  waiting for transfers between devices  8.64 us (5%)
    pallas_call x2, Pallas kernels, exchange(): pl.pallas_call(functools.partial(exchange_kernel, route, lanes), out_shap...  91.6 us
    all_to_all x1, starting transfers between devices, per_device(): lax.all_to_all(jnp.broadcast_to(own_lists, (peers, own_lists.shape[1])),...  11.5 us
    ppermute x2, waiting for transfers between devices, shifted(): return lax.ppermute(block, axis, route)  7.76 us
    ppermute x2, starting transfers between devices, shifted(): return lax.ppermute(block, axis, route)  6.98 us
    dot_general x2, local copies, waits for them, and re-layouts, ffn_terms(): jnp.einsum('sf,kfe->ske', hidden, down_blocks[0], preferred_element_type=...  6.23 us
    ppermute x1, starting transfers between devices, per_device(): arrived_half = lax.ppermute(theirs, 'head', [(0, 1), (1, 0)])  6.1 us
    slice x2, local copies, waits for them, and re-layouts, attend(): tail_keys = child_tails[0].reshape(row_count, tail_size, groups, HD)  5.28 us
    gather x2, local copies, waits for them, and re-layouts, per_device(): pool_pages[:, page_table]  5.2 us
  transfers between devices with their start and end apart: 4, of which 2 were waited for; matrix products, arithmetic and copies ran while one was open for 13% of the time, Pallas kernels for 0%

profile of v5, /device:TPU:1, one launch (start us, length us, event | category | flops | bytes accessed | tf_op | source)
XLA Modules:
  0.0 184.3 jit_solution(14848953137687230270)
XLA Ops:
  0.0 0.0 copy-start
  0.0 0.8 compare_select_fusion
  0.8 0.1 reshape.99
  0.9 0.7 copy-done
  1.6 2.0 %gather_fusion.1 = bf16[64,2,16,512]{3,2,1,0:T(8,128)(2,1)} fusion(bf16[2,64,16,512]{3,2,1,0:T(8,128)(2,1)S(1)} %copy-done, s32[1024]{0:T(1024)S(1)} %pad_clamp_fusion), kind=kCustom, calls=%fused_computation.1 | custom fusion | bytes 4194560 | tf_op jit(solution)/shard_map/gather | solution.py:154
  3.6 0.0 copy-start.5
  3.7 3.2 %copy.38 = bf16[64,2,16,512]{3,2,0,1:T(8,128)(2,1)} copy(bf16[64,2,16,512]{3,2,1,0:T(8,128)(2,1)} %gather_fusion.1) | data formatting | bytes 4194304 | tf_op jit(solution)/shard_map/gather | solution.py:154
  6.8 5.1 %collective-permute-start.1 = (bf16[2,4,256,512]{3,2,1,0:T(8,128)(2,1)}, bf16[2,4,256,512]{3,2,1,0:T(8,128)(2,1)}, u32[]{:S(2)}, u32[]{:S(2)}) collective-permute-start(bf16[2,4,256,512]{3,2,1,0:T(8,128)(2,1)} %bitcast.2), channel_id=1, source_target_pairs={{0,2},{2,4},{4,6},{6,8},{8,10},{10,12},{12,14},{14,16},{16,18},{18... | collective-permute-start | bytes 6291464 | tf_op jit(solution)/shard_map/ppermute | solution.py:80
  11.9 0.0 copy-done.9
  11.9 1.9 %collective-permute-start = (bf16[4]{0:T(256)(128)(2,1)S(1)}, bf16[4]{0:T(256)(128)(2,1)S(1)}, u32[]{:S(2)}, u32[]{:S(2)}) collective-permute-start(bf16[4]{0:T(256)(128)(2,1)S(1)} %convert_element_type.63), channel_id=1, source_target_pairs={{0,2},{2,4},{4,6},{6,8},{8,10},{10,12},{12,14},{14,16},{16,18},{18... | collective-permute-start | bytes 32 | tf_op jit(solution)/shard_map/ppermute | solution.py:80
  13.9 0.0 copy-done.10
  13.9 0.0 copy-done.11
  13.9 0.1 add_bitcast_fusion
  14.0 0.7 broadcast_in_dim.45
  14.6 11.5 %all-to-all-start = ((s32[128,1,64]{2,1,0:T(1,128)}), s32[128,1,64]{2,1,0:T(1,128)S(1)}, u32[]{:S(2)}, u32[]{:S(2)}) async-start(s32[128,1,64]{2,1,0:T(1,128)} %broadcast_in_dim.45), calls=%async_computation | async-start | bytes 131072 | tf_op jit(solution)/shard_map/all_to_all | solution.py:179
  26.1 0.0 copy-done.5
  26.1 1.6 copy.46
  27.8 0.1 fusion.25
  27.9 7.8 %collective-permute-done = bf16[4]{0:T(256)(128)(2,1)S(1)} collective-permute-done((bf16[4]{0:T(256)(128)(2,1)S(1)}, bf16[4]{0:T(256)(128)(2,1)S(1)}, u32[]{:S(2)}, u32[]{:S(2)}) %collective-permute-start) | collective-permute-done | bytes 40 | tf_op jit(solution)/shard_map/ppermute | solution.py:80
  35.7 0.1 maximum_convert_fusion
  35.8 0.6 gather_fusion
  36.4 0.1 iota_compare_fusion.3
  36.5 0.0 collective-permute-done.1
  36.5 4.5 %pad_maximum_fusion = bf16[2,8,256,512]{3,2,1,0:T(8,128)(2,1)} fusion(bf16[2,4,256,512]{3,2,1,0:T(8,128)(2,1)} %bitcast.2, bf16[2,4,256,512]{3,2,1,0:T(8,128)(2,1)} %collective-permute-done.1), kind=kLoop, calls=%fused_computation.4 | loop fusion | flops 2097152 | bytes 8388608 | tf_op jit(solution)/shard_map/concatenate | solution.py:157
  41.0 4.2 %gather_fusion.2 = bf16[4,2,256,512]{3,2,1,0:T(8,128)(2,1)} fusion(bf16[2,8,256,512]{3,2,1,0:T(8,128)(2,1)} %pad_maximum_fusion, s32[1024]{0:T(1024)S(1)} %pad_clamp_fusion.1), kind=kCustom, calls=%fused_computation.2 | custom fusion | bytes 4194320 | tf_op jit(solution)/shard_map/gather | solution.py:160
  45.2 3.0 %fusion.38 = (bf16[1,4,256,512]{3,2,0,1:T(8,128)(2,1)}, bf16[1,4,256,512]{3,2,0,1:T(8,128)(2,1)}) fusion(bf16[2,4,256,512]{3,2,0,1:T(8,128)(2,1)} %bitcast.85), kind=kLoop, calls=%fused_computation.78 | loop fusion | bytes 4194304 | tf_op jit(solution)/shard_map/slice | solution.py:89
  48.2 2.3 %copy.39 = bf16[1,4,256,512]{2,3,1,0:T(8,128)(2,1)} copy(bf16[1,4,256,512]{3,2,0,1:T(8,128)(2,1)} %get-tuple-element.9) | data formatting | bytes 2097152 | tf_op jit(solution)/shard_map/slice | solution.py:89
  50.5 1.6 select_reduce_fusion
  52.1 0.2 bitcast_reduce_fusion
  52.3 0.0 copy-start.1
  52.3 0.0 copy-start.3
  52.3 2.3 %copy.41 = bf16[1,4,256,512]{2,3,1,0:T(8,128)(2,1)} copy(bf16[1,4,256,512]{3,2,0,1:T(8,128)(2,1)} %get-tuple-element.10) | data formatting | bytes 2097152 | tf_op jit(solution)/shard_map/slice | solution.py:90
  54.6 1.6 fusion.1
  56.3 6.1 %collective-permute-start.2 = (bf16[2,4096]{1,0:T(2,128)(2,1)S(1)}, bf16[2,4096]{1,0:T(2,128)(2,1)S(1)}, u32[]{:S(2)}, u32[]{:S(2)}) collective-permute-start(bf16[2,4096]{1,0:T(2,128)(2,1)S(1)} %get-tuple-element.13), channel_id=1, source_target_pairs={{0,1},{1,0},{2,3},{3,2},{4,5},{5,4},{6,7},{7,6},{8,9},{9,8},{10,11... | collective-permute-start | bytes 49160 | tf_op jit(solution)/shard_map/ppermute | solution.py:167
  62.4 0.0 all-to-all-done
  62.4 0.1 fusion.39
  62.5 0.1 eq.38
  62.6 0.1 eq.35
  62.7 0.9 collective-permute-done.2
  63.5 0.2 multiply_reduce_fusion.4
  63.8 0.0 copy-done.3
  63.8 0.1 multiply_convert_fusion.4
  63.9 2.0 %convolution_convert_fusion = bf16[4096,256]{1,0:T(8,128)(2,1)} fusion(s32[4096]{0:T(1024)S(1)} %eq.38, bf16[8,8,2,128]{3,2,1,0:T(2,128)(2,1)S(1)} %bitcast.95), kind=kOutput, calls=%fused_computation.3 | convolution fusion | flops 135528448 | bytes 2146304 | tf_op jit(solution)/shard_map/dot_general | solution.py:193
  65.9 50.2 %shard_map.163 = bf16[128,32,256]{2,1,0:T(8,128)(2,1)} custom-call(bf16[128,32,256]{2,1,0:T(8,128)(2,1)} %bitcast.87), custom_call_target="tpu_custom_call" | custom-call | tf_op jit(solution)/shard_map/pallas_call | solution.py:67
  116.1 0.0 copy-start.7
  116.1 0.0 copy-start.13
  116.2 2.0 %fusion.37 = (bf16[128,32,128]{2,1,0:T(8,128)(2,1)S(1)}, bf16[128,32,128]{2,1,0:T(8,128)(2,1)S(1)}) fusion(bf16[128,32,256]{2,1,0:T(8,128)(2,1)} %shard_map.163), kind=kLoop, calls=%fused_computation.77 | loop fusion | bytes 4194304 | tf_op jit(solution)/shard_map/slice | solution.py:199
  118.2 0.7 multiply_reduce_fusion
  118.9 0.0 copy-start.8
  118.9 0.0 copy-start.14
  118.9 0.7 multiply_reduce_fusion.2
  119.6 0.5 copy-done.8
  120.1 0.7 multiply_reduce_fusion.1
  120.8 0.7 multiply_reduce_fusion.3
  121.6 1.8 fusion.22
  123.3 3.1 %copy.51 = f32[128,32,128]{2,1,0:T(8,128)} copy(f32[128,32,128]{0,2,1:T(8,128)} %bitcast.88) | data formatting | bytes 4194304 | tf_op jit(solution)/shard_map/sf,kfe->ske/dot_general | solution.py:128
  126.5 1.8 fusion.21
  128.3 3.1 %copy.47 = f32[128,32,128]{2,1,0:T(8,128)} copy(f32[128,32,128]{0,2,1:T(8,128)} %bitcast.86) | data formatting | bytes 4194304 | tf_op jit(solution)/shard_map/sf,kfe->ske/dot_general | solution.py:128
  131.4 2.8 %multiply_convert_fusion.1 = (bf16[128,32,128]{2,1,0:T(8,128)(2,1)S(1)}, bf16[128,32,128]{2,1,0:T(8,128)(2,1)S(1)}) fusion(f32[128,32,128]{2,1,0:T(8,128)} %copy.47, f32[32]{0:T(128)S(1)} %bitcast.101, f32[128,32,128]{2,1,0:T(8,128)} %copy.51), kind=kLoop, calls=%fused_computation.9 | loop fusion | flops 2097152 | bytes 6291584 | tf_op jit(solution)/shard_map/convert_element_type | solution.py:130
  134.1 1.6 pad_maximum_fusion.1.x_ref
  135.8 41.4 %shard_map.164 = bf16[128,32,256]{2,1,0:T(8,128)(2,1)} custom-call(bf16[128,32,256]{2,1,0:T(8,128)(2,1)} %pad_maximum_fusion.1.x_ref), custom_call_target="tpu_custom_call" | custom-call | tf_op jit(solution)/shard_map/pallas_call | solution.py:67
  177.1 4.1 %copy.52 = bf16[256,4096]{1,0:T(8,128)(2,1)} copy(bf16[256,4096]{0,1:T(8,128)(2,1)} %bitcast.90) | data formatting | bytes 4194304 | tf_op jit(solution)/shard_map/dot_general | solution.py:211
  181.3 2.4 %convolution_bitcast_fusion = f32[1,2,64,128]{3,2,1,0:T(8,128)S(1)} fusion(bf16[2,128,4096]{2,1,0:T(8,128)(2,1)} %bitcast.89, s32[4096]{0:T(1024)S(1)} %eq.35), kind=kOutput, calls=%fused_computation.15 | convolution fusion | flops 134479872 | bytes 2179072 | tf_op jit(solution)/shard_map/dot_general | solution.py:211
  183.6 0.7 fusion.16
  (26 shorter events, 0.2 us)
Async XLA Ops:
  0.0 1.6 copy-start
  3.6 8.3 %copy-start.9 = (s32[4]{0:T(128)S(1)}, s32[4]{0:T(128)}, u32[]{:S(2)}) copy-start(s32[4]{0:T(128)} %param.22) | copy-start | bytes 52
  3.6 10.2 %copy-start.10 = (s32[1,32]{1,0:T(1,128)S(1)}, s32[1,32]{1,0:T(1,128)}, u32[]{:S(2)}) copy-start(s32[1,32]{1,0:T(1,128)} %param.32) | copy-start | bytes 388
  3.6 10.2 %copy-start.11 = (s32[1,32]{1,0:T(1,128)S(1)}, s32[1,32]{1,0:T(1,128)}, u32[]{:S(2)}) copy-start(s32[1,32]{1,0:T(1,128)} %param.28) | copy-start | bytes 388
  3.6 22.5 %copy-start.4 = (bf16[4,512]{1,0:T(4,128)(2,1)S(1)}, bf16[4,512]{1,0:T(4,128)(2,1)}, u32[]{:S(2)}) copy-start(bf16[4,512]{1,0:T(4,128)(2,1)} %param.18) | copy-start | bytes 12292
  3.6 22.5 %copy-start.5 = (bf16[4,512]{1,0:T(4,128)(2,1)S(1)}, bf16[4,512]{1,0:T(4,128)(2,1)}, u32[]{:S(2)}) copy-start(bf16[4,512]{1,0:T(4,128)(2,1)} %param.19) | copy-start | bytes 12292
  6.8 20.9 %copy-start.12 = (s32[4]{0:T(128)S(1)}, s32[4]{0:T(128)}, u32[]{:S(2)}) copy-start(s32[4]{0:T(128)} %param.23) | copy-start | bytes 52
  6.8 21.0 %copy-start.2 = (bf16[4,4096]{1,0:T(4,128)(2,1)S(1)}, bf16[4,4096]{1,0:T(4,128)(2,1)}, u32[]{:S(2)}) copy-start(bf16[4,4096]{1,0:T(4,128)(2,1)} %param.17) | copy-start | bytes 98308
  6.8 29.7 %collective-permute-start.1 = (bf16[2,4,256,512]{3,2,1,0:T(8,128)(2,1)}, bf16[2,4,256,512]{3,2,1,0:T(8,128)(2,1)}, u32[]{:S(2)}, u32[]{:S(2)}) collective-permute-start(bf16[2,4,256,512]{3,2,1,0:T(8,128)(2,1)} %bitcast.2), channel_id=1, source_target_pairs={{0,2},{2,4},{4,6},{6,8},{8,10},{10,12},{12,14},{14,16},{16,18},{18... | collective-permute-start | bytes 6291464 | tf_op jit(solution)/shard_map/ppermute | solution.py:80
  11.9 23.8 %collective-permute-start = (bf16[4]{0:T(256)(128)(2,1)S(1)}, bf16[4]{0:T(256)(128)(2,1)S(1)}, u32[]{:S(2)}, u32[]{:S(2)}) collective-permute-start(bf16[4]{0:T(256)(128)(2,1)S(1)} %convert_element_type.63), channel_id=1, source_target_pairs={{0,2},{2,4},{4,6},{6,8},{8,10},{10,12},{12,14},{14,16},{16,18},{18... | collective-permute-start | bytes 32 | tf_op jit(solution)/shard_map/ppermute | solution.py:80
  14.6 47.8 %all-to-all-start = ((s32[128,1,64]{2,1,0:T(1,128)}), s32[128,1,64]{2,1,0:T(1,128)S(1)}, u32[]{:S(2)}, u32[]{:S(2)}) async-start(s32[128,1,64]{2,1,0:T(1,128)} %broadcast_in_dim.45), calls=%async_computation | async-start | bytes 131072 | tf_op jit(solution)/shard_map/all_to_all | solution.py:179
  52.3 11.3 %copy-start.1 = (bf16[2,8192]{1,0:T(2,128)(2,1)S(1)}, bf16[2,8192]{1,0:T(2,128)(2,1)}, u32[]{:S(2)}) copy-start(bf16[2,8192]{1,0:T(2,128)(2,1)} %param.24) | copy-start | bytes 98308
  52.3 11.5 %copy-start.3 = (f32[8192]{0:T(1024)S(1)}, f32[8192]{0:T(1024)}, u32[]{:S(2)}) copy-start(f32[8192]{0:T(1024)} %param.25) | copy-start | bytes 98308
  56.3 7.2 %collective-permute-start.2 = (bf16[2,4096]{1,0:T(2,128)(2,1)S(1)}, bf16[2,4096]{1,0:T(2,128)(2,1)S(1)}, u32[]{:S(2)}, u32[]{:S(2)}) collective-permute-start(bf16[2,4096]{1,0:T(2,128)(2,1)S(1)} %get-tuple-element.13), channel_id=1, source_target_pairs={{0,1},{1,0},{2,3},{3,2},{4,5},{5,4},{6,7},{7,6},{8,9},{9,8},{10,11... | collective-permute-start | bytes 49160 | tf_op jit(solution)/shard_map/ppermute | solution.py:167
  116.1 2.0 %copy-start.7 = (bf16[1,32,128,128]{3,2,1,0:T(8,128)(2,1)S(1)}, bf16[1,32,128,128]{3,2,1,0:T(8,128)(2,1)}, u32[]{:S(2)}) copy-start(bf16[1,32,128,128]{3,2,1,0:T(8,128)(2,1)} %param.27) | copy-start | bytes 3145732
  116.1 2.0 %copy-start.13 = (f32[1,32]{1,0:T(1,128)S(1)}, f32[1,32]{1,0:T(1,128)}, u32[]{:S(2)}) copy-start(f32[1,32]{1,0:T(1,128)} %param.30) | copy-start | bytes 388
  118.9 1.2 copy-start.8
  118.9 1.2 copy-start.14
  128.2 3.1 %copy-start.6 = (f32[1,32]{1,0:T(1,128)S(1)}, f32[1,32]{1,0:T(1,128)}, u32[]{:S(2)}) copy-start(f32[1,32]{1,0:T(1,128)} %param.33) | copy-start | bytes 388

commit v6 on v5

--- a/solution.py
+++ b/solution.py
@@ -80,39 +80,57 @@
     return lax.ppermute(block, axis, route)
 
 
-def attend(branch_query, key_new, value_new, child_tails, child_length):
+def attend(branch_query, key_new, value_new, pools, tables, lengths, source, row):
     row_count = branch_query.shape[0]
     groups = key_new.shape[1] // HD
     per_group = branch_query.shape[1] // (groups * HD)
-    tail_size = child_tails.shape[2]
+    pages, page_size = pools[0].shape[1], pools[0].shape[2]
     queries = branch_query.reshape(row_count, groups, per_group, HD)
-    tail_keys = child_tails[0].reshape(row_count, tail_size, groups, HD)
-    tail_values = child_tails[1].reshape(row_count, tail_size, groups, HD)
     own_keys = key_new.reshape(row_count, groups, HD)
     own_values = value_new.reshape(row_count, groups, HD)
     factor = 1.0 / math.sqrt(HD)
-    tail_scores = (
-        jnp.einsum("rgjd,rtgd->rgjt", queries, tail_keys, preferred_element_type=jnp.float32)
-        * factor
-    )
+    page_ids = jnp.arange(pages, dtype=jnp.int32)
+    slots = jnp.arange(tables[0].shape[1], dtype=jnp.int32)
+    offsets = jnp.arange(page_size, dtype=jnp.int32)
+    scores, masks = [], []
+    for which, (pool, table, length) in enumerate(zip(pools, tables, lengths)):
+        parent_table = table[row]
+        match = parent_table[:, None, :] == page_ids[None, :, None]
+        slot = jnp.sum(jnp.where(match, slots[None, None, :], 0), axis=-1)
+        found = jnp.any(match, axis=-1) & (source == which)[:, None]
+        live = found[:, :, None] & (
+            slot[:, :, None] * page_size + offsets[None, None, :] < length[row][:, None, None]
+        )
+        keys = pool[0].reshape(pages * page_size, groups, HD)
+        part = (
+            jnp.einsum("rgjd,tgd->rgjt", queries, keys, preferred_element_type=jnp.float32)
+            * factor
+        )
+        scores.append(part)
+        masks.append(live.reshape(row_count, 1, 1, pages * page_size))
+    tail_scores = jnp.concatenate(scores, axis=-1)
+    live_mask = jnp.concatenate(masks, axis=-1)
     own_scores = (
         jnp.einsum("rgjd,rgd->rgj", queries, own_keys, preferred_element_type=jnp.float32) * factor
     )
-    live_mask = (jnp.arange(tail_size, dtype=jnp.float32)[None, :] < child_length[:, None])[
-        :, None, None, :
-    ]
     top_score = jnp.maximum(jnp.max(jnp.where(live_mask, tail_scores, -1e30), axis=-1), own_scores)
     tail_exp = jnp.where(live_mask, jnp.exp(tail_scores - top_score[..., None]), 0.0)
     own_exp = jnp.exp(own_scores - top_score)
     totals = jnp.sum(tail_exp, axis=-1) + own_exp
     tail_weights = (tail_exp / totals[..., None]).astype(jnp.bfloat16)
     own_weights = (own_exp / totals).astype(jnp.bfloat16)
-    mixture = jnp.einsum(
-        "rgjt,rtgd->rgjd", tail_weights, tail_values, preferred_element_type=jnp.float32
-    )
-    mixture = mixture + own_weights[..., None].astype(jnp.float32) * own_values[
-        :, :, None, :
-    ].astype(jnp.float32)
+    span = pages * page_size
+    mixture = own_weights[..., None].astype(jnp.float32) * own_values[:, :, None, :].astype(
+        jnp.float32
+    )
+    for which, pool in enumerate(pools):
+        values = pool[1].reshape(span, groups, HD)
+        mixture = mixture + jnp.einsum(
+            "rgjt,tgd->rgjd",
+            tail_weights[..., which * span : (which + 1) * span],
+            values,
+            preferred_element_type=jnp.float32,
+        )
     return mixture.reshape(row_count, -1).astype(jnp.bfloat16)
 
 
@@ -150,16 +168,18 @@
     down_scale,
 ):
     row_count = branch_query.shape[0]
-    tail_size = page_table.shape[1] * pool_pages.shape[2]
-    own_tails = pool_pages[:, page_table].reshape(2, row_count, tail_size, pool_pages.shape[3])
-    own_length = tail_length.astype(jnp.bfloat16)
-    prior_tails, prior_length = shifted((own_tails, own_length), "wide", 1)
-    both_tails = jnp.concatenate([prior_tails, own_tails], axis=1)
-    both_length = jnp.concatenate([prior_length, own_length]).astype(jnp.float32)
+    prior = shifted((pool_pages, page_table, tail_length), "wide", 1)
     local_parent = parent_row - (lax.axis_index("wide") - 1) * row_count
-    child_tails = both_tails[:, local_parent]
-    child_length = both_length[local_parent]
-    attention = attend(branch_query, key_new, value_new, child_tails, child_length)
+    attention = attend(
+        branch_query,
+        key_new,
+        value_new,
+        (prior[0], pool_pages),
+        (prior[1], page_table),
+        (prior[2], tail_length),
+        local_parent // row_count,
+        local_parent % row_count,
+    )
     half = residual.shape[0]
     here = lax.axis_index("head")
     mine = lax.dynamic_slice_in_dim(attention, here * half, half, axis=0)

time: 185 us -> 172 us (0.930)
  waiting for transfers between devices: 8.64 us -> 0.89 us
  local copies, waits for them, and re-layouts: 33.9 us -> 30.8 us
  starting transfers between devices: 24.5 us -> 27.5 us
  Pallas kernels: 91.6 us -> 88.9 us
  other arithmetic: 11.2 us -> 8.62 us
    ppermute x2 -> x3, waiting for transfers between devices: 7.76 us -> 0.01 us  [shifted(): return lax.ppermute(block, axis, route)]
    gather x4, local copies, waits for them, and re-layouts: 10 us -> 3.74 us  [the longest x2 1.94 us: attend(): length[row][:, None, None]]
    another operation x0 -> x4, local copies, waits for them, and re-layouts: none -> 5.99 us  [the longest x2 3.53 us: attend(): keys = pool[0].reshape(pages * page_size, groups, HD)]
    concatenate x1 -> x0, other arithmetic: 4.53 us -> none  [per_device(): both_tails = jnp.concatenate([prior_tails, own_tails], axis=1)]
    ppermute x2 -> x3, starting transfers between devices: 6.98 us -> 10.9 us  [shifted(): return lax.ppermute(block, axis, route)]
    pallas_call x2, Pallas kernels: 91.6 us -> 88.9 us  [exchange(): pl.pallas_call(functools.partial(exchange_kernel, route, lanes), out_shap...]
    slice x3 -> x2, local copies, waits for them, and re-layouts: 7.56 us -> 5.78 us  [the longest x1 3.08 us: attend(): values = pool[1].reshape(span, groups, HD)]
    dot_general x2 -> x4, matrix products: 3.2 us -> 4.98 us  [the longest x2 2.83 us: attend(): jnp.einsum('rgjt,tgd->rgjd', tail_weights[..., which * span:(which + 1) *...]
  transfers between devices with their start and end apart: 4 -> 5, of which waited for: 2 -> 1; matrix products, arithmetic and copies ran while one was open for 13% -> 16% of each run, Pallas kernels for 0% -> 0%
where the time goes in v6:
time: 172 us; the launch traced here: 171 us
  Pallas kernels  88.9 us (52%)
  local copies, waits for them, and re-layouts  30.8 us (18%)
  starting transfers between devices  27.5 us (16%)
  matrix products  14.3 us (8%)
  other arithmetic  8.62 us (5%)
    pallas_call x2, Pallas kernels, exchange(): pl.pallas_call(functools.partial(exchange_kernel, route, lanes), out_shap...  88.9 us
    ppermute x3, starting transfers between devices, shifted(): return lax.ppermute(block, axis, route)  10.9 us
    all_to_all x1, starting transfers between devices, per_device(): lax.all_to_all(jnp.broadcast_to(own_lists, (peers, own_lists.shape[1])),...  10.4 us
    dot_general x2, local copies, waits for them, and re-layouts, ffn_terms(): jnp.einsum('sf,kfe->ske', hidden, down_blocks[0], preferred_element_type=...  6.36 us
    ppermute x1, starting transfers between devices, per_device(): arrived_half = lax.ppermute(theirs, 'head', [(0, 1), (1, 0)])  6.1 us
    another operation x2, local copies, waits for them, and re-layouts, attend(): keys = pool[0].reshape(pages * page_size, groups, HD)  3.53 us
    unnamed x2, matrix products  3.53 us
  transfers between devices with their start and end apart: 5, of which 1 were waited for; matrix products, arithmetic and copies ran while one was open for 16% of the time, Pallas kernels for 0%

profile of v6, /device:TPU:1, one launch (start us, length us, event | category | flops | bytes accessed | tf_op | source)
XLA Modules:
  0.0 171.4 jit_solution(17027749059765537805)
XLA Ops:
  0.0 5.1 %collective-permute-start = (s32[4,16]{1,0:T(4,128)}, s32[4,16]{1,0:T(4,128)S(1)}, u32[]{:S(2)}, u32[]{:S(2)}) collective-permute-start(s32[4,16]{1,0:T(4,128)} %param.21), channel_id=1, source_target_pairs={{0,2},{2,4},{4,6},{6,8},{8,10},{10,12},{12,14},{14,16},{16,18},{18... | collective-permute-start | bytes 776 | tf_op jit(solution)/shard_map/ppermute | solution.py:80
  5.1 1.9 %collective-permute-start.1 = (s32[4]{0:T(128)}, s32[4]{0:T(128)S(1)}, u32[]{:S(2)}, u32[]{:S(2)}) collective-permute-start(s32[4]{0:T(128)} %param.22), channel_id=1, source_target_pairs={{0,2},{2,4},{4,6},{6,8},{8,10},{10,12},{12,14},{14,16},{16,18},{18... | collective-permute-start | bytes 56 | tf_op jit(solution)/shard_map/ppermute | solution.py:80
  7.0 3.9 %collective-permute-start.2 = (bf16[2,64,16,512]{3,2,1,0:T(8,128)(2,1)}, bf16[2,64,16,512]{3,2,1,0:T(8,128)(2,1)}, u32[]{:S(2)}, u32[]{:S(2)}) collective-permute-start(bf16[2,64,16,512]{3,2,1,0:T(8,128)(2,1)} %param.20), channel_id=1, source_target_pairs={{0,2},{2,4},{4,6},{6,8},{8,10},{10,12},{12,14},{14,16},{16,18},{18... | collective-permute-start | bytes 6291464 | tf_op jit(solution)/shard_map/ppermute | solution.py:80
  10.9 0.7 add_bitcast_fusion.1
  11.7 0.7 broadcast_in_dim.95
  12.3 10.4 %all-to-all-start = ((s32[128,1,64]{2,1,0:T(1,128)}), s32[128,1,64]{2,1,0:T(1,128)S(1)}, u32[]{:S(2)}, u32[]{:S(2)}) async-start(s32[128,1,64]{2,1,0:T(1,128)} %broadcast_in_dim.95), calls=%async_computation | async-start | bytes 131072 | tf_op jit(solution)/shard_map/all_to_all | solution.py:199
  22.8 0.7 broadcast_compare_fusion.1
  23.5 1.2 gather_fusion.2
  24.7 0.1 fusion.31
  24.8 0.1 select_reduce_fusion.1
  24.9 1.3 gather_fusion.3
  26.3 0.1 and.79
  26.4 0.1 and.80
  26.6 0.1 add.95
  26.7 0.1 add.96
  26.9 2.7 %fusion.44 = (bf16[1,64,16,512]{3,2,1,0:T(8,128)(2,1)}, bf16[1,64,16,512]{3,2,1,0:T(8,128)(2,1)S(1)}) fusion(bf16[2,64,16,512]{3,2,1,0:T(8,128)(2,1)} %param.20), kind=kLoop, calls=%fused_computation.104 | loop fusion | bytes 4194304 | tf_op jit(solution)/shard_map/slice | solution.py:104
  29.6 1.4 reshape_squeeze.13
  31.0 1.1 reshape_squeeze.15
  32.1 0.1 fusion.46
  32.2 0.5 fusion
  32.7 1.6 copy.73
  34.4 0.6 gather_fusion.1
  35.0 0.6 gather_fusion
  35.6 0.1 fusion.32
  35.7 0.1 and.74
  35.8 0.1 and.75
  36.0 0.1 select_reduce_fusion.2
  36.1 0.1 add.92
  36.2 0.1 add.93
  36.3 0.1 fusion.35
  36.4 3.1 %fusion.43 = (bf16[1,64,16,512]{3,2,1,0:T(8,128)(2,1)}, bf16[1,64,16,512]{3,2,1,0:T(8,128)(2,1)}) fusion(bf16[2,64,16,512]{3,2,1,0:T(8,128)(2,1)} %collective-permute-done.2), kind=kLoop, calls=%fused_computation.103 | loop fusion | bytes 4194304 | tf_op jit(solution)/shard_map/slice | solution.py:127
  39.5 2.2 %reshape_squeeze.12 = bf16[1024,4,128]{2,1,0:T(4,128)(2,1)} reshape(bf16[1,64,16,512]{3,2,1,0:T(8,128)(2,1)} %get-tuple-element.13) | data formatting | bytes 2097152 | tf_op jit(solution)/shard_map/reshape;squeeze | solution.py:104
  41.7 1.7 fusion.1
  43.3 0.2 select_reduce_fusion
  43.6 0.4 fusion.20
  43.9 1.1 divide_convert_fusion
  45.1 1.3 reshape_squeeze.14
  46.4 1.6 convolution_bitcast_fusion
  48.0 1.2 fusion.4
  49.4 6.1 %collective-permute-start.3 = (bf16[2,4096]{1,0:T(2,128)(2,1)S(1)}, bf16[2,4096]{1,0:T(2,128)(2,1)S(1)}, u32[]{:S(2)}, u32[]{:S(2)}) collective-permute-start(bf16[2,4096]{1,0:T(2,128)(2,1)S(1)} %get-tuple-element.18), channel_id=1, source_target_pairs={{0,1},{1,0},{2,3},{3,2},{4,5},{5,4},{6,7},{7,6},{8,9},{9,8},{10,11... | collective-permute-start | bytes 49160 | tf_op jit(solution)/shard_map/ppermute | solution.py:187
  55.5 0.1 fusion.45
  55.5 0.1 eq.80
  55.6 0.1 eq.77
  55.7 0.9 collective-permute-done.3
  56.6 0.2 multiply_reduce_fusion.4
  56.8 0.1 multiply_convert_fusion.4
  56.9 2.0 %convolution_convert_fusion = bf16[4096,256]{1,0:T(8,128)(2,1)} fusion(s32[4096]{0:T(1024)S(1)} %eq.80, bf16[8,8,2,128]{3,2,1,0:T(2,128)(2,1)S(1)} %bitcast.129), kind=kOutput, calls=%fused_computation.4 | convolution fusion | flops 135528448 | bytes 2146304 | tf_op jit(solution)/shard_map/dot_general | solution.py:213
  59.0 47.8 %shard_map.163 = bf16[128,32,256]{2,1,0:T(8,128)(2,1)} custom-call(bf16[128,32,256]{2,1,0:T(8,128)(2,1)} %bitcast.119), custom_call_target="tpu_custom_call" | custom-call | tf_op jit(solution)/shard_map/pallas_call | solution.py:67
  106.8 1.9 %fusion.42 = (bf16[128,32,128]{2,1,0:T(8,128)(2,1)S(1)}, bf16[128,32,128]{2,1,0:T(8,128)(2,1)S(1)}) fusion(bf16[128,32,256]{2,1,0:T(8,128)(2,1)} %shard_map.163), kind=kLoop, calls=%fused_computation.102 | loop fusion | bytes 4194304 | tf_op jit(solution)/shard_map/slice | solution.py:219
  108.7 0.7 multiply_reduce_fusion
  109.5 0.7 multiply_reduce_fusion.2
  110.2 0.5 copy-done.8
  110.7 0.7 multiply_reduce_fusion.1
  111.4 0.7 multiply_reduce_fusion.3
  112.1 1.8 %fusion.26 = f32[128,4096]{0,1} fusion(bf16[128,4096]{0,1:T(8,128)(2,1)S(1)} %bitcast.116, f32[128,128]{1,0:T(8,128)S(1)} %multiply_reduce_fusion, f32[128,128]{1,0:T(8,128)S(1)} %multiply_reduce_fusion.1), kind=kOutput, calls=%fused_computation.55 | convolution fusion | flops 134316032 | bytes 3276800
  113.9 3.1 %copy.78 = f32[128,32,128]{2,1,0:T(8,128)} copy(f32[128,32,128]{0,2,1:T(8,128)} %bitcast.120) | data formatting | bytes 4194304 | tf_op jit(solution)/shard_map/sf,kfe->ske/dot_general | solution.py:146
  117.0 1.8 %fusion.25 = f32[128,4096]{0,1} fusion(bf16[128,4096]{0,1:T(8,128)(2,1)S(1)} %bitcast.117, f32[128,128]{1,0:T(8,128)S(1)} %multiply_reduce_fusion.2, f32[128,128]{1,0:T(8,128)S(1)} %multiply_reduce_fusion.3), kind=kOutput, calls=%fused_computation.54 | convolution fusion | flops 134316032 | bytes 3276800
  118.8 3.2 %copy.74 = f32[128,32,128]{2,1,0:T(8,128)} copy(f32[128,32,128]{0,2,1:T(8,128)} %bitcast.118) | data formatting | bytes 4194304 | tf_op jit(solution)/shard_map/sf,kfe->ske/dot_general | solution.py:146
  122.0 2.2 %multiply_convert_fusion.1 = (bf16[128,32,128]{2,1,0:T(8,128)(2,1)S(1)}, bf16[128,32,128]{2,1,0:T(8,128)(2,1)S(1)}) fusion(f32[128,32,128]{2,1,0:T(8,128)} %copy.74, f32[32]{0:T(128)S(1)} %bitcast.135, f32[128,32,128]{2,1,0:T(8,128)S(1)} %copy-done.1), kind=kLoop, calls=%fused_computation.9 | loop fusion | flops 2097152 | bytes 6291584 | tf_op jit(solution)/shard_map/convert_element_type | solution.py:148
  124.2 1.7 pad_maximum_fusion.x_ref
  125.9 41.1 %shard_map.164 = bf16[128,32,256]{2,1,0:T(8,128)(2,1)} custom-call(bf16[128,32,256]{2,1,0:T(8,128)(2,1)} %pad_maximum_fusion.x_ref), custom_call_target="tpu_custom_call" | custom-call | tf_op jit(solution)/shard_map/pallas_call | solution.py:67
  167.0 2.9 %copy.79 = bf16[256,4096]{1,0:T(8,128)(2,1)S(1)} copy(bf16[256,4096]{0,1:T(8,128)(2,1)} %bitcast.122) | data formatting | bytes 4194304 | tf_op jit(solution)/shard_map/dot_general | solution.py:231
  169.9 0.8 convolution_bitcast_fusion.2
  170.7 0.7 fusion.24
  (43 shorter events, 0.5 us)
Async XLA Ops:
  0.0 108.7 %copy-start = (bf16[1,32,128,128]{3,2,1,0:T(8,128)(2,1)S(1)}, bf16[1,32,128,128]{3,2,1,0:T(8,128)(2,1)}, u32[]{:S(2)}) copy-start(bf16[1,32,128,128]{3,2,1,0:T(8,128)(2,1)} %param.27) | copy-start | bytes 3145732
  0.0 35.0 %collective-permute-start = (s32[4,16]{1,0:T(4,128)}, s32[4,16]{1,0:T(4,128)S(1)}, u32[]{:S(2)}, u32[]{:S(2)}) collective-permute-start(s32[4,16]{1,0:T(4,128)} %param.21), channel_id=1, source_target_pairs={{0,2},{2,4},{4,6},{6,8},{8,10},{10,12},{12,14},{14,16},{16,18},{18... | collective-permute-start | bytes 776 | tf_op jit(solution)/shard_map/ppermute | solution.py:80
  5.1 29.3 %collective-permute-start.1 = (s32[4]{0:T(128)}, s32[4]{0:T(128)S(1)}, u32[]{:S(2)}, u32[]{:S(2)}) collective-permute-start(s32[4]{0:T(128)} %param.22), channel_id=1, source_target_pairs={{0,2},{2,4},{4,6},{6,8},{8,10},{10,12},{12,14},{14,16},{16,18},{18... | collective-permute-start | bytes 56 | tf_op jit(solution)/shard_map/ppermute | solution.py:80
  7.0 29.4 %collective-permute-start.2 = (bf16[2,64,16,512]{3,2,1,0:T(8,128)(2,1)}, bf16[2,64,16,512]{3,2,1,0:T(8,128)(2,1)}, u32[]{:S(2)}, u32[]{:S(2)}) collective-permute-start(bf16[2,64,16,512]{3,2,1,0:T(8,128)(2,1)} %param.20), channel_id=1, source_target_pairs={{0,2},{2,4},{4,6},{6,8},{8,10},{10,12},{12,14},{14,16},{16,18},{18... | collective-permute-start | bytes 6291464 | tf_op jit(solution)/shard_map/ppermute | solution.py:80
  12.3 43.1 %all-to-all-start = ((s32[128,1,64]{2,1,0:T(1,128)}), s32[128,1,64]{2,1,0:T(1,128)S(1)}, u32[]{:S(2)}, u32[]{:S(2)}) async-start(s32[128,1,64]{2,1,0:T(1,128)} %broadcast_in_dim.95), calls=%async_computation | async-start | bytes 131072 | tf_op jit(solution)/shard_map/all_to_all | solution.py:199
  29.6 1.4 copy-start.5
  29.6 2.5 %copy-start.6 = (bf16[4,512]{1,0:T(4,128)(2,1)S(1)}, bf16[4,512]{1,0:T(4,128)(2,1)}, u32[]{:S(2)}) copy-start(bf16[4,512]{1,0:T(4,128)(2,1)} %param.19) | copy-start | bytes 12292
  29.6 2.5 %copy-start.3 = (bf16[4,4096]{1,0:T(4,128)(2,1)S(1)}, bf16[4,4096]{1,0:T(4,128)(2,1)}, u32[]{:S(2)}) copy-start(bf16[4,4096]{1,0:T(4,128)(2,1)} %param.17) | copy-start | bytes 98308
  46.4 10.2 %copy-start.2 = (bf16[2,8192]{1,0:T(2,128)(2,1)S(1)}, bf16[2,8192]{1,0:T(2,128)(2,1)}, u32[]{:S(2)}) copy-start(bf16[2,8192]{1,0:T(2,128)(2,1)} %param.24) | copy-start | bytes 98308
  46.4 10.4 %copy-start.4 = (f32[8192]{0:T(1024)S(1)}, f32[8192]{0:T(1024)}, u32[]{:S(2)}) copy-start(f32[8192]{0:T(1024)} %param.25) | copy-start | bytes 98308
  49.4 7.2 %collective-permute-start.3 = (bf16[2,4096]{1,0:T(2,128)(2,1)S(1)}, bf16[2,4096]{1,0:T(2,128)(2,1)S(1)}, u32[]{:S(2)}, u32[]{:S(2)}) collective-permute-start(bf16[2,4096]{1,0:T(2,128)(2,1)S(1)} %get-tuple-element.18), channel_id=1, source_target_pairs={{0,1},{1,0},{2,3},{3,2},{4,5},{5,4},{6,7},{7,6},{8,9},{9,8},{10,11... | collective-permute-start | bytes 49160 | tf_op jit(solution)/shard_map/ppermute | solution.py:187
  106.8 1.9 %copy-start.9 = (f32[1,32]{1,0:T(1,128)S(1)}, f32[1,32]{1,0:T(1,128)}, u32[]{:S(2)}) copy-start(f32[1,32]{1,0:T(1,128)} %param.30) | copy-start | bytes 388
  109.4 1.2 copy-start.8
  109.4 1.2 copy-start.10
  118.8 3.2 %copy-start.1 = (f32[128,32,128]{2,1,0:T(8,128)S(1)}, f32[128,32,128]{2,1,0:T(8,128)}, u32[]{:S(2)}) copy-start(f32[128,32,128]{2,1,0:T(8,128)} %copy.78) | copy-start | bytes 6291460
  118.8 3.3 %copy-start.7 = (f32[1,32]{1,0:T(1,128)S(1)}, f32[1,32]{1,0:T(1,128)}, u32[]{:S(2)}) copy-start(f32[1,32]{1,0:T(1,128)} %param.33) | copy-start | bytes 388

commit v7 on v6

--- a/solution.py
+++ b/solution.py
@@ -101,11 +101,19 @@
         live = found[:, :, None] & (
             slot[:, :, None] * page_size + offsets[None, None, :] < length[row][:, None, None]
         )
-        keys = pool[0].reshape(pages * page_size, groups, HD)
-        part = (
-            jnp.einsum("rgjd,tgd->rgjt", queries, keys, preferred_element_type=jnp.float32)
-            * factor
-        )
+        keys = pool[0].reshape(pages * page_size, groups * HD)
+        part = jnp.stack(
+            [
+                jnp.einsum(
+                    "rjd,td->rjt",
+                    queries[:, g],
+                    keys[:, g * HD : (g + 1) * HD],
+                    preferred_element_type=jnp.float32,
+                )
+                for g in range(groups)
+            ],
+            axis=1,
+        ) * factor
         scores.append(part)
         masks.append(live.reshape(row_count, 1, 1, pages * page_size))
     tail_scores = jnp.concatenate(scores, axis=-1)
@@ -124,12 +132,19 @@
         jnp.float32
     )
     for which, pool in enumerate(pools):
-        values = pool[1].reshape(span, groups, HD)
-        mixture = mixture + jnp.einsum(
-            "rgjt,tgd->rgjd",
-            tail_weights[..., which * span : (which + 1) * span],
-            values,
-            preferred_element_type=jnp.float32,
+        values = pool[1].reshape(span, groups * HD)
+        weights = tail_weights[..., which * span : (which + 1) * span]
+        mixture = mixture + jnp.stack(
+            [
+                jnp.einsum(
+                    "rjt,td->rjd",
+                    weights[:, g],
+                    values[:, g * HD : (g + 1) * HD],
+                    preferred_element_type=jnp.float32,
+                )
+                for g in range(groups)
+            ],
+            axis=1,
         )
     return mixture.reshape(row_count, -1).astype(jnp.bfloat16)
 
@@ -168,7 +183,10 @@
     down_scale,
 ):
     row_count = branch_query.shape[0]
-    prior = shifted((pool_pages, page_table, tail_length), "wide", 1)
+    prior_pool, prior_meta = shifted(
+        (pool_pages, jnp.concatenate([page_table, tail_length[:, None]], axis=1)), "wide", 1
+    )
+    prior = (prior_pool, prior_meta[:, :-1], prior_meta[:, -1])
     local_parent = parent_row - (lax.axis_index("wide") - 1) * row_count
     attention = attend(
         branch_query,

time: 172 us -> 163 us (0.948)
  local copies, waits for them, and re-layouts: 30.8 us -> 24.1 us
  starting transfers between devices: 27.5 us -> 24.7 us
  matrix products: 14.3 us -> 12.1 us
  Pallas kernels: 88.9 us -> 91.1 us
    another operation x4 -> x0, local copies, waits for them, and re-layouts: 5.99 us -> none  [the longest x2 3.53 us: attend(): keys = pool[0].reshape(pages * page_size, groups, HD)]
    ppermute x3 -> x2, starting transfers between devices: 10.9 us -> 6.85 us  [shifted(): return lax.ppermute(block, axis, route)]
    dot_general x4 -> x16, matrix products: 4.98 us -> 2.79 us  [the longest x8 1.53 us: attend(): jnp.einsum('rjd,td->rjt', queries[:, g], keys[:, g * HD:(g + 1) * HD], pr...]
    pallas_call x2, Pallas kernels: 88.9 us -> 91.1 us  [exchange(): pl.pallas_call(functools.partial(exchange_kernel, route, lanes), out_shap...]
    slice x2 -> x3, local copies, waits for them, and re-layouts: 5.78 us -> 4.61 us  [the longest x1 2.71 us: attend(): values = pool[1].reshape(span, groups * HD)]
  transfers between devices with their start and end apart: 5 -> 4, of which waited for: 1 -> 1; matrix products, arithmetic and copies ran while one was open for 16% -> 11% of each run, Pallas kernels for 0% -> 0%
where the time goes in v7:
time: 163 us; the launch traced here: 162 us
  Pallas kernels  91.1 us (56%)
  starting transfers between devices  24.7 us (15%)
  local copies, waits for them, and re-layouts  24.1 us (15%)
  matrix products  12.1 us (7%)
  other arithmetic  8.77 us (5%)
    pallas_call x2, Pallas kernels, exchange(): pl.pallas_call(functools.partial(exchange_kernel, route, lanes), out_shap...  91.1 us
    all_to_all x1, starting transfers between devices, per_device(): lax.all_to_all(jnp.broadcast_to(own_lists, (peers, own_lists.shape[1])),...  11.5 us
    ppermute x2, starting transfers between devices, shifted(): return lax.ppermute(block, axis, route)  6.85 us
    dot_general x2, local copies, waits for them, and re-layouts, ffn_terms(): jnp.einsum('sf,kfe->ske', hidden, down_blocks[0], preferred_element_type=...  6.36 us
    ppermute x1, starting transfers between devices, per_device(): arrived_half = lax.ppermute(theirs, 'head', [(0, 1), (1, 0)])  6.35 us
    unnamed x2, matrix products  3.52 us
  transfers between devices with their start and end apart: 4, of which 1 were waited for; matrix products, arithmetic and copies ran while one was open for 11% of the time, Pallas kernels for 0%

profile of v7, /device:TPU:1, one launch (start us, length us, event | category | flops | bytes accessed | tf_op | source)
XLA Modules:
  0.0 162.1 jit_solution(878874729245519094)
XLA Ops:
  0.0 0.8 copy.59
  0.8 0.8 pad_add_fusion
  1.6 4.9 %collective-permute-start = (s32[4,17]{1,0:T(4,128)S(1)}, s32[4,17]{1,0:T(4,128)S(1)}, u32[]{:S(2)}, u32[]{:S(2)}) collective-permute-start(s32[4,17]{1,0:T(4,128)S(1)} %pad_add_fusion), channel_id=1, source_target_pairs={{0,2},{2,4},{4,6},{6,8},{8,10},{10,12},{12,14},{14,16},{16,18},{18... | collective-permute-start | bytes 824 | tf_op jit(solution)/shard_map/ppermute | solution.py:80
  6.5 1.9 %collective-permute-start.1 = (bf16[2,64,16,512]{3,2,1,0:T(8,128)(2,1)}, bf16[2,64,16,512]{3,2,1,0:T(8,128)(2,1)}, u32[]{:S(2)}, u32[]{:S(2)}) collective-permute-start(bf16[2,64,16,512]{3,2,1,0:T(8,128)(2,1)} %param.20), channel_id=1, source_target_pairs={{0,2},{2,4},{4,6},{6,8},{8,10},{10,12},{12,14},{14,16},{16,18},{18... | collective-permute-start | bytes 6291464 | tf_op jit(solution)/shard_map/ppermute | solution.py:80
  8.5 0.7 add_bitcast_fusion.1
  9.2 0.7 broadcast_in_dim.99
  9.9 11.5 %all-to-all-start = ((s32[128,1,64]{2,1,0:T(1,128)}), s32[128,1,64]{2,1,0:T(1,128)S(1)}, u32[]{:S(2)}, u32[]{:S(2)}) async-start(s32[128,1,64]{2,1,0:T(1,128)} %broadcast_in_dim.99), calls=%async_computation | async-start | bytes 131072 | tf_op jit(solution)/shard_map/all_to_all | solution.py:217
  21.3 0.7 broadcast_compare_fusion.1
  22.0 1.2 gather_fusion.2
  23.5 2.7 %fusion.32 = (bf16[1,64,16,512]{3,2,1,0:T(8,128)(2,1)}, bf16[1,64,16,512]{3,2,1,0:T(8,128)(2,1)S(1)}) fusion(bf16[2,64,16,512]{3,2,1,0:T(8,128)(2,1)} %param.20), kind=kLoop, calls=%fused_computation.137 | loop fusion | bytes 4194304 | tf_op jit(solution)/shard_map/slice | solution.py:135
  26.3 0.2 convolution_bitcast_fusion
  26.5 0.2 convolution_bitcast_fusion.1
  26.7 0.6 gather_fusion.3
  27.5 0.1 and.80
  27.7 0.1 add.100
  27.9 0.2 convolution_bitcast_fusion.2
  28.1 0.2 convolution_bitcast_fusion.3
  28.4 0.1 fusion.35
  28.5 1.6 %copy.69 = bf16[32,128,128]{1,2,0:T(8,128)(2,1)S(1)} copy(bf16[32,128,128]{2,1,0:T(8,128)(2,1)} %bitcast.241) | data formatting | bytes 2097152 | tf_op jit(solution)/shard_map/squeeze | solution.py:161
  30.2 0.6 gather_fusion
  30.9 0.1 and.74
  31.0 0.1 and.75
  31.4 0.1 add.97
  31.5 0.2 slice_reduce_fusion
  31.7 0.6 gather_fusion.1
  32.4 1.7 %fusion.33 = (bf16[1,64,16,512]{3,2,1,0:T(8,128)(2,1)S(1)}, bf16[1,64,16,512]{3,2,1,0:T(8,128)(2,1)S(1)}) fusion(bf16[2,64,16,512]{3,2,1,0:T(8,128)(2,1)} %collective-permute-done.1), kind=kLoop, calls=%fused_computation.138 | loop fusion | bytes 4194304 | tf_op jit(solution)/shard_map/slice | solution.py:104
  34.1 0.2 convolution_bitcast_fusion.4
  34.3 0.2 convolution_bitcast_fusion.5
  34.5 0.2 convolution_bitcast_fusion.6
  34.7 0.2 convolution_bitcast_fusion.7
  35.0 0.2 select_reduce_fusion
  35.2 0.4 fusion.11
  35.6 0.3 divide_convert_fusion
  35.9 0.3 copy-done.3
  36.2 0.2 convolution_bitcast_fusion.12
  36.4 0.2 convolution_bitcast_fusion.11
  36.5 0.2 convolution_bitcast_fusion.10
  36.7 0.2 convolution_bitcast_fusion.9
  36.9 0.2 convolution_bitcast_fusion.16
  37.0 0.2 convolution_bitcast_fusion.15
  37.2 0.2 convolution_bitcast_fusion.14
  37.4 0.2 convolution_bitcast_fusion.13
  37.7 6.4 %collective-permute-start.2 = (bf16[2,4096]{1,0:T(2,128)(2,1)S(1)}, bf16[2,4096]{1,0:T(2,128)(2,1)S(1)}, u32[]{:S(2)}, u32[]{:S(2)}) collective-permute-start(bf16[2,4096]{1,0:T(2,128)(2,1)S(1)} %get-tuple-element.18), channel_id=1, source_target_pairs={{0,1},{1,0},{2,3},{3,2},{4,5},{5,4},{6,7},{7,6},{8,9},{9,8},{10,11... | collective-permute-start | bytes 49160 | tf_op jit(solution)/shard_map/ppermute | solution.py:205
  44.3 0.9 collective-permute-done.2
  45.2 0.2 multiply_reduce_fusion.4
  45.4 0.1 multiply_convert_fusion.4
  45.5 2.0 %convolution_convert_fusion = bf16[4096,256]{1,0:T(8,128)(2,1)} fusion(s32[4096]{0:T(1024)S(1)} %eq.80, bf16[8,8,2,128]{3,2,1,0:T(2,128)(2,1)S(1)} %bitcast.253), kind=kOutput, calls=%fused_computation.4 | convolution fusion | flops 135528448 | bytes 2146304 | tf_op jit(solution)/shard_map/dot_general | solution.py:231
  47.5 50.0 %shard_map.163 = bf16[128,32,256]{2,1,0:T(8,128)(2,1)} custom-call(bf16[128,32,256]{2,1,0:T(8,128)(2,1)} %bitcast.221), custom_call_target="tpu_custom_call" | custom-call | tf_op jit(solution)/shard_map/pallas_call | solution.py:67
  97.6 1.9 %fusion.31 = (bf16[128,32,128]{2,1,0:T(8,128)(2,1)S(1)}, bf16[128,32,128]{2,1,0:T(8,128)(2,1)S(1)}) fusion(bf16[128,32,256]{2,1,0:T(8,128)(2,1)} %shard_map.163), kind=kLoop, calls=%fused_computation.136 | loop fusion | bytes 4194304 | tf_op jit(solution)/shard_map/slice | solution.py:237
  99.5 0.7 multiply_reduce_fusion
  100.2 0.7 multiply_reduce_fusion.2
  100.9 0.5 copy-done.10
  101.4 0.7 multiply_reduce_fusion.1
  102.2 0.7 multiply_reduce_fusion.3
  102.9 1.7 %fusion.17 = f32[128,4096]{0,1} fusion(bf16[128,4096]{0,1:T(8,128)(2,1)S(1)} %bitcast.218, f32[128,128]{1,0:T(8,128)S(1)} %multiply_reduce_fusion, f32[128,128]{1,0:T(8,128)S(1)} %multiply_reduce_fusion.1), kind=kOutput, calls=%fused_computation.85 | convolution fusion | flops 134316032 | bytes 3276800
  104.6 3.1 %copy.74 = f32[128,32,128]{2,1,0:T(8,128)} copy(f32[128,32,128]{0,2,1:T(8,128)} %bitcast.222) | data formatting | bytes 4194304 | tf_op jit(solution)/shard_map/sf,kfe->ske/dot_general | solution.py:161
  107.7 1.8 %fusion.16 = f32[128,4096]{0,1} fusion(bf16[128,4096]{0,1:T(8,128)(2,1)S(1)} %bitcast.219, f32[128,128]{1,0:T(8,128)S(1)} %multiply_reduce_fusion.2, f32[128,128]{1,0:T(8,128)S(1)} %multiply_reduce_fusion.3), kind=kOutput, calls=%fused_computation.84 | convolution fusion | flops 134316032 | bytes 3276800
  109.5 3.2 %copy.70 = f32[128,32,128]{2,1,0:T(8,128)} copy(f32[128,32,128]{0,2,1:T(8,128)} %bitcast.220) | data formatting | bytes 4194304 | tf_op jit(solution)/shard_map/sf,kfe->ske/dot_general | solution.py:161
  112.8 2.2 %multiply_convert_fusion.1 = (bf16[128,32,128]{2,1,0:T(8,128)(2,1)S(1)}, bf16[128,32,128]{2,1,0:T(8,128)(2,1)S(1)}) fusion(f32[128,32,128]{2,1,0:T(8,128)} %copy.70, f32[32]{0:T(128)S(1)} %bitcast.256, f32[128,32,128]{2,1,0:T(8,128)S(1)} %copy-done.2), kind=kLoop, calls=%fused_computation.9 | loop fusion | flops 2097152 | bytes 6291584 | tf_op jit(solution)/shard_map/convert_element_type | solution.py:163
  114.9 1.7 %pad_maximum_fusion.x_ref = bf16[128,32,256]{2,1,0:T(8,128)(2,1)} fusion(bf16[128,32,128]{2,1,0:T(8,128)(2,1)S(1)} %get-tuple-element.25, bf16[128,32,128]{2,1,0:T(8,128)(2,1)S(1)} %get-tuple-element.24), kind=kLoop, calls=%fused_computation.5 | loop fusion | flops 4194304 | bytes 4194304 | tf_op jit(solution)/shard_map/concatenate | solution.py:247
  116.6 41.1 %shard_map.164 = bf16[128,32,256]{2,1,0:T(8,128)(2,1)} custom-call(bf16[128,32,256]{2,1,0:T(8,128)(2,1)} %pad_maximum_fusion.x_ref), custom_call_target="tpu_custom_call" | custom-call | tf_op jit(solution)/shard_map/pallas_call | solution.py:67
  157.7 2.9 %copy.75 = bf16[256,4096]{1,0:T(8,128)(2,1)S(1)} copy(bf16[256,4096]{0,1:T(8,128)(2,1)} %bitcast.224) | data formatting | bytes 4194304 | tf_op jit(solution)/shard_map/dot_general | solution.py:249
  160.7 0.8 convolution_bitcast_fusion.8
  161.4 0.7 fusion.13
  (59 shorter events, 1.7 us)
Async XLA Ops:
  0.0 99.5 %copy-start = (bf16[1,32,128,128]{3,2,1,0:T(8,128)(2,1)S(1)}, bf16[1,32,128,128]{3,2,1,0:T(8,128)(2,1)}, u32[]{:S(2)}) copy-start(bf16[1,32,128,128]{3,2,1,0:T(8,128)(2,1)} %param.27) | copy-start | bytes 3145732
  1.6 28.6 %collective-permute-start = (s32[4,17]{1,0:T(4,128)S(1)}, s32[4,17]{1,0:T(4,128)S(1)}, u32[]{:S(2)}, u32[]{:S(2)}) collective-permute-start(s32[4,17]{1,0:T(4,128)S(1)} %pad_add_fusion), channel_id=1, source_target_pairs={{0,2},{2,4},{4,6},{6,8},{8,10},{10,12},{12,14},{14,16},{16,18},{18... | collective-permute-start | bytes 824 | tf_op jit(solution)/shard_map/ppermute | solution.py:80
  6.5 25.9 %collective-permute-start.1 = (bf16[2,64,16,512]{3,2,1,0:T(8,128)(2,1)}, bf16[2,64,16,512]{3,2,1,0:T(8,128)(2,1)}, u32[]{:S(2)}, u32[]{:S(2)}) collective-permute-start(bf16[2,64,16,512]{3,2,1,0:T(8,128)(2,1)} %param.20), channel_id=1, source_target_pairs={{0,2},{2,4},{4,6},{6,8},{8,10},{10,12},{12,14},{14,16},{16,18},{18... | collective-permute-start | bytes 6291464 | tf_op jit(solution)/shard_map/ppermute | solution.py:80
  9.9 34.2 %all-to-all-start = ((s32[128,1,64]{2,1,0:T(1,128)}), s32[128,1,64]{2,1,0:T(1,128)S(1)}, u32[]{:S(2)}, u32[]{:S(2)}) async-start(s32[128,1,64]{2,1,0:T(1,128)} %broadcast_in_dim.99), calls=%async_computation | async-start | bytes 131072 | tf_op jit(solution)/shard_map/all_to_all | solution.py:217
  23.5 2.8 %copy-start.5 = (bf16[4,4096]{1,0:T(4,128)(2,1)S(1)}, bf16[4,4096]{1,0:T(4,128)(2,1)}, u32[]{:S(2)}) copy-start(bf16[4,4096]{1,0:T(4,128)(2,1)} %param.17) | copy-start | bytes 98308
  23.5 3.2 %copy-start.1 = (s32[4]{0:T(128)S(1)}, s32[4]{0:T(128)}, u32[]{:S(2)}) copy-start(s32[4]{0:T(128)} %param.22) | copy-start | bytes 52
  23.5 4.4 %copy-start.7 = (bf16[4,512]{1,0:T(4,128)(2,1)S(1)}, bf16[4,512]{1,0:T(4,128)(2,1)}, u32[]{:S(2)}) copy-start(bf16[4,512]{1,0:T(4,128)(2,1)} %param.18) | copy-start | bytes 12292
  26.2 2.2 %copy-start.8 = (bf16[4,512]{1,0:T(4,128)(2,1)S(1)}, bf16[4,512]{1,0:T(4,128)(2,1)}, u32[]{:S(2)}) copy-start(bf16[4,512]{1,0:T(4,128)(2,1)} %param.19) | copy-start | bytes 12292
  35.0 1.2 copy-start.3
  35.9 9.3 %copy-start.4 = (bf16[2,8192]{1,0:T(2,128)(2,1)S(1)}, bf16[2,8192]{1,0:T(2,128)(2,1)}, u32[]{:S(2)}) copy-start(bf16[2,8192]{1,0:T(2,128)(2,1)} %param.24) | copy-start | bytes 98308
  35.9 9.5 %copy-start.6 = (f32[8192]{0:T(1024)S(1)}, f32[8192]{0:T(1024)}, u32[]{:S(2)}) copy-start(f32[8192]{0:T(1024)} %param.25) | copy-start | bytes 98308
  37.7 7.5 %collective-permute-start.2 = (bf16[2,4096]{1,0:T(2,128)(2,1)S(1)}, bf16[2,4096]{1,0:T(2,128)(2,1)S(1)}, u32[]{:S(2)}, u32[]{:S(2)}) collective-permute-start(bf16[2,4096]{1,0:T(2,128)(2,1)S(1)} %get-tuple-element.18), channel_id=1, source_target_pairs={{0,1},{1,0},{2,3},{3,2},{4,5},{5,4},{6,7},{7,6},{8,9},{9,8},{10,11... | collective-permute-start | bytes 49160 | tf_op jit(solution)/shard_map/ppermute | solution.py:205
  97.5 1.9 %copy-start.11 = (f32[1,32]{1,0:T(1,128)S(1)}, f32[1,32]{1,0:T(1,128)}, u32[]{:S(2)}) copy-start(f32[1,32]{1,0:T(1,128)} %param.30) | copy-start | bytes 388
  100.2 1.2 copy-start.10
  100.2 1.2 copy-start.12
  109.5 3.2 %copy-start.2 = (f32[128,32,128]{2,1,0:T(8,128)S(1)}, f32[128,32,128]{2,1,0:T(8,128)}, u32[]{:S(2)}) copy-start(f32[128,32,128]{2,1,0:T(8,128)} %copy.74) | copy-start | bytes 6291460
  109.5 3.3 %copy-start.9 = (f32[1,32]{1,0:T(1,128)S(1)}, f32[1,32]{1,0:T(1,128)}, u32[]{:S(2)}) copy-start(f32[1,32]{1,0:T(1,128)} %param.33) | copy-start | bytes 388

commit v8 on v7

--- a/solution.py
+++ b/solution.py
@@ -149,18 +149,14 @@
     return mixture.reshape(row_count, -1).astype(jnp.bfloat16)
 
 
-def ffn_terms(picked, gate_blocks, up_blocks, gate_scale, up_scale, down_blocks, down_scale):
+def hidden_units(picked, gate_blocks, up_blocks, gate_scale, up_scale):
     gate_part = jnp.einsum(
         "skd,kdf->ksf", picked, gate_blocks[0], preferred_element_type=jnp.float32
     )
     up_part = jnp.einsum("skd,kdf->ksf", picked, up_blocks[0], preferred_element_type=jnp.float32)
     gate_sum = jnp.sum(gate_part * gate_scale[0][:, None, None], axis=0)
     up_sum = jnp.sum(up_part * up_scale[0][:, None, None], axis=0)
-    hidden = (jax.nn.silu(gate_sum) * up_sum).astype(jnp.bfloat16)
-    return (
-        jnp.einsum("sf,kfe->ske", hidden, down_blocks[0], preferred_element_type=jnp.float32)
-        * down_scale[0][None, :, None]
-    ).astype(jnp.bfloat16)
+    return (jax.nn.silu(gate_sum) * up_sum).astype(jnp.bfloat16)
 
 
 def per_device(
@@ -232,24 +228,35 @@
         choose, by_block.reshape(feature_blocks, rows * BLK), preferred_element_type=jnp.float32
     ).astype(jnp.bfloat16)
     picked = exchange(outgoing.reshape(peers, keep, rows * BLK), gather_route, Z_LANES)
-    terms = [
-        ffn_terms(
-            picked[:, :, r * BLK : (r + 1) * BLK],
-            gate_blocks,
-            up_blocks,
-            gate_scale,
-            up_scale,
-            down_blocks,
-            down_scale,
-        )
-        for r in range(rows)
-    ]
-    arrived = exchange(jnp.concatenate(terms, axis=2), return_route, Z_LANES)
+    hidden = jnp.concatenate(
+        [
+            hidden_units(
+                picked[:, :, r * BLK : (r + 1) * BLK], gate_blocks, up_blocks, gate_scale, up_scale
+            )
+            for r in range(rows)
+        ],
+        axis=0,
+    )
+    down_flat = jnp.swapaxes(down_blocks[0], 0, 1).reshape(BLK, keep * BLK)
+    down_part = jnp.dot(hidden, down_flat, preferred_element_type=jnp.float32)
+    column_scale = jnp.repeat(down_scale[0], BLK)
+    contrib = lax.optimization_barrier((down_part * column_scale[None, :]).astype(jnp.bfloat16))
+    contrib = contrib.reshape(rows, peers, keep, BLK)
+    outgoing_sums = jnp.concatenate([contrib[r] for r in range(rows)], axis=-1)
+    arrived = exchange(outgoing_sums, return_route, Z_LANES)
     placement = (blocks[:, None] == out_keep.reshape(1, peers * keep)).astype(jnp.bfloat16)
-    summed = jnp.dot(
-        placement, arrived.reshape(peers * keep, rows * BLK), preferred_element_type=jnp.float32
-    )
-    ffn_share = jnp.swapaxes(summed.reshape(feature_blocks, rows, BLK), 0, 1).reshape(rows, -1)
+    summed = jnp.stack(
+        [
+            jnp.dot(
+                placement,
+                arrived[:, :, r * BLK : (r + 1) * BLK].reshape(peers * keep, BLK),
+                preferred_element_type=jnp.float32,
+            )
+            for r in range(rows)
+        ],
+        axis=0,
+    )
+    ffn_share = summed.reshape(rows, -1)
     return (middle + ffn_share).astype(jnp.bfloat16)
 
 

time: 163 us -> 151 us (0.926)
  local copies, waits for them, and re-layouts: 24.1 us -> 17.5 us
  matrix products: 12.1 us -> 9.12 us
  other arithmetic: 8.77 us -> 6.69 us
    dot_general x3 -> x0, local copies, waits for them, and re-layouts: 9.28 us -> none  [the longest x2 6.36 us: ffn_terms(): jnp.einsum('sf,kfe->ske', hidden, down_blocks[0], preferred_element_type=...]
    unnamed x2 -> x0, matrix products: 3.52 us -> none
    unnamed x28 -> x30, local copies, waits for them, and re-layouts: 0.88 us -> 3.16 us
    convert_element_type x1, other arithmetic: 2.15 us -> 0.05 us  [hidden_units(): return (jax.nn.silu(gate_sum) * up_sum).astype(jnp.bfloat16)]
    slice x0 -> x1, local copies, waits for them, and re-layouts: none -> 1.9 us  [per_device(): arrived[:, :, r * BLK:(r + 1) * BLK].reshape(peers * keep, BLK)]
    dot_general x5 -> x7, matrix products: 3.61 us -> 4.15 us  [the longest x2 1.45 us: hidden_units(): jnp.einsum('skd,kdf->ksf', picked, gate_blocks[0], preferred_element_type...]
  transfers between devices with their start and end apart: 4 -> 4, of which waited for: 1 -> 1; matrix products, arithmetic and copies ran while one was open for 11% -> 12% of each run, Pallas kernels for 0% -> 0%
where the time goes in v8:
time: 151 us; the launch traced here: 150 us
  Pallas kernels  91 us (60%)
  starting transfers between devices  24.7 us (16%)
  local copies, waits for them, and re-layouts  17.5 us (12%)
  matrix products  9.12 us (6%)
  other arithmetic  6.69 us (4%)
    pallas_call x2, Pallas kernels, exchange(): pl.pallas_call(functools.partial(exchange_kernel, route, lanes), out_shap...  91 us
    all_to_all x1, starting transfers between devices, per_device(): lax.all_to_all(jnp.broadcast_to(own_lists, (peers, own_lists.shape[1])),...  11.5 us
    ppermute x2, starting transfers between devices, shifted(): return lax.ppermute(block, axis, route)  6.85 us
    ppermute x1, starting transfers between devices, per_device(): arrived_half = lax.ppermute(theirs, 'head', [(0, 1), (1, 0)])  6.35 us
    unnamed x30, local copies, waits for them, and re-layouts  3.16 us
  transfers between devices with their start and end apart: 4, of which 1 were waited for; matrix products, arithmetic and copies ran while one was open for 12% of the time, Pallas kernels for 0%

profile of v8, /device:TPU:1, one launch (start us, length us, event | category | flops | bytes accessed | tf_op | source)
XLA Modules:
  0.0 150.4 jit_solution(16015781245679140636)
XLA Ops:
  0.0 0.8 copy.46
  0.8 0.8 pad_add_fusion
  1.6 4.9 %collective-permute-start = (s32[4,17]{1,0:T(4,128)S(1)}, s32[4,17]{1,0:T(4,128)S(1)}, u32[]{:S(2)}, u32[]{:S(2)}) collective-permute-start(s32[4,17]{1,0:T(4,128)S(1)} %pad_add_fusion), channel_id=1, source_target_pairs={{0,2},{2,4},{4,6},{6,8},{8,10},{10,12},{12,14},{14,16},{16,18},{18... | collective-permute-start | bytes 824 | tf_op jit(solution)/shard_map/ppermute | solution.py:80
  6.5 1.9 %collective-permute-start.1 = (bf16[2,64,16,512]{3,2,1,0:T(8,128)(2,1)}, bf16[2,64,16,512]{3,2,1,0:T(8,128)(2,1)}, u32[]{:S(2)}, u32[]{:S(2)}) collective-permute-start(bf16[2,64,16,512]{3,2,1,0:T(8,128)(2,1)} %param.20), channel_id=1, source_target_pairs={{0,2},{2,4},{4,6},{6,8},{8,10},{10,12},{12,14},{14,16},{16,18},{18... | collective-permute-start | bytes 6291464 | tf_op jit(solution)/shard_map/ppermute | solution.py:80
  8.5 0.7 add_bitcast_fusion.1
  9.2 0.7 broadcast_in_dim.102
  9.9 11.5 %all-to-all-start = ((s32[128,1,64]{2,1,0:T(1,128)}), s32[128,1,64]{2,1,0:T(1,128)S(1)}, u32[]{:S(2)}, u32[]{:S(2)}) async-start(s32[128,1,64]{2,1,0:T(1,128)} %broadcast_in_dim.102), calls=%async_computation | async-start | bytes 131072 | tf_op jit(solution)/shard_map/all_to_all | solution.py:213
  21.3 0.7 broadcast_compare_fusion.1
  22.0 1.2 gather_fusion.2
  23.5 2.7 %fusion.33 = (bf16[1,64,16,512]{3,2,1,0:T(8,128)(2,1)}, bf16[1,64,16,512]{3,2,1,0:T(8,128)(2,1)S(1)}) fusion(bf16[2,64,16,512]{3,2,1,0:T(8,128)(2,1)} %param.20), kind=kLoop, calls=%fused_computation.140 | loop fusion | bytes 4194304 | tf_op jit(solution)/shard_map/slice | solution.py:135
  26.2 0.2 convolution_bitcast_fusion
  26.4 0.2 convolution_bitcast_fusion.1
  26.6 0.2 convolution_bitcast_fusion.2
  26.9 0.2 convolution_bitcast_fusion.3
  27.1 0.6 gather_fusion.3
  27.9 0.1 and.80
  28.1 0.1 add.100
  28.4 0.1 fusion.36
  28.6 1.6 %copy.58 = bf16[1,32,128,128]{2,3,1,0:T(8,128)(2,1)S(1)} copy(bf16[1,32,128,128]{3,2,1,0:T(8,128)(2,1)} %param.31) | data formatting | bytes 2097152 | tf_op args[14]
  30.3 0.6 gather_fusion
  31.0 0.1 and.74
  31.1 0.1 and.75
  31.4 0.1 add.97
  31.6 0.2 slice_reduce_fusion
  31.7 0.6 gather_fusion.1
  32.5 1.7 %fusion.34 = (bf16[1,64,16,512]{3,2,1,0:T(8,128)(2,1)S(1)}, bf16[1,64,16,512]{3,2,1,0:T(8,128)(2,1)S(1)}) fusion(bf16[2,64,16,512]{3,2,1,0:T(8,128)(2,1)} %collective-permute-done.1), kind=kLoop, calls=%fused_computation.141 | loop fusion | bytes 4194304 | tf_op jit(solution)/shard_map/slice | solution.py:104
  34.2 0.2 convolution_bitcast_fusion.4
  34.4 0.2 convolution_bitcast_fusion.5
  34.6 0.2 convolution_bitcast_fusion.6
  34.8 0.2 convolution_bitcast_fusion.7
  35.1 0.2 select_reduce_fusion
  35.3 0.4 fusion.12
  35.7 0.3 divide_convert_fusion
  36.0 0.3 copy-done.2
  36.3 0.2 convolution_bitcast_fusion.11
  36.5 0.2 convolution_bitcast_fusion.10
  36.6 0.2 convolution_bitcast_fusion.9
  36.8 0.2 convolution_bitcast_fusion.8
  37.0 0.2 convolution_bitcast_fusion.15
  37.1 0.2 convolution_bitcast_fusion.14
  37.3 0.2 convolution_bitcast_fusion.13
  37.5 0.2 convolution_bitcast_fusion.12
  37.8 6.4 %collective-permute-start.2 = (bf16[2,4096]{1,0:T(2,128)(2,1)S(1)}, bf16[2,4096]{1,0:T(2,128)(2,1)S(1)}, u32[]{:S(2)}, u32[]{:S(2)}) collective-permute-start(bf16[2,4096]{1,0:T(2,128)(2,1)S(1)} %get-tuple-element.22), channel_id=1, source_target_pairs={{0,1},{1,0},{2,3},{3,2},{4,5},{5,4},{6,7},{7,6},{8,9},{9,8},{10,11... | collective-permute-start | bytes 49160 | tf_op jit(solution)/shard_map/ppermute | solution.py:201
  44.4 0.9 collective-permute-done.2
  45.3 0.2 multiply_reduce_fusion.4
  45.5 0.1 multiply_convert_fusion.2
  45.6 2.0 %convolution_convert_fusion = bf16[4096,256]{1,0:T(8,128)(2,1)} fusion(s32[4096]{0:T(1024)S(1)} %eq.80, bf16[8,8,2,128]{3,2,1,0:T(2,128)(2,1)S(1)} %bitcast.246), kind=kOutput, calls=%fused_computation.6 | convolution fusion | flops 135528448 | bytes 2146304 | tf_op jit(solution)/shard_map/dot_general | solution.py:227
  47.6 49.9 %shard_map.163 = bf16[128,32,256]{2,1,0:T(8,128)(2,1)} custom-call(bf16[128,32,256]{2,1,0:T(8,128)(2,1)} %bitcast.213), custom_call_target="tpu_custom_call" | custom-call | tf_op jit(solution)/shard_map/pallas_call | solution.py:67
  97.6 1.9 %fusion.32 = (bf16[128,32,128]{2,1,0:T(8,128)(2,1)S(1)}, bf16[128,32,128]{2,1,0:T(8,128)(2,1)S(1)}) fusion(bf16[128,32,256]{2,1,0:T(8,128)(2,1)} %shard_map.163), kind=kLoop, calls=%fused_computation.139 | loop fusion | bytes 4194304 | tf_op jit(solution)/shard_map/slice | solution.py:234
  99.5 0.7 multiply_reduce_fusion
  100.2 0.7 multiply_reduce_fusion.2
  100.9 0.5 copy-done.9
  101.4 0.7 multiply_reduce_fusion.1
  102.2 0.7 multiply_reduce_fusion.3
  102.9 0.7 fusion
  103.7 0.2 slice_bitcast_fusion.1
  103.9 0.2 copy.68
  104.1 0.2 copy.69
  104.4 1.7 %pad_maximum_fusion.x_ref = bf16[128,32,256]{2,1,0:T(8,128)(2,1)} fusion(bf16[128,32,128]{2,1,0:T(8,128)(2,1)S(1)} %bitcast.234, bf16[128,32,128]{2,1,0:T(8,128)(2,1)S(1)} %bitcast.232), kind=kLoop, calls=%fused_computation.7 | loop fusion | flops 4194304 | bytes 4194304 | tf_op jit(solution)/shard_map/concatenate | solution.py:245
  106.0 41.1 %shard_map.164 = bf16[128,32,256]{2,1,0:T(8,128)(2,1)} custom-call(bf16[128,32,256]{2,1,0:T(8,128)(2,1)} %pad_maximum_fusion.x_ref), custom_call_target="tpu_custom_call" | custom-call | tf_op jit(solution)/shard_map/pallas_call | solution.py:67
  147.2 1.9 %fusion.31 = (bf16[128,32,128]{2,1,0:T(8,128)(2,1)S(1)}, bf16[128,32,128]{2,1,0:T(8,128)(2,1)S(1)}) fusion(bf16[128,32,256]{2,1,0:T(8,128)(2,1)} %shard_map.164), kind=kLoop, calls=%fused_computation.138 | loop fusion | bytes 4194304 | tf_op jit(solution)/shard_map/slice | solution.py:252
  149.1 0.3 fusion.7
  149.4 0.3 fusion.6
  149.7 0.7 fusion.20
  (59 shorter events, 1.8 us)
Async XLA Ops:
  0.0 99.5 %copy-start = (bf16[1,32,128,128]{3,2,1,0:T(8,128)(2,1)S(1)}, bf16[1,32,128,128]{3,2,1,0:T(8,128)(2,1)}, u32[]{:S(2)}) copy-start(bf16[1,32,128,128]{3,2,1,0:T(8,128)(2,1)} %param.27) | copy-start | bytes 3145732
  1.6 28.7 %collective-permute-start = (s32[4,17]{1,0:T(4,128)S(1)}, s32[4,17]{1,0:T(4,128)S(1)}, u32[]{:S(2)}, u32[]{:S(2)}) collective-permute-start(s32[4,17]{1,0:T(4,128)S(1)} %pad_add_fusion), channel_id=1, source_target_pairs={{0,2},{2,4},{4,6},{6,8},{8,10},{10,12},{12,14},{14,16},{16,18},{18... | collective-permute-start | bytes 824 | tf_op jit(solution)/shard_map/ppermute | solution.py:80
  6.5 26.0 %collective-permute-start.1 = (bf16[2,64,16,512]{3,2,1,0:T(8,128)(2,1)}, bf16[2,64,16,512]{3,2,1,0:T(8,128)(2,1)}, u32[]{:S(2)}, u32[]{:S(2)}) collective-permute-start(bf16[2,64,16,512]{3,2,1,0:T(8,128)(2,1)} %param.20), channel_id=1, source_target_pairs={{0,2},{2,4},{4,6},{6,8},{8,10},{10,12},{12,14},{14,16},{16,18},{18... | collective-permute-start | bytes 6291464 | tf_op jit(solution)/shard_map/ppermute | solution.py:80
  9.9 34.3 %all-to-all-start = ((s32[128,1,64]{2,1,0:T(1,128)}), s32[128,1,64]{2,1,0:T(1,128)S(1)}, u32[]{:S(2)}, u32[]{:S(2)}) async-start(s32[128,1,64]{2,1,0:T(1,128)} %broadcast_in_dim.102), calls=%async_computation | async-start | bytes 131072 | tf_op jit(solution)/shard_map/all_to_all | solution.py:213
  23.5 2.7 %copy-start.4 = (bf16[4,4096]{1,0:T(4,128)(2,1)S(1)}, bf16[4,4096]{1,0:T(4,128)(2,1)}, u32[]{:S(2)}) copy-start(bf16[4,4096]{1,0:T(4,128)(2,1)} %param.17) | copy-start | bytes 98308
  23.5 3.6 %copy-start.1 = (s32[4]{0:T(128)S(1)}, s32[4]{0:T(128)}, u32[]{:S(2)}) copy-start(s32[4]{0:T(128)} %param.22) | copy-start | bytes 52
  26.2 2.0 %copy-start.6 = (bf16[4,512]{1,0:T(4,128)(2,1)S(1)}, bf16[4,512]{1,0:T(4,128)(2,1)}, u32[]{:S(2)}) copy-start(bf16[4,512]{1,0:T(4,128)(2,1)} %param.18) | copy-start | bytes 12292
  26.2 2.1 %copy-start.7 = (bf16[4,512]{1,0:T(4,128)(2,1)S(1)}, bf16[4,512]{1,0:T(4,128)(2,1)}, u32[]{:S(2)}) copy-start(bf16[4,512]{1,0:T(4,128)(2,1)} %param.19) | copy-start | bytes 12292
  26.2 2.1 %copy-start.8 = (f32[1,32]{1,0:T(1,128)S(1)}, f32[1,32]{1,0:T(1,128)}, u32[]{:S(2)}) copy-start(f32[1,32]{1,0:T(1,128)} %param.33) | copy-start | bytes 388
  35.1 1.2 copy-start.2
  36.0 9.3 %copy-start.3 = (bf16[2,8192]{1,0:T(2,128)(2,1)S(1)}, bf16[2,8192]{1,0:T(2,128)(2,1)}, u32[]{:S(2)}) copy-start(bf16[2,8192]{1,0:T(2,128)(2,1)} %param.24) | copy-start | bytes 98308
  36.0 9.5 %copy-start.5 = (f32[8192]{0:T(1024)S(1)}, f32[8192]{0:T(1024)}, u32[]{:S(2)}) copy-start(f32[8192]{0:T(1024)} %param.25) | copy-start | bytes 98308
  37.8 7.5 %collective-permute-start.2 = (bf16[2,4096]{1,0:T(2,128)(2,1)S(1)}, bf16[2,4096]{1,0:T(2,128)(2,1)S(1)}, u32[]{:S(2)}, u32[]{:S(2)}) collective-permute-start(bf16[2,4096]{1,0:T(2,128)(2,1)S(1)} %get-tuple-element.22), channel_id=1, source_target_pairs={{0,1},{1,0},{2,3},{3,2},{4,5},{5,4},{6,7},{7,6},{8,9},{9,8},{10,11... | collective-permute-start | bytes 49160 | tf_op jit(solution)/shard_map/ppermute | solution.py:201
  97.6 1.9 %copy-start.10 = (f32[1,32]{1,0:T(1,128)S(1)}, f32[1,32]{1,0:T(1,128)}, u32[]{:S(2)}) copy-start(f32[1,32]{1,0:T(1,128)} %param.30) | copy-start | bytes 388
  100.2 1.2 copy-start.9
  100.2 1.2 copy-start.11

commit v9 on v8

--- a/solution.py
+++ b/solution.py
@@ -72,6 +72,63 @@
         scratch_shapes=[pltpu.SemaphoreType.DMA, pltpu.SemaphoreType.DMA, pltpu.SemaphoreType.DMA],
         compiler_params=pltpu.CompilerParams(has_side_effects=True),
     )(x)
+
+
+def swap_kernel(lanes, half_ref, lists_ref, half_out, lists_out, sems):
+    me = lax.axis_index("wide")
+    here = lax.axis_index("head")
+    n = lists_ref.shape[0]
+    partner = pltpu.make_async_remote_copy(
+        src_ref=half_ref,
+        dst_ref=half_out,
+        send_sem=sems.at[0],
+        recv_sem=sems.at[1],
+        device_id=(me, 1 - here),
+        device_id_type=pl.DeviceIdType.MESH,
+    )
+    partner.start()
+    local = pltpu.make_async_copy(lists_ref.at[me], lists_out.at[me], sems.at[4])
+    local.start()
+
+    def send(j, carry):
+        peer = lax.rem(me + j, n)
+        pltpu.make_async_remote_copy(
+            src_ref=lists_ref.at[peer],
+            dst_ref=lists_out.at[me],
+            send_sem=sems.at[2],
+            recv_sem=sems.at[3],
+            device_id=(peer, return_route(me, here, peer, lanes)),
+            device_id_type=pl.DeviceIdType.MESH,
+        ).start()
+        return carry
+
+    lax.fori_loop(1, n, send, 0)
+    every = pltpu.make_async_remote_copy(
+        src_ref=lists_ref.at[pl.ds(0, n - 1)],
+        dst_ref=lists_out.at[pl.ds(0, n - 1)],
+        send_sem=sems.at[2],
+        recv_sem=sems.at[3],
+        device_id=(me, here),
+        device_id_type=pl.DeviceIdType.MESH,
+    )
+    every.wait_send()
+    every.wait_recv()
+    partner.wait()
+    local.wait()
+
+
+def swap(half, lists, lanes):
+    return pl.pallas_call(
+        functools.partial(swap_kernel, lanes),
+        out_shape=(
+            jax.ShapeDtypeStruct(half.shape, half.dtype),
+            jax.ShapeDtypeStruct(lists.shape, lists.dtype),
+        ),
+        in_specs=[pl.BlockSpec(memory_space=pl.ANY)] * 2,
+        out_specs=(pl.BlockSpec(memory_space=pl.ANY),) * 2,
+        scratch_shapes=[pltpu.SemaphoreType.DMA((5,))],
+        compiler_params=pltpu.CompilerParams(has_side_effects=True),
+    )(half, lists)
 
 
 def shifted(block, axis, distance):
@@ -198,7 +255,14 @@
     here = lax.axis_index("head")
     mine = lax.dynamic_slice_in_dim(attention, here * half, half, axis=0)
     theirs = lax.dynamic_slice_in_dim(attention, (1 - here) * half, half, axis=0)
-    arrived_half = lax.ppermute(theirs, "head", [(0, 1), (1, 0)])
+    peers = lax.axis_size("wide")
+    own_lists = jnp.concatenate([gate_up_keep, down_keep], axis=1)
+    list_width = own_lists.shape[1]
+    padded = jnp.pad(own_lists, ((0, 7), (0, BLK - list_width)))
+    arrived_half, keep_lists = swap(
+        theirs, jnp.broadcast_to(padded, (peers,) + padded.shape), Z_LANES
+    )
+    keep_lists = keep_lists[:, 0, :list_width]
     head_rows = jnp.where(
         here == 0,
         jnp.concatenate([mine, arrived_half], axis=1),
@@ -208,15 +272,6 @@
     normed = (
         middle * lax.rsqrt(jnp.mean(middle * middle, axis=-1, keepdims=True) + 1e-05) * norm_gain
     ).astype(jnp.bfloat16)
-    peers = lax.axis_size("wide")
-    own_lists = jnp.concatenate([gate_up_keep, down_keep], axis=1)
-    keep_lists = lax.all_to_all(
-        jnp.broadcast_to(own_lists, (peers, own_lists.shape[1])),
-        "wide",
-        split_axis=0,
-        concat_axis=0,
-        tiled=True,
-    )
     keep = gate_up_keep.shape[1]
     in_keep, out_keep = keep_lists[:, :keep], keep_lists[:, keep:]
     feature_blocks = normed.shape[1] // BLK

time: 151 us -> 169 us (1.12)
  Pallas kernels: 91 us -> 114 us
  starting transfers between devices: 24.7 us -> 6.85 us
  waiting for transfers between devices: 0.89 us -> 11.4 us
  local copies, waits for them, and re-layouts: 17.5 us -> 20 us
    pallas_call x0 -> x1, Pallas kernels: none -> 30.2 us  [swap(): pl.pallas_call(functools.partial(swap_kernel, lanes), out_shape=(jax.Shap...]
    all_to_all x1 -> x0, starting transfers between devices: 11.5 us -> none  [per_device(): lax.all_to_all(jnp.broadcast_to(own_lists, (peers, own_lists.shape[1])),...]
    ppermute x2, waiting for transfers between devices: 0.01 us -> 11.4 us  [shifted(): return lax.ppermute(block, axis, route)]
    pallas_call x2, Pallas kernels: 91 us -> 83.4 us  [exchange(): pl.pallas_call(functools.partial(exchange_kernel, route, lanes), out_shap...]
    ppermute x1 -> x0, starting transfers between devices: 6.35 us -> none  [per_device(): arrived_half = lax.ppermute(theirs, 'head', [(0, 1), (1, 0)])]
  transfers between devices with their start and end apart: 4 -> 2, of which waited for: 1 -> 1; matrix products, arithmetic and copies ran while one was open for 12% -> 7% of each run, Pallas kernels for 0% -> 0%
where the time goes in v9:
time: 169 us; the launch traced here: 168 us
  Pallas kernels  114 us (67%)
  local copies, waits for them, and re-layouts  20 us (12%)
  waiting for transfers between devices  11.4 us (7%)
  matrix products  9.13 us (5%)
  starting transfers between devices  6.85 us (4%)
  other arithmetic  6.82 us (4%)
    pallas_call x2, Pallas kernels, exchange(): pl.pallas_call(functools.partial(exchange_kernel, route, lanes), out_shap...  83.4 us
    pallas_call x1, Pallas kernels, swap(): pl.pallas_call(functools.partial(swap_kernel, lanes), out_shape=(jax.Shap...  30.2 us
    ppermute x2, waiting for transfers between devices, shifted(): return lax.ppermute(block, axis, route)  11.4 us
    ppermute x2, starting transfers between devices, shifted(): return lax.ppermute(block, axis, route)  6.85 us
  transfers between devices with their start and end apart: 2, of which 1 were waited for; matrix products, arithmetic and copies ran while one was open for 7% of the time, Pallas kernels for 0%

profile of v9, /device:TPU:1, one launch (start us, length us, event | category | flops | bytes accessed | tf_op | source)
XLA Modules:
  0.0 168.3 jit_solution(7163839906997300023)
XLA Ops:
  0.0 0.8 copy.34
  0.8 0.8 pad_add_fusion
  1.6 4.9 %collective-permute-start = (s32[4,17]{1,0:T(4,128)S(1)}, s32[4,17]{1,0:T(4,128)S(1)}, u32[]{:S(2)}, u32[]{:S(2)}) collective-permute-start(s32[4,17]{1,0:T(4,128)S(1)} %pad_add_fusion), channel_id=1, source_target_pairs={{0,2},{2,4},{4,6},{6,8},{8,10},{10,12},{12,14},{14,16},{16,18},{18... | collective-permute-start | bytes 824 | tf_op jit(solution)/shard_map/ppermute | solution.py:137
  6.5 1.9 %collective-permute-start.1 = (bf16[2,64,16,512]{3,2,1,0:T(8,128)(2,1)}, bf16[2,64,16,512]{3,2,1,0:T(8,128)(2,1)}, u32[]{:S(2)}, u32[]{:S(2)}) collective-permute-start(bf16[2,64,16,512]{3,2,1,0:T(8,128)(2,1)} %param.20), channel_id=1, source_target_pairs={{0,2},{2,4},{4,6},{6,8},{8,10},{10,12},{12,14},{14,16},{16,18},{18... | collective-permute-start | bytes 6291464 | tf_op jit(solution)/shard_map/ppermute | solution.py:137
  8.5 0.7 broadcast_compare_fusion.1
  9.2 1.2 gather_fusion.2
  10.6 1.3 gather_fusion.3
  11.9 2.7 %fusion.33 = (bf16[1,64,16,512]{3,2,1,0:T(8,128)(2,1)}, bf16[1,64,16,512]{3,2,1,0:T(8,128)(2,1)S(1)}) fusion(bf16[2,64,16,512]{3,2,1,0:T(8,128)(2,1)} %param.20), kind=kLoop, calls=%fused_computation.140 | loop fusion | bytes 4194304 | tf_op jit(solution)/shard_map/slice | solution.py:192
  14.6 0.2 convolution_bitcast_fusion
  14.8 0.2 convolution_bitcast_fusion.1
  15.0 0.2 convolution_bitcast_fusion.2
  15.2 0.2 convolution_bitcast_fusion.3
  15.6 0.1 and.80
  15.9 0.1 add.102
  16.3 0.1 fusion.36
  16.5 1.6 copy.46
  18.1 0.6 gather_fusion
  18.9 0.1 and.74
  19.0 0.1 and.75
  19.3 0.1 add.99
  19.4 0.2 slice_reduce_fusion
  19.6 0.6 gather_fusion.1
  20.4 11.4 %collective-permute-done.1 = bf16[2,64,16,512]{3,2,1,0:T(8,128)(2,1)} collective-permute-done((bf16[2,64,16,512]{3,2,1,0:T(8,128)(2,1)}, bf16[2,64,16,512]{3,2,1,0:T(8,128)(2,1)}, u32[]{:S(2)}, u32[]{:S(2)}) %collective-permute-start.1) | collective-permute-done | bytes 2097184 | tf_op jit(solution)/shard_map/ppermute | solution.py:137
  31.7 1.7 %fusion.34 = (bf16[1,64,16,512]{3,2,1,0:T(8,128)(2,1)S(1)}, bf16[1,64,16,512]{3,2,1,0:T(8,128)(2,1)S(1)}) fusion(bf16[2,64,16,512]{3,2,1,0:T(8,128)(2,1)} %collective-permute-done.1), kind=kLoop, calls=%fused_computation.141 | loop fusion | bytes 4194304 | tf_op jit(solution)/shard_map/slice | solution.py:161
  33.4 0.2 convolution_bitcast_fusion.4
  33.6 0.2 convolution_bitcast_fusion.5
  33.8 0.2 convolution_bitcast_fusion.6
  34.0 0.2 convolution_bitcast_fusion.7
  34.3 0.2 select_reduce_fusion
  34.5 0.4 fusion.12
  34.9 0.3 divide_convert_fusion
  35.2 0.3 copy-done.1
  35.5 0.2 convolution_bitcast_fusion.11
  35.7 0.2 convolution_bitcast_fusion.10
  35.8 0.2 convolution_bitcast_fusion.9
  36.0 0.2 convolution_bitcast_fusion.8
  36.2 0.2 convolution_bitcast_fusion.15
  36.3 0.2 convolution_bitcast_fusion.14
  36.5 0.2 convolution_bitcast_fusion.13
  36.7 0.2 convolution_bitcast_fusion.12
  37.0 0.7 constant_dynamic-slice_fusion.1
  37.6 0.8 broadcast_in_dim.100.lists_ref
  38.4 30.2 %shard_map.163 = (bf16[2,4096]{1,0:T(2,128)(2,1)}, s32[128,8,128]{2,1,0:T(8,128)}) custom-call(bf16[2,4096]{1,0:T(2,128)(2,1)} %get-tuple-element.27.half_ref, s32[128,8,128]{2,1,0:T(8,128)} %broadcast_in_dim.100.lists_ref), custom_call_target="tpu_custom_call" | custom-call | tf_op jit(solution)/shard_map/pallas_call | solution.py:121
  68.6 1.0 multiply_reduce_fusion.4
  69.7 1.1 slice.179
  70.9 0.1 multiply_convert_fusion.2
  71.0 2.0 %convolution_convert_fusion = bf16[4096,256]{1,0:T(8,128)(2,1)} fusion(s32[4096]{0:T(1024)S(1)} %eq.80, bf16[8,8,2,128]{3,2,1,0:T(2,128)(2,1)S(1)} %bitcast.244), kind=kOutput, calls=%fused_computation.6 | convolution fusion | flops 135528448 | bytes 2146304 | tf_op jit(solution)/shard_map/dot_general | solution.py:282
  73.1 42.1 %shard_map.164 = bf16[128,32,256]{2,1,0:T(8,128)(2,1)} custom-call(bf16[128,32,256]{2,1,0:T(8,128)(2,1)} %bitcast.211), custom_call_target="tpu_custom_call" | custom-call | tf_op jit(solution)/shard_map/pallas_call | solution.py:67
  115.2 1.9 %fusion.32 = (bf16[128,32,128]{2,1,0:T(8,128)(2,1)S(1)}, bf16[128,32,128]{2,1,0:T(8,128)(2,1)S(1)}) fusion(bf16[128,32,256]{2,1,0:T(8,128)(2,1)} %shard_map.164), kind=kLoop, calls=%fused_computation.139 | loop fusion | bytes 4194304 | tf_op jit(solution)/shard_map/slice | solution.py:289
  117.1 0.7 multiply_reduce_fusion
  117.8 0.7 multiply_reduce_fusion.2
  118.5 0.5 copy-done.8
  119.0 0.7 multiply_reduce_fusion.1
  119.7 0.7 multiply_reduce_fusion.3
  120.5 0.7 fusion
  121.3 0.2 slice_bitcast_fusion.1
  121.4 0.2 copy.56
  121.7 0.2 copy.57
  121.9 1.7 pad_maximum_fusion.x_ref
  123.6 41.4 %shard_map.165 = bf16[128,32,256]{2,1,0:T(8,128)(2,1)} custom-call(bf16[128,32,256]{2,1,0:T(8,128)(2,1)} %pad_maximum_fusion.x_ref), custom_call_target="tpu_custom_call" | custom-call | tf_op jit(solution)/shard_map/pallas_call | solution.py:67
  165.0 1.9 %fusion.31 = (bf16[128,32,128]{2,1,0:T(8,128)(2,1)S(1)}, bf16[128,32,128]{2,1,0:T(8,128)(2,1)S(1)}) fusion(bf16[128,32,256]{2,1,0:T(8,128)(2,1)} %shard_map.165), kind=kLoop, calls=%fused_computation.138 | loop fusion | bytes 4194304 | tf_op jit(solution)/shard_map/slice | solution.py:307
  167.0 0.3 fusion.7
  167.3 0.3 fusion.6
  167.6 0.7 fusion.20
  (60 shorter events, 1.8 us)
Async XLA Ops:
  0.0 117.1 %copy-start = (bf16[1,32,128,128]{3,2,1,0:T(8,128)(2,1)S(1)}, bf16[1,32,128,128]{3,2,1,0:T(8,128)(2,1)}, u32[]{:S(2)}) copy-start(bf16[1,32,128,128]{3,2,1,0:T(8,128)(2,1)} %param.27) | copy-start | bytes 3145732
  1.6 16.5 %collective-permute-start = (s32[4,17]{1,0:T(4,128)S(1)}, s32[4,17]{1,0:T(4,128)S(1)}, u32[]{:S(2)}, u32[]{:S(2)}) collective-permute-start(s32[4,17]{1,0:T(4,128)S(1)} %pad_add_fusion), channel_id=1, source_target_pairs={{0,2},{2,4},{4,6},{6,8},{8,10},{10,12},{12,14},{14,16},{16,18},{18... | collective-permute-start | bytes 824 | tf_op jit(solution)/shard_map/ppermute | solution.py:137
  6.5 25.2 %collective-permute-start.1 = (bf16[2,64,16,512]{3,2,1,0:T(8,128)(2,1)}, bf16[2,64,16,512]{3,2,1,0:T(8,128)(2,1)}, u32[]{:S(2)}, u32[]{:S(2)}) collective-permute-start(bf16[2,64,16,512]{3,2,1,0:T(8,128)(2,1)} %param.20), channel_id=1, source_target_pairs={{0,2},{2,4},{4,6},{6,8},{8,10},{10,12},{12,14},{14,16},{16,18},{18... | collective-permute-start | bytes 6291464 | tf_op jit(solution)/shard_map/ppermute | solution.py:137
  11.9 2.7 %copy-start.3 = (bf16[4,4096]{1,0:T(4,128)(2,1)S(1)}, bf16[4,4096]{1,0:T(4,128)(2,1)}, u32[]{:S(2)}) copy-start(bf16[4,4096]{1,0:T(4,128)(2,1)} %param.17) | copy-start | bytes 98308
  14.6 1.5 copy-start.5
  14.6 1.5 copy-start.9
  14.6 1.5 copy-start.10
  14.6 1.6 copy-start.6
  14.6 1.7 copy-start.7
  34.3 1.2 copy-start.1
  35.2 33.4 %copy-start.2 = (bf16[2,8192]{1,0:T(2,128)(2,1)S(1)}, bf16[2,8192]{1,0:T(2,128)(2,1)}, u32[]{:S(2)}) copy-start(bf16[2,8192]{1,0:T(2,128)(2,1)} %param.24) | copy-start | bytes 98308
  35.8 35.1 %copy-start.4 = (f32[8192]{0:T(1024)S(1)}, f32[8192]{0:T(1024)}, u32[]{:S(2)}) copy-start(f32[8192]{0:T(1024)} %param.25) | copy-start | bytes 98308
  115.1 1.9 %copy-start.11 = (f32[1,32]{1,0:T(1,128)S(1)}, f32[1,32]{1,0:T(1,128)}, u32[]{:S(2)}) copy-start(f32[1,32]{1,0:T(1,128)} %param.30) | copy-start | bytes 388
  117.8 1.2 copy-start.8
  117.8 1.2 copy-start.12

commit v10 on v8

--- a/solution.py
+++ b/solution.py
@@ -72,6 +72,87 @@
         scratch_shapes=[pltpu.SemaphoreType.DMA, pltpu.SemaphoreType.DMA, pltpu.SemaphoreType.DMA],
         compiler_params=pltpu.CompilerParams(has_side_effects=True),
     )(x)
+
+
+def staged_kernel(route, lanes, x_ref, y_ref, mid_ref, sems):
+    me = lax.axis_index("wide")
+    here = lax.axis_index("head")
+    inner, outer = x_ref.shape[0], x_ref.shape[1]
+    near, far = me % inner, me // inner
+    first_local = pltpu.make_async_copy(x_ref.at[near], mid_ref.at[near], sems.at[0])
+    first_local.start()
+
+    def first(j, carry):
+        part = lax.rem(near + j, inner)
+        peer = far * inner + part
+        pltpu.make_async_remote_copy(
+            src_ref=x_ref.at[part],
+            dst_ref=mid_ref.at[near],
+            send_sem=sems.at[1],
+            recv_sem=sems.at[2],
+            device_id=(peer, route(me, here, peer, lanes)),
+            device_id_type=pl.DeviceIdType.MESH,
+        ).start()
+        return carry
+
+    lax.fori_loop(1, inner, first, 0)
+    first_all = pltpu.make_async_remote_copy(
+        src_ref=mid_ref.at[pl.ds(0, inner - 1)],
+        dst_ref=mid_ref.at[pl.ds(0, inner - 1)],
+        send_sem=sems.at[1],
+        recv_sem=sems.at[2],
+        device_id=(me, here),
+        device_id_type=pl.DeviceIdType.MESH,
+    )
+    first_all.wait_recv()
+    first_local.wait()
+    second_local = pltpu.make_async_copy(mid_ref.at[:, far], y_ref.at[far], sems.at[3])
+    second_local.start()
+
+    def second(j, carry):
+        part = lax.rem(far + j, outer)
+        pltpu.make_async_remote_copy(
+            src_ref=mid_ref.at[:, part],
+            dst_ref=y_ref.at[far],
+            send_sem=sems.at[4],
+            recv_sem=sems.at[5],
+            device_id=(part * inner + near, here),
+            device_id_type=pl.DeviceIdType.MESH,
+        ).start()
+        return carry
+
+    lax.fori_loop(1, outer, second, 0)
+    second_all = pltpu.make_async_remote_copy(
+        src_ref=y_ref.at[pl.ds(0, outer - 1)],
+        dst_ref=y_ref.at[pl.ds(0, outer - 1)],
+        send_sem=sems.at[4],
+        recv_sem=sems.at[5],
+        device_id=(me, here),
+        device_id_type=pl.DeviceIdType.MESH,
+    )
+    second_all.wait_recv()
+    second_all.wait_send()
+    first_all.wait_send()
+    second_local.wait()
+
+
+def staged_exchange(x, route, lanes):
+    peers, depth, width = x.shape
+    inner = 2 * lanes
+    outer = peers // inner
+    by_part = jnp.swapaxes(x.reshape(outer, inner, depth, width), 0, 1)
+    y, _ = pl.pallas_call(
+        functools.partial(staged_kernel, route, lanes),
+        out_shape=(
+            jax.ShapeDtypeStruct((outer, inner, depth, width), x.dtype),
+            jax.ShapeDtypeStruct((inner, outer, depth, width), x.dtype),
+        ),
+        in_specs=[pl.BlockSpec(memory_space=pl.ANY)],
+        out_specs=(pl.BlockSpec(memory_space=pl.ANY),) * 2,
+        scratch_shapes=[pltpu.SemaphoreType.DMA((6,))],
+        compiler_params=pltpu.CompilerParams(has_side_effects=True),
+    )(by_part)
+    return y.reshape(peers, depth, width)
 
 
 def shifted(block, axis, distance):
@@ -227,7 +308,7 @@
     outgoing = jnp.dot(
         choose, by_block.reshape(feature_blocks, rows * BLK), preferred_element_type=jnp.float32
     ).astype(jnp.bfloat16)
-    picked = exchange(outgoing.reshape(peers, keep, rows * BLK), gather_route, Z_LANES)
+    picked = staged_exchange(outgoing.reshape(peers, keep, rows * BLK), gather_route, Z_LANES)
     hidden = jnp.concatenate(
         [
             hidden_units(
@@ -243,7 +324,7 @@
     contrib = lax.optimization_barrier((down_part * column_scale[None, :]).astype(jnp.bfloat16))
     contrib = contrib.reshape(rows, peers, keep, BLK)
     outgoing_sums = jnp.concatenate([contrib[r] for r in range(rows)], axis=-1)
-    arrived = exchange(outgoing_sums, return_route, Z_LANES)
+    arrived = staged_exchange(outgoing_sums, return_route, Z_LANES)
     placement = (blocks[:, None] == out_keep.reshape(1, peers * keep)).astype(jnp.bfloat16)
     summed = jnp.stack(
         [

time: 151 us -> 209 us (1.38)
  the two profiles are of different devices: /device:TPU:1 before, /device:TPU:28 now
where the time goes in v10:
time: 209 us
  Pallas kernels  144 us (69%)
  starting transfers between devices  24.7 us (12%)
  local copies, waits for them, and re-layouts  19 us (9%)
  matrix products  9.3 us (4%)
  other arithmetic  6.7 us (3%)
  waiting for transfers between devices  4.29 us (2%)
    pallas_call x2, Pallas kernels, staged_exchange(): pl.pallas_call(functools.partial(staged_kernel, route, lanes), out_shape=...  144 us
    all_to_all x1, starting transfers between devices, per_device(): lax.all_to_all(jnp.broadcast_to(own_lists, (peers, own_lists.shape[1])),...  11.6 us
    ppermute x1, starting transfers between devices, per_device(): arrived_half = lax.ppermute(theirs, 'head', [(0, 1), (1, 0)])  7.27 us
    ppermute x2, starting transfers between devices, shifted(): return lax.ppermute(block, axis, route)  5.84 us
  transfers between devices with their start and end apart: 4, of which 2 were waited for; matrix products, arithmetic and copies ran while one was open for 8% of the time, Pallas kernels for 0%

profile of v10, /device:TPU:28, one launch (start us, length us, event | category | flops | bytes accessed | tf_op | source)
XLA Modules:
  0.0 208.9 jit_solution(2042788757360991549)
XLA Ops:
  0.0 0.8 copy.50
  0.8 0.8 pad_add_fusion
  1.6 1.9 collective-permute-start
  3.5 3.9 %collective-permute-start.1 = (bf16[2,64,16,512]{3,2,1,0:T(8,128)(2,1)}, bf16[2,64,16,512]{3,2,1,0:T(8,128)(2,1)}, u32[]{:S(2)}, u32[]{:S(2)}) collective-permute-start(bf16[2,64,16,512]{3,2,1,0:T(8,128)(2,1)} %param.20), channel_id=1, source_target_pairs={{0,2},{2,4},{4,6},{6,8},{8,10},{10,12},{12,14},{14,16},{16,18},{18... | collective-permute-start | bytes 6291464 | tf_op jit(solution)/shard_map/ppermute | solution.py:161
  7.4 0.7 add_bitcast_fusion.1
  8.2 0.7 broadcast_in_dim.102
  8.8 11.6 %all-to-all-start = ((s32[128,1,64]{2,1,0:T(1,128)}), s32[128,1,64]{2,1,0:T(1,128)S(1)}, u32[]{:S(2)}, u32[]{:S(2)}) async-start(s32[128,1,64]{2,1,0:T(1,128)} %broadcast_in_dim.102), calls=%async_computation | async-start | bytes 131072 | tf_op jit(solution)/shard_map/all_to_all | solution.py:294
  20.5 0.7 broadcast_compare_fusion.1
  21.2 1.2 gather_fusion.2
  22.6 2.7 %fusion.33 = (bf16[1,64,16,512]{3,2,1,0:T(8,128)(2,1)}, bf16[1,64,16,512]{3,2,1,0:T(8,128)(2,1)S(1)}) fusion(bf16[2,64,16,512]{3,2,1,0:T(8,128)(2,1)} %param.20), kind=kLoop, calls=%fused_computation.144 | loop fusion | bytes 4194304 | tf_op jit(solution)/shard_map/slice | solution.py:216
  25.4 0.2 convolution_bitcast_fusion
  25.6 0.2 convolution_bitcast_fusion.1
  25.8 0.2 convolution_bitcast_fusion.2
  26.1 0.2 convolution_bitcast_fusion.3
  26.3 0.6 gather_fusion.3
  27.0 0.1 and.80
  27.2 0.1 add.100
  27.6 0.1 fusion.36
  27.8 1.6 copy.61
  29.4 0.6 gather_fusion
  30.3 0.1 and.75
  30.6 0.1 add.97
  30.7 0.2 slice_reduce_fusion
  30.9 0.6 gather_fusion.1
  31.6 2.8 %collective-permute-done.1 = bf16[2,64,16,512]{3,2,1,0:T(8,128)(2,1)} collective-permute-done((bf16[2,64,16,512]{3,2,1,0:T(8,128)(2,1)}, bf16[2,64,16,512]{3,2,1,0:T(8,128)(2,1)}, u32[]{:S(2)}, u32[]{:S(2)}) %collective-permute-start.1) | collective-permute-done | bytes 2097184 | tf_op jit(solution)/shard_map/ppermute | solution.py:161
  34.5 1.7 fusion.34
  36.2 0.2 convolution_bitcast_fusion.4
  36.4 0.2 convolution_bitcast_fusion.5
  36.6 0.2 convolution_bitcast_fusion.6
  36.8 0.2 convolution_bitcast_fusion.7
  37.0 0.2 select_reduce_fusion
  37.3 0.4 fusion.12
  37.6 0.3 divide_convert_fusion
  38.0 0.3 copy-done.2
  38.3 0.2 convolution_bitcast_fusion.11
  38.4 0.2 convolution_bitcast_fusion.10
  38.6 0.2 convolution_bitcast_fusion.9
  38.7 0.2 convolution_bitcast_fusion.8
  38.9 0.2 convolution_bitcast_fusion.15
  39.1 0.2 convolution_bitcast_fusion.14
  39.2 0.2 convolution_bitcast_fusion.13
  39.4 0.2 convolution_bitcast_fusion.12
  39.7 7.3 %collective-permute-start.2 = (bf16[2,4096]{1,0:T(2,128)(2,1)S(1)}, bf16[2,4096]{1,0:T(2,128)(2,1)S(1)}, u32[]{:S(2)}, u32[]{:S(2)}) collective-permute-start(bf16[2,4096]{1,0:T(2,128)(2,1)S(1)} %get-tuple-element.26), channel_id=1, source_target_pairs={{0,1},{1,0},{2,3},{3,2},{4,5},{5,4},{6,7},{7,6},{8,9},{9,8},{10,11... | collective-permute-start | bytes 49160 | tf_op jit(solution)/shard_map/ppermute | solution.py:282
  47.3 1.5 collective-permute-done.2
  48.7 0.2 multiply_reduce_fusion.4
  49.1 2.2 %convolution_convert_fusion = bf16[4096,256]{1,0:T(8,128)(2,1)S(1)} fusion(s32[4096]{0:T(1024)S(1)} %eq.80, bf16[8,8,2,128]{3,2,1,0:T(2,128)(2,1)S(1)} %bitcast.260), kind=kOutput, calls=%fused_computation.6 | convolution fusion | flops 135528448 | bytes 2146304 | tf_op jit(solution)/shard_map/dot_general | solution.py:308
  51.3 1.5 copy.112
  52.8 65.8 %shard_map.163 = (bf16[16,8,32,256]{3,2,1,0:T(8,128)(2,1)}, bf16[8,16,32,256]{3,2,1,0:T(8,128)(2,1)}) custom-call(bf16[8,16,32,256]{3,2,1,0:T(8,128)(2,1)} %bitcast.226), custom_call_target="tpu_custom_call" | custom-call | tf_op jit(solution)/shard_map/pallas_call | solution.py:144
  118.6 1.9 fusion.32
  120.6 0.7 multiply_reduce_fusion
  121.3 0.7 multiply_reduce_fusion.2
  122.0 0.5 copy-done.9
  122.5 0.7 multiply_reduce_fusion.1
  123.2 0.7 multiply_reduce_fusion.3
  124.0 0.7 fusion
  124.8 0.2 slice_bitcast_fusion.1
  124.9 0.2 copy.113
  125.2 0.2 copy.114
  125.4 1.7 copy_bitcast_fusion.x_ref
  127.1 78.5 %shard_map.164 = (bf16[16,8,32,256]{3,2,1,0:T(8,128)(2,1)}, bf16[8,16,32,256]{3,2,1,0:T(8,128)(2,1)}) custom-call(bf16[8,16,32,256]{3,2,1,0:T(8,128)(2,1)} %copy_bitcast_fusion.x_ref), custom_call_target="tpu_custom_call" | custom-call | tf_op jit(solution)/shard_map/pallas_call | solution.py:144
  205.6 1.9 fusion.31
  207.5 0.3 fusion.7
  207.8 0.3 fusion.6
  208.1 0.7 fusion.20
  (60 shorter events, 2.0 us)
Async XLA Ops:
  0.0 120.6 %copy-start = (bf16[1,32,128,128]{3,2,1,0:T(8,128)(2,1)S(1)}, bf16[1,32,128,128]{3,2,1,0:T(8,128)(2,1)}, u32[]{:S(2)}) copy-start(bf16[1,32,128,128]{3,2,1,0:T(8,128)(2,1)} %param.27) | copy-start | bytes 3145732
  1.6 27.8 %collective-permute-start = (s32[4,17]{1,0:T(4,128)S(1)}, s32[4,17]{1,0:T(4,128)S(1)}, u32[]{:S(2)}, u32[]{:S(2)}) collective-permute-start(s32[4,17]{1,0:T(4,128)S(1)} %pad_add_fusion), channel_id=1, source_target_pairs={{0,2},{2,4},{4,6},{6,8},{8,10},{10,12},{12,14},{14,16},{16,18},{18... | collective-permute-start | bytes 824 | tf_op jit(solution)/shard_map/ppermute | solution.py:161
  3.5 31.0 %collective-permute-start.1 = (bf16[2,64,16,512]{3,2,1,0:T(8,128)(2,1)}, bf16[2,64,16,512]{3,2,1,0:T(8,128)(2,1)}, u32[]{:S(2)}, u32[]{:S(2)}) collective-permute-start(bf16[2,64,16,512]{3,2,1,0:T(8,128)(2,1)} %param.20), channel_id=1, source_target_pairs={{0,2},{2,4},{4,6},{6,8},{8,10},{10,12},{12,14},{14,16},{16,18},{18... | collective-permute-start | bytes 6291464 | tf_op jit(solution)/shard_map/ppermute | solution.py:161
  8.8 38.2 %all-to-all-start = ((s32[128,1,64]{2,1,0:T(1,128)}), s32[128,1,64]{2,1,0:T(1,128)S(1)}, u32[]{:S(2)}, u32[]{:S(2)}) async-start(s32[128,1,64]{2,1,0:T(1,128)} %broadcast_in_dim.102), calls=%async_computation | async-start | bytes 131072 | tf_op jit(solution)/shard_map/all_to_all | solution.py:294
  22.6 2.7 %copy-start.4 = (bf16[4,4096]{1,0:T(4,128)(2,1)S(1)}, bf16[4,4096]{1,0:T(4,128)(2,1)}, u32[]{:S(2)}) copy-start(bf16[4,4096]{1,0:T(4,128)(2,1)} %param.17) | copy-start | bytes 98308
  22.6 3.6 %copy-start.1 = (s32[4]{0:T(128)S(1)}, s32[4]{0:T(128)}, u32[]{:S(2)}) copy-start(s32[4]{0:T(128)} %param.22) | copy-start | bytes 52
  25.4 2.0 copy-start.6
  25.4 2.1 %copy-start.7 = (bf16[4,512]{1,0:T(4,128)(2,1)S(1)}, bf16[4,512]{1,0:T(4,128)(2,1)}, u32[]{:S(2)}) copy-start(bf16[4,512]{1,0:T(4,128)(2,1)} %param.19) | copy-start | bytes 12292
  25.4 2.1 %copy-start.8 = (f32[1,32]{1,0:T(1,128)S(1)}, f32[1,32]{1,0:T(1,128)}, u32[]{:S(2)}) copy-start(f32[1,32]{1,0:T(1,128)} %param.33) | copy-start | bytes 388
  37.0 1.2 copy-start.2
  38.0 10.8 %copy-start.3 = (bf16[2,8192]{1,0:T(2,128)(2,1)S(1)}, bf16[2,8192]{1,0:T(2,128)(2,1)}, u32[]{:S(2)}) copy-start(bf16[2,8192]{1,0:T(2,128)(2,1)} %param.24) | copy-start | bytes 98308
  38.0 11.0 %copy-start.5 = (f32[8192]{0:T(1024)S(1)}, f32[8192]{0:T(1024)}, u32[]{:S(2)}) copy-start(f32[8192]{0:T(1024)} %param.25) | copy-start | bytes 98308
  39.7 9.0 %collective-permute-start.2 = (bf16[2,4096]{1,0:T(2,128)(2,1)S(1)}, bf16[2,4096]{1,0:T(2,128)(2,1)S(1)}, u32[]{:S(2)}, u32[]{:S(2)}) collective-permute-start(bf16[2,4096]{1,0:T(2,128)(2,1)S(1)} %get-tuple-element.26), channel_id=1, source_target_pairs={{0,1},{1,0},{2,3},{3,2},{4,5},{5,4},{6,7},{7,6},{8,9},{9,8},{10,11... | collective-permute-start | bytes 49160 | tf_op jit(solution)/shard_map/ppermute | solution.py:282
  118.6 1.9 copy-start.10
  121.3 1.2 copy-start.9
  121.3 1.2 copy-start.11

commit v11 on v8

--- a/solution.py
+++ b/solution.py
@@ -34,42 +34,50 @@
     me = lax.axis_index("wide")
     here = lax.axis_index("head")
     n = x_ref.shape[0]
+    ways = send_sem.shape[0]
     local = pltpu.make_async_copy(x_ref.at[me], y_ref.at[me], local_sem)
     local.start()
-
-    def send(j, carry):
-        peer = lax.rem(me + j, n)
-        pltpu.make_async_remote_copy(
-            src_ref=x_ref.at[peer],
-            dst_ref=y_ref.at[me],
-            send_sem=send_sem,
-            recv_sem=recv_sem,
-            device_id=(peer, route(me, here, peer, lanes)),
+    for way in range(ways):
+
+        def send(step, carry, way=way):
+            peer = lax.rem(me + step * ways + way, n)
+            pltpu.make_async_remote_copy(
+                src_ref=x_ref.at[peer],
+                dst_ref=y_ref.at[me],
+                send_sem=send_sem.at[way],
+                recv_sem=recv_sem.at[way],
+                device_id=(peer, route(me, here, peer, lanes)),
+                device_id_type=pl.DeviceIdType.MESH,
+            ).start()
+            return carry
+
+        lax.fori_loop(1 if way == 0 else 0, (n - way + ways - 1) // ways, send, 0)
+    for way in range(ways):
+        count = (n - way + ways - 1) // ways - (1 if way == 0 else 0)
+        every = pltpu.make_async_remote_copy(
+            src_ref=x_ref.at[pl.ds(0, count)],
+            dst_ref=y_ref.at[pl.ds(0, count)],
+            send_sem=send_sem.at[way],
+            recv_sem=recv_sem.at[way],
+            device_id=(me, here),
             device_id_type=pl.DeviceIdType.MESH,
-        ).start()
-        return carry
-
-    lax.fori_loop(1, n, send, 0)
-    every = pltpu.make_async_remote_copy(
-        src_ref=x_ref.at[pl.ds(0, n - 1)],
-        dst_ref=y_ref.at[pl.ds(0, n - 1)],
-        send_sem=send_sem,
-        recv_sem=recv_sem,
-        device_id=(me, here),
-        device_id_type=pl.DeviceIdType.MESH,
-    )
-    every.wait_send()
-    every.wait_recv()
+        )
+        every.wait_send()
+        every.wait_recv()
     local.wait()
 
 
-def exchange(x, route, lanes):
+def exchange(x, route, lanes, ways=8):
     return pl.pallas_call(
         functools.partial(exchange_kernel, route, lanes),
         out_shape=jax.ShapeDtypeStruct(x.shape, x.dtype),
         in_specs=[pl.BlockSpec(memory_space=pl.ANY)],
         out_specs=pl.BlockSpec(memory_space=pl.ANY),
-        scratch_shapes=[pltpu.SemaphoreType.DMA, pltpu.SemaphoreType.DMA, pltpu.SemaphoreType.DMA],
+        scratch_shapes=[
+            pltpu.SemaphoreType.DMA((ways,)),
+            pltpu.SemaphoreType.DMA((ways,)),
+            pltpu.SemaphoreType.DMA,
+        ],
         compiler_params=pltpu.CompilerParams(has_side_effects=True),
     )(x)
 

time: 151 us -> 146 us (0.967)
  Pallas kernels: 91 us -> 86.5 us
    pallas_call x2, Pallas kernels: 91 us -> 86.5 us  [exchange(): pl.pallas_call(functools.partial(exchange_kernel, route, lanes), out_shap...]
where the time goes in v11:
time: 146 us
  Pallas kernels  86.5 us (59%)
  starting transfers between devices  24.7 us (17%)
  local copies, waits for them, and re-layouts  17.5 us (12%)
  matrix products  9.12 us (6%)
  other arithmetic  6.69 us (5%)
    pallas_call x2, Pallas kernels, exchange(): pl.pallas_call(functools.partial(exchange_kernel, route, lanes), out_shap...  86.5 us
    all_to_all x1, starting transfers between devices, per_device(): lax.all_to_all(jnp.broadcast_to(own_lists, (peers, own_lists.shape[1])),...  11.5 us
    ppermute x2, starting transfers between devices, shifted(): return lax.ppermute(block, axis, route)  6.85 us
    ppermute x1, starting transfers between devices, per_device(): arrived_half = lax.ppermute(theirs, 'head', [(0, 1), (1, 0)])  6.35 us
    unnamed x30, local copies, waits for them, and re-layouts  3.16 us
  transfers between devices with their start and end apart: 4, of which 1 were waited for; matrix products, arithmetic and copies ran while one was open for 12% of the time, Pallas kernels for 0%

profile of v11, /device:TPU:1, one launch (start us, length us, event | category | flops | bytes accessed | tf_op | source)
XLA Modules:
  0.0 145.9 jit_solution(16586302694281556431)
XLA Ops:
  0.0 0.8 copy.46
  0.8 0.8 pad_add_fusion
  1.6 4.9 %collective-permute-start = (s32[4,17]{1,0:T(4,128)S(1)}, s32[4,17]{1,0:T(4,128)S(1)}, u32[]{:S(2)}, u32[]{:S(2)}) collective-permute-start(s32[4,17]{1,0:T(4,128)S(1)} %pad_add_fusion), channel_id=1, source_target_pairs={{0,2},{2,4},{4,6},{6,8},{8,10},{10,12},{12,14},{14,16},{16,18},{18... | collective-permute-start | bytes 824 | tf_op jit(solution)/shard_map/ppermute | solution.py:88
  6.5 1.9 %collective-permute-start.1 = (bf16[2,64,16,512]{3,2,1,0:T(8,128)(2,1)}, bf16[2,64,16,512]{3,2,1,0:T(8,128)(2,1)}, u32[]{:S(2)}, u32[]{:S(2)}) collective-permute-start(bf16[2,64,16,512]{3,2,1,0:T(8,128)(2,1)} %param.20), channel_id=1, source_target_pairs={{0,2},{2,4},{4,6},{6,8},{8,10},{10,12},{12,14},{14,16},{16,18},{18... | collective-permute-start | bytes 6291464 | tf_op jit(solution)/shard_map/ppermute | solution.py:88
  8.5 0.7 add_bitcast_fusion.1
  9.2 0.7 broadcast_in_dim.102
  9.9 11.5 %all-to-all-start = ((s32[128,1,64]{2,1,0:T(1,128)}), s32[128,1,64]{2,1,0:T(1,128)S(1)}, u32[]{:S(2)}, u32[]{:S(2)}) async-start(s32[128,1,64]{2,1,0:T(1,128)} %broadcast_in_dim.102), calls=%async_computation | async-start | bytes 131072 | tf_op jit(solution)/shard_map/all_to_all | solution.py:221
  21.3 0.7 broadcast_compare_fusion.1
  22.0 1.2 gather_fusion.2
  23.5 2.7 %fusion.33 = (bf16[1,64,16,512]{3,2,1,0:T(8,128)(2,1)}, bf16[1,64,16,512]{3,2,1,0:T(8,128)(2,1)S(1)}) fusion(bf16[2,64,16,512]{3,2,1,0:T(8,128)(2,1)} %param.20), kind=kLoop, calls=%fused_computation.140 | loop fusion | bytes 4194304 | tf_op jit(solution)/shard_map/slice | solution.py:143
  26.2 0.2 convolution_bitcast_fusion
  26.4 0.2 convolution_bitcast_fusion.1
  26.6 0.2 convolution_bitcast_fusion.2
  26.9 0.2 convolution_bitcast_fusion.3
  27.1 0.6 gather_fusion.3
  27.9 0.1 and.80
  28.1 0.1 add.100
  28.4 0.1 fusion.36
  28.6 1.6 %copy.58 = bf16[1,32,128,128]{2,3,1,0:T(8,128)(2,1)S(1)} copy(bf16[1,32,128,128]{3,2,1,0:T(8,128)(2,1)} %param.31) | data formatting | bytes 2097152 | tf_op args[14]
  30.3 0.6 gather_fusion
  31.0 0.1 and.74
  31.1 0.1 and.75
  31.4 0.1 add.97
  31.6 0.2 slice_reduce_fusion
  31.7 0.6 gather_fusion.1
  32.5 1.7 %fusion.34 = (bf16[1,64,16,512]{3,2,1,0:T(8,128)(2,1)S(1)}, bf16[1,64,16,512]{3,2,1,0:T(8,128)(2,1)S(1)}) fusion(bf16[2,64,16,512]{3,2,1,0:T(8,128)(2,1)} %collective-permute-done.1), kind=kLoop, calls=%fused_computation.141 | loop fusion | bytes 4194304 | tf_op jit(solution)/shard_map/slice | solution.py:112
  34.2 0.2 convolution_bitcast_fusion.4
  34.4 0.2 convolution_bitcast_fusion.5
  34.6 0.2 convolution_bitcast_fusion.6
  34.8 0.2 convolution_bitcast_fusion.7
  35.1 0.2 select_reduce_fusion
  35.3 0.4 fusion.12
  35.7 0.3 divide_convert_fusion
  36.0 0.3 copy-done.2
  36.3 0.2 convolution_bitcast_fusion.11
  36.5 0.2 convolution_bitcast_fusion.10
  36.6 0.2 convolution_bitcast_fusion.9
  36.8 0.2 convolution_bitcast_fusion.8
  37.0 0.2 convolution_bitcast_fusion.15
  37.1 0.2 convolution_bitcast_fusion.14
  37.3 0.2 convolution_bitcast_fusion.13
  37.5 0.2 convolution_bitcast_fusion.12
  37.8 6.4 %collective-permute-start.2 = (bf16[2,4096]{1,0:T(2,128)(2,1)S(1)}, bf16[2,4096]{1,0:T(2,128)(2,1)S(1)}, u32[]{:S(2)}, u32[]{:S(2)}) collective-permute-start(bf16[2,4096]{1,0:T(2,128)(2,1)S(1)} %get-tuple-element.22), channel_id=1, source_target_pairs={{0,1},{1,0},{2,3},{3,2},{4,5},{5,4},{6,7},{7,6},{8,9},{9,8},{10,11... | collective-permute-start | bytes 49160 | tf_op jit(solution)/shard_map/ppermute | solution.py:209
  44.4 0.9 collective-permute-done.2
  45.3 0.2 multiply_reduce_fusion.4
  45.5 0.1 multiply_convert_fusion.2
  45.6 2.0 %convolution_convert_fusion = bf16[4096,256]{1,0:T(8,128)(2,1)} fusion(s32[4096]{0:T(1024)S(1)} %eq.80, bf16[8,8,2,128]{3,2,1,0:T(2,128)(2,1)S(1)} %bitcast.246), kind=kOutput, calls=%fused_computation.6 | convolution fusion | flops 135528448 | bytes 2146304 | tf_op jit(solution)/shard_map/dot_general | solution.py:235
  47.6 48.1 %shard_map.163 = bf16[128,32,256]{2,1,0:T(8,128)(2,1)} custom-call(bf16[128,32,256]{2,1,0:T(8,128)(2,1)} %bitcast.213), custom_call_target="tpu_custom_call" | custom-call | tf_op jit(solution)/shard_map/pallas_call | solution.py:71
  95.8 1.9 %fusion.32 = (bf16[128,32,128]{2,1,0:T(8,128)(2,1)S(1)}, bf16[128,32,128]{2,1,0:T(8,128)(2,1)S(1)}) fusion(bf16[128,32,256]{2,1,0:T(8,128)(2,1)} %shard_map.163), kind=kLoop, calls=%fused_computation.139 | loop fusion | bytes 4194304 | tf_op jit(solution)/shard_map/slice | solution.py:242
  97.7 0.7 multiply_reduce_fusion
  98.4 0.7 multiply_reduce_fusion.2
  99.1 0.5 copy-done.9
  99.6 0.7 multiply_reduce_fusion.1
  100.4 0.7 multiply_reduce_fusion.3
  101.2 0.7 fusion
  101.9 0.2 slice_bitcast_fusion.1
  102.1 0.2 copy.68
  102.3 0.2 copy.69
  102.6 1.7 %pad_maximum_fusion.x_ref = bf16[128,32,256]{2,1,0:T(8,128)(2,1)} fusion(bf16[128,32,128]{2,1,0:T(8,128)(2,1)S(1)} %bitcast.234, bf16[128,32,128]{2,1,0:T(8,128)(2,1)S(1)} %bitcast.232), kind=kLoop, calls=%fused_computation.7 | loop fusion | flops 4194304 | bytes 4194304 | tf_op jit(solution)/shard_map/concatenate | solution.py:253
  104.2 38.4 %shard_map.164 = bf16[128,32,256]{2,1,0:T(8,128)(2,1)} custom-call(bf16[128,32,256]{2,1,0:T(8,128)(2,1)} %pad_maximum_fusion.x_ref), custom_call_target="tpu_custom_call" | custom-call | tf_op jit(solution)/shard_map/pallas_call | solution.py:71
  142.7 1.9 %fusion.31 = (bf16[128,32,128]{2,1,0:T(8,128)(2,1)S(1)}, bf16[128,32,128]{2,1,0:T(8,128)(2,1)S(1)}) fusion(bf16[128,32,256]{2,1,0:T(8,128)(2,1)} %shard_map.164), kind=kLoop, calls=%fused_computation.138 | loop fusion | bytes 4194304 | tf_op jit(solution)/shard_map/slice | solution.py:260
  144.6 0.3 fusion.7
  144.9 0.3 fusion.6
  145.2 0.7 fusion.20
  (59 shorter events, 1.8 us)
Async XLA Ops:
  0.0 97.7 %copy-start = (bf16[1,32,128,128]{3,2,1,0:T(8,128)(2,1)S(1)}, bf16[1,32,128,128]{3,2,1,0:T(8,128)(2,1)}, u32[]{:S(2)}) copy-start(bf16[1,32,128,128]{3,2,1,0:T(8,128)(2,1)} %param.27) | copy-start | bytes 3145732
  1.6 28.7 %collective-permute-start = (s32[4,17]{1,0:T(4,128)S(1)}, s32[4,17]{1,0:T(4,128)S(1)}, u32[]{:S(2)}, u32[]{:S(2)}) collective-permute-start(s32[4,17]{1,0:T(4,128)S(1)} %pad_add_fusion), channel_id=1, source_target_pairs={{0,2},{2,4},{4,6},{6,8},{8,10},{10,12},{12,14},{14,16},{16,18},{18... | collective-permute-start | bytes 824 | tf_op jit(solution)/shard_map/ppermute | solution.py:88
  6.5 26.0 %collective-permute-start.1 = (bf16[2,64,16,512]{3,2,1,0:T(8,128)(2,1)}, bf16[2,64,16,512]{3,2,1,0:T(8,128)(2,1)}, u32[]{:S(2)}, u32[]{:S(2)}) collective-permute-start(bf16[2,64,16,512]{3,2,1,0:T(8,128)(2,1)} %param.20), channel_id=1, source_target_pairs={{0,2},{2,4},{4,6},{6,8},{8,10},{10,12},{12,14},{14,16},{16,18},{18... | collective-permute-start | bytes 6291464 | tf_op jit(solution)/shard_map/ppermute | solution.py:88
  9.9 34.3 %all-to-all-start = ((s32[128,1,64]{2,1,0:T(1,128)}), s32[128,1,64]{2,1,0:T(1,128)S(1)}, u32[]{:S(2)}, u32[]{:S(2)}) async-start(s32[128,1,64]{2,1,0:T(1,128)} %broadcast_in_dim.102), calls=%async_computation | async-start | bytes 131072 | tf_op jit(solution)/shard_map/all_to_all | solution.py:221
  23.5 2.7 %copy-start.4 = (bf16[4,4096]{1,0:T(4,128)(2,1)S(1)}, bf16[4,4096]{1,0:T(4,128)(2,1)}, u32[]{:S(2)}) copy-start(bf16[4,4096]{1,0:T(4,128)(2,1)} %param.17) | copy-start | bytes 98308
  23.5 3.6 %copy-start.1 = (s32[4]{0:T(128)S(1)}, s32[4]{0:T(128)}, u32[]{:S(2)}) copy-start(s32[4]{0:T(128)} %param.22) | copy-start | bytes 52
  26.2 2.0 %copy-start.6 = (bf16[4,512]{1,0:T(4,128)(2,1)S(1)}, bf16[4,512]{1,0:T(4,128)(2,1)}, u32[]{:S(2)}) copy-start(bf16[4,512]{1,0:T(4,128)(2,1)} %param.18) | copy-start | bytes 12292
  26.2 2.1 %copy-start.7 = (bf16[4,512]{1,0:T(4,128)(2,1)S(1)}, bf16[4,512]{1,0:T(4,128)(2,1)}, u32[]{:S(2)}) copy-start(bf16[4,512]{1,0:T(4,128)(2,1)} %param.19) | copy-start | bytes 12292
  26.2 2.1 %copy-start.8 = (f32[1,32]{1,0:T(1,128)S(1)}, f32[1,32]{1,0:T(1,128)}, u32[]{:S(2)}) copy-start(f32[1,32]{1,0:T(1,128)} %param.33) | copy-start | bytes 388
  35.1 1.2 copy-start.2
  36.0 9.3 %copy-start.3 = (bf16[2,8192]{1,0:T(2,128)(2,1)S(1)}, bf16[2,8192]{1,0:T(2,128)(2,1)}, u32[]{:S(2)}) copy-start(bf16[2,8192]{1,0:T(2,128)(2,1)} %param.24) | copy-start | bytes 98308
  36.0 9.5 %copy-start.5 = (f32[8192]{0:T(1024)S(1)}, f32[8192]{0:T(1024)}, u32[]{:S(2)}) copy-start(f32[8192]{0:T(1024)} %param.25) | copy-start | bytes 98308
  37.8 7.5 %collective-permute-start.2 = (bf16[2,4096]{1,0:T(2,128)(2,1)S(1)}, bf16[2,4096]{1,0:T(2,128)(2,1)S(1)}, u32[]{:S(2)}, u32[]{:S(2)}) collective-permute-start(bf16[2,4096]{1,0:T(2,128)(2,1)S(1)} %get-tuple-element.22), channel_id=1, source_target_pairs={{0,1},{1,0},{2,3},{3,2},{4,5},{5,4},{6,7},{7,6},{8,9},{9,8},{10,11... | collective-permute-start | bytes 49160 | tf_op jit(solution)/shard_map/ppermute | solution.py:209
  95.8 1.9 %copy-start.10 = (f32[1,32]{1,0:T(1,128)S(1)}, f32[1,32]{1,0:T(1,128)}, u32[]{:S(2)}) copy-start(f32[1,32]{1,0:T(1,128)} %param.30) | copy-start | bytes 388
  98.4 1.2 copy-start.9
  98.4 1.2 copy-start.11

commit v12 on v11

--- a/solution.py
+++ b/solution.py
@@ -67,7 +67,7 @@
     local.wait()
 
 
-def exchange(x, route, lanes, ways=8):
+def exchange(x, route, lanes, ways=32):
     return pl.pallas_call(
         functools.partial(exchange_kernel, route, lanes),
         out_shape=jax.ShapeDtypeStruct(x.shape, x.dtype),

time: 146 us -> 153 us (1.048); the launches traced: 146 us -> 151 us
  Pallas kernels: 86.5 us -> 91.8 us
    pallas_call x2, Pallas kernels: 86.5 us -> 91.8 us  [exchange(): pl.pallas_call(functools.partial(exchange_kernel, route, lanes), out_shap...]
where the time goes in v12:
time: 153 us; the launch traced here: 151 us
  Pallas kernels  91.8 us (60%)
  starting transfers between devices  24.7 us (16%)
  local copies, waits for them, and re-layouts  17.5 us (11%)
  matrix products  9.13 us (6%)
  other arithmetic  6.69 us (4%)
    pallas_call x2, Pallas kernels, exchange(): pl.pallas_call(functools.partial(exchange_kernel, route, lanes), out_shap...  91.8 us
    all_to_all x1, starting transfers between devices, per_device(): lax.all_to_all(jnp.broadcast_to(own_lists, (peers, own_lists.shape[1])),...  11.5 us
    ppermute x2, starting transfers between devices, shifted(): return lax.ppermute(block, axis, route)  6.85 us
    ppermute x1, starting transfers between devices, per_device(): arrived_half = lax.ppermute(theirs, 'head', [(0, 1), (1, 0)])  6.35 us
    unnamed x30, local copies, waits for them, and re-layouts  3.16 us
  transfers between devices with their start and end apart: 4, of which 1 were waited for; matrix products, arithmetic and copies ran while one was open for 12% of the time, Pallas kernels for 0%

profile of v12, /device:TPU:1, one launch (start us, length us, event | category | flops | bytes accessed | tf_op | source)
XLA Modules:
  0.0 151.2 jit_solution(5602856952818789320)
XLA Ops:
  0.0 0.8 copy.46
  0.8 0.8 pad_add_fusion
  1.6 4.9 %collective-permute-start = (s32[4,17]{1,0:T(4,128)S(1)}, s32[4,17]{1,0:T(4,128)S(1)}, u32[]{:S(2)}, u32[]{:S(2)}) collective-permute-start(s32[4,17]{1,0:T(4,128)S(1)} %pad_add_fusion), channel_id=1, source_target_pairs={{0,2},{2,4},{4,6},{6,8},{8,10},{10,12},{12,14},{14,16},{16,18},{18... | collective-permute-start | bytes 824 | tf_op jit(solution)/shard_map/ppermute | solution.py:88
  6.5 1.9 %collective-permute-start.1 = (bf16[2,64,16,512]{3,2,1,0:T(8,128)(2,1)}, bf16[2,64,16,512]{3,2,1,0:T(8,128)(2,1)}, u32[]{:S(2)}, u32[]{:S(2)}) collective-permute-start(bf16[2,64,16,512]{3,2,1,0:T(8,128)(2,1)} %param.20), channel_id=1, source_target_pairs={{0,2},{2,4},{4,6},{6,8},{8,10},{10,12},{12,14},{14,16},{16,18},{18... | collective-permute-start | bytes 6291464 | tf_op jit(solution)/shard_map/ppermute | solution.py:88
  8.5 0.7 add_bitcast_fusion.1
  9.2 0.7 broadcast_in_dim.102
  9.9 11.5 %all-to-all-start = ((s32[128,1,64]{2,1,0:T(1,128)}), s32[128,1,64]{2,1,0:T(1,128)S(1)}, u32[]{:S(2)}, u32[]{:S(2)}) async-start(s32[128,1,64]{2,1,0:T(1,128)} %broadcast_in_dim.102), calls=%async_computation | async-start | bytes 131072 | tf_op jit(solution)/shard_map/all_to_all | solution.py:221
  21.3 0.7 broadcast_compare_fusion.1
  22.0 1.2 gather_fusion.2
  23.5 2.7 %fusion.33 = (bf16[1,64,16,512]{3,2,1,0:T(8,128)(2,1)}, bf16[1,64,16,512]{3,2,1,0:T(8,128)(2,1)S(1)}) fusion(bf16[2,64,16,512]{3,2,1,0:T(8,128)(2,1)} %param.20), kind=kLoop, calls=%fused_computation.140 | loop fusion | bytes 4194304 | tf_op jit(solution)/shard_map/slice | solution.py:143
  26.2 0.2 convolution_bitcast_fusion
  26.4 0.2 convolution_bitcast_fusion.1
  26.6 0.2 convolution_bitcast_fusion.2
  26.9 0.2 convolution_bitcast_fusion.3
  27.1 0.6 gather_fusion.3
  27.9 0.1 and.80
  28.1 0.1 add.100
  28.4 0.1 fusion.36
  28.6 1.6 %copy.58 = bf16[1,32,128,128]{2,3,1,0:T(8,128)(2,1)S(1)} copy(bf16[1,32,128,128]{3,2,1,0:T(8,128)(2,1)} %param.31) | data formatting | bytes 2097152 | tf_op args[14]
  30.3 0.6 gather_fusion
  31.0 0.1 and.74
  31.1 0.1 and.75
  31.4 0.1 add.97
  31.6 0.2 slice_reduce_fusion
  31.7 0.6 gather_fusion.1
  32.5 1.7 %fusion.34 = (bf16[1,64,16,512]{3,2,1,0:T(8,128)(2,1)S(1)}, bf16[1,64,16,512]{3,2,1,0:T(8,128)(2,1)S(1)}) fusion(bf16[2,64,16,512]{3,2,1,0:T(8,128)(2,1)} %collective-permute-done.1), kind=kLoop, calls=%fused_computation.141 | loop fusion | bytes 4194304 | tf_op jit(solution)/shard_map/slice | solution.py:112
  34.2 0.2 convolution_bitcast_fusion.4
  34.4 0.2 convolution_bitcast_fusion.5
  34.6 0.2 convolution_bitcast_fusion.6
  34.8 0.2 convolution_bitcast_fusion.7
  35.1 0.2 select_reduce_fusion
  35.3 0.4 fusion.12
  35.7 0.3 divide_convert_fusion
  36.0 0.3 copy-done.2
  36.3 0.2 convolution_bitcast_fusion.11
  36.5 0.2 convolution_bitcast_fusion.10
  36.6 0.2 convolution_bitcast_fusion.9
  36.8 0.2 convolution_bitcast_fusion.8
  37.0 0.2 convolution_bitcast_fusion.15
  37.1 0.2 convolution_bitcast_fusion.14
  37.3 0.2 convolution_bitcast_fusion.13
  37.5 0.2 convolution_bitcast_fusion.12
  37.8 6.4 %collective-permute-start.2 = (bf16[2,4096]{1,0:T(2,128)(2,1)S(1)}, bf16[2,4096]{1,0:T(2,128)(2,1)S(1)}, u32[]{:S(2)}, u32[]{:S(2)}) collective-permute-start(bf16[2,4096]{1,0:T(2,128)(2,1)S(1)} %get-tuple-element.22), channel_id=1, source_target_pairs={{0,1},{1,0},{2,3},{3,2},{4,5},{5,4},{6,7},{7,6},{8,9},{9,8},{10,11... | collective-permute-start | bytes 49160 | tf_op jit(solution)/shard_map/ppermute | solution.py:209
  44.4 0.9 collective-permute-done.2
  45.3 0.2 multiply_reduce_fusion.4
  45.5 0.1 multiply_convert_fusion.2
  45.6 2.0 %convolution_convert_fusion = bf16[4096,256]{1,0:T(8,128)(2,1)} fusion(s32[4096]{0:T(1024)S(1)} %eq.80, bf16[8,8,2,128]{3,2,1,0:T(2,128)(2,1)S(1)} %bitcast.246), kind=kOutput, calls=%fused_computation.6 | convolution fusion | flops 135528448 | bytes 2146304 | tf_op jit(solution)/shard_map/dot_general | solution.py:235
  47.6 50.3 %shard_map.163 = bf16[128,32,256]{2,1,0:T(8,128)(2,1)} custom-call(bf16[128,32,256]{2,1,0:T(8,128)(2,1)} %bitcast.213), custom_call_target="tpu_custom_call" | custom-call | tf_op jit(solution)/shard_map/pallas_call | solution.py:71
  98.0 1.9 %fusion.32 = (bf16[128,32,128]{2,1,0:T(8,128)(2,1)S(1)}, bf16[128,32,128]{2,1,0:T(8,128)(2,1)S(1)}) fusion(bf16[128,32,256]{2,1,0:T(8,128)(2,1)} %shard_map.163), kind=kLoop, calls=%fused_computation.139 | loop fusion | bytes 4194304 | tf_op jit(solution)/shard_map/slice | solution.py:242
  99.9 0.7 multiply_reduce_fusion
  100.7 0.7 multiply_reduce_fusion.2
  101.4 0.5 copy-done.9
  101.9 0.7 multiply_reduce_fusion.1
  102.6 0.7 multiply_reduce_fusion.3
  103.4 0.7 fusion
  104.1 0.2 slice_bitcast_fusion.1
  104.3 0.2 copy.68
  104.5 0.2 copy.69
  104.8 1.7 %pad_maximum_fusion.x_ref = bf16[128,32,256]{2,1,0:T(8,128)(2,1)} fusion(bf16[128,32,128]{2,1,0:T(8,128)(2,1)S(1)} %bitcast.234, bf16[128,32,128]{2,1,0:T(8,128)(2,1)S(1)} %bitcast.232), kind=kLoop, calls=%fused_computation.7 | loop fusion | flops 4194304 | bytes 4194304 | tf_op jit(solution)/shard_map/concatenate | solution.py:253
  106.5 41.5 %shard_map.164 = bf16[128,32,256]{2,1,0:T(8,128)(2,1)} custom-call(bf16[128,32,256]{2,1,0:T(8,128)(2,1)} %pad_maximum_fusion.x_ref), custom_call_target="tpu_custom_call" | custom-call | tf_op jit(solution)/shard_map/pallas_call | solution.py:71
  148.0 1.9 %fusion.31 = (bf16[128,32,128]{2,1,0:T(8,128)(2,1)S(1)}, bf16[128,32,128]{2,1,0:T(8,128)(2,1)S(1)}) fusion(bf16[128,32,256]{2,1,0:T(8,128)(2,1)} %shard_map.164), kind=kLoop, calls=%fused_computation.138 | loop fusion | bytes 4194304 | tf_op jit(solution)/shard_map/slice | solution.py:260
  149.9 0.3 fusion.7
  150.2 0.3 fusion.6
  150.5 0.7 fusion.20
  (59 shorter events, 1.8 us)
Async XLA Ops:
  0.0 99.9 %copy-start = (bf16[1,32,128,128]{3,2,1,0:T(8,128)(2,1)S(1)}, bf16[1,32,128,128]{3,2,1,0:T(8,128)(2,1)}, u32[]{:S(2)}) copy-start(bf16[1,32,128,128]{3,2,1,0:T(8,128)(2,1)} %param.27) | copy-start | bytes 3145732
  1.6 28.7 %collective-permute-start = (s32[4,17]{1,0:T(4,128)S(1)}, s32[4,17]{1,0:T(4,128)S(1)}, u32[]{:S(2)}, u32[]{:S(2)}) collective-permute-start(s32[4,17]{1,0:T(4,128)S(1)} %pad_add_fusion), channel_id=1, source_target_pairs={{0,2},{2,4},{4,6},{6,8},{8,10},{10,12},{12,14},{14,16},{16,18},{18... | collective-permute-start | bytes 824 | tf_op jit(solution)/shard_map/ppermute | solution.py:88
  6.5 26.0 %collective-permute-start.1 = (bf16[2,64,16,512]{3,2,1,0:T(8,128)(2,1)}, bf16[2,64,16,512]{3,2,1,0:T(8,128)(2,1)}, u32[]{:S(2)}, u32[]{:S(2)}) collective-permute-start(bf16[2,64,16,512]{3,2,1,0:T(8,128)(2,1)} %param.20), channel_id=1, source_target_pairs={{0,2},{2,4},{4,6},{6,8},{8,10},{10,12},{12,14},{14,16},{16,18},{18... | collective-permute-start | bytes 6291464 | tf_op jit(solution)/shard_map/ppermute | solution.py:88
  9.9 34.3 %all-to-all-start = ((s32[128,1,64]{2,1,0:T(1,128)}), s32[128,1,64]{2,1,0:T(1,128)S(1)}, u32[]{:S(2)}, u32[]{:S(2)}) async-start(s32[128,1,64]{2,1,0:T(1,128)} %broadcast_in_dim.102), calls=%async_computation | async-start | bytes 131072 | tf_op jit(solution)/shard_map/all_to_all | solution.py:221
  23.5 2.7 %copy-start.4 = (bf16[4,4096]{1,0:T(4,128)(2,1)S(1)}, bf16[4,4096]{1,0:T(4,128)(2,1)}, u32[]{:S(2)}) copy-start(bf16[4,4096]{1,0:T(4,128)(2,1)} %param.17) | copy-start | bytes 98308
  23.5 3.6 %copy-start.1 = (s32[4]{0:T(128)S(1)}, s32[4]{0:T(128)}, u32[]{:S(2)}) copy-start(s32[4]{0:T(128)} %param.22) | copy-start | bytes 52
  26.2 2.0 %copy-start.6 = (bf16[4,512]{1,0:T(4,128)(2,1)S(1)}, bf16[4,512]{1,0:T(4,128)(2,1)}, u32[]{:S(2)}) copy-start(bf16[4,512]{1,0:T(4,128)(2,1)} %param.18) | copy-start | bytes 12292
  26.2 2.1 %copy-start.7 = (bf16[4,512]{1,0:T(4,128)(2,1)S(1)}, bf16[4,512]{1,0:T(4,128)(2,1)}, u32[]{:S(2)}) copy-start(bf16[4,512]{1,0:T(4,128)(2,1)} %param.19) | copy-start | bytes 12292
  26.2 2.1 %copy-start.8 = (f32[1,32]{1,0:T(1,128)S(1)}, f32[1,32]{1,0:T(1,128)}, u32[]{:S(2)}) copy-start(f32[1,32]{1,0:T(1,128)} %param.33) | copy-start | bytes 388
  35.1 1.2 copy-start.2
  36.0 9.3 %copy-start.3 = (bf16[2,8192]{1,0:T(2,128)(2,1)S(1)}, bf16[2,8192]{1,0:T(2,128)(2,1)}, u32[]{:S(2)}) copy-start(bf16[2,8192]{1,0:T(2,128)(2,1)} %param.24) | copy-start | bytes 98308
  36.0 9.5 %copy-start.5 = (f32[8192]{0:T(1024)S(1)}, f32[8192]{0:T(1024)}, u32[]{:S(2)}) copy-start(f32[8192]{0:T(1024)} %param.25) | copy-start | bytes 98308
  37.8 7.5 %collective-permute-start.2 = (bf16[2,4096]{1,0:T(2,128)(2,1)S(1)}, bf16[2,4096]{1,0:T(2,128)(2,1)S(1)}, u32[]{:S(2)}, u32[]{:S(2)}) collective-permute-start(bf16[2,4096]{1,0:T(2,128)(2,1)S(1)} %get-tuple-element.22), channel_id=1, source_target_pairs={{0,1},{1,0},{2,3},{3,2},{4,5},{5,4},{6,7},{7,6},{8,9},{9,8},{10,11... | collective-permute-start | bytes 49160 | tf_op jit(solution)/shard_map/ppermute | solution.py:209
  98.0 1.9 %copy-start.10 = (f32[1,32]{1,0:T(1,128)S(1)}, f32[1,32]{1,0:T(1,128)}, u32[]{:S(2)}) copy-start(f32[1,32]{1,0:T(1,128)} %param.30) | copy-start | bytes 388
  100.6 1.2 copy-start.9
  100.6 1.2 copy-start.11

commit v13 on v12

--- a/solution.py
+++ b/solution.py
@@ -67,7 +67,7 @@
     local.wait()
 
 
-def exchange(x, route, lanes, ways=32):
+def exchange(x, route, lanes, ways=4):
     return pl.pallas_call(
         functools.partial(exchange_kernel, route, lanes),
         out_shape=jax.ShapeDtypeStruct(x.shape, x.dtype),

time: 153 us -> 146 us (0.954)
  Pallas kernels: 91.8 us -> 85.6 us
    pallas_call x2, Pallas kernels: 91.8 us -> 85.6 us  [exchange(): pl.pallas_call(functools.partial(exchange_kernel, route, lanes), out_shap...]
where the time goes in v13:
time: 146 us; the launch traced here: 145 us
  Pallas kernels  85.6 us (59%)
  starting transfers between devices  24.7 us (17%)
  local copies, waits for them, and re-layouts  17.5 us (12%)
  matrix products  9.12 us (6%)
  other arithmetic  6.69 us (5%)
    pallas_call x2, Pallas kernels, exchange(): pl.pallas_call(functools.partial(exchange_kernel, route, lanes), out_shap...  85.6 us
    all_to_all x1, starting transfers between devices, per_device(): lax.all_to_all(jnp.broadcast_to(own_lists, (peers, own_lists.shape[1])),...  11.5 us
    ppermute x2, starting transfers between devices, shifted(): return lax.ppermute(block, axis, route)  6.85 us
    ppermute x1, starting transfers between devices, per_device(): arrived_half = lax.ppermute(theirs, 'head', [(0, 1), (1, 0)])  6.35 us
    unnamed x30, local copies, waits for them, and re-layouts  3.16 us
  transfers between devices with their start and end apart: 4, of which 1 were waited for; matrix products, arithmetic and copies ran while one was open for 12% of the time, Pallas kernels for 0%

profile of v13, /device:TPU:1, one launch (start us, length us, event | category | flops | bytes accessed | tf_op | source)
XLA Modules:
  0.0 144.9 jit_solution(10946637972563915976)
XLA Ops:
  0.0 0.8 copy.46
  0.8 0.8 pad_add_fusion
  1.6 4.9 %collective-permute-start = (s32[4,17]{1,0:T(4,128)S(1)}, s32[4,17]{1,0:T(4,128)S(1)}, u32[]{:S(2)}, u32[]{:S(2)}) collective-permute-start(s32[4,17]{1,0:T(4,128)S(1)} %pad_add_fusion), channel_id=1, source_target_pairs={{0,2},{2,4},{4,6},{6,8},{8,10},{10,12},{12,14},{14,16},{16,18},{18... | collective-permute-start | bytes 824 | tf_op jit(solution)/shard_map/ppermute | solution.py:88
  6.5 1.9 %collective-permute-start.1 = (bf16[2,64,16,512]{3,2,1,0:T(8,128)(2,1)}, bf16[2,64,16,512]{3,2,1,0:T(8,128)(2,1)}, u32[]{:S(2)}, u32[]{:S(2)}) collective-permute-start(bf16[2,64,16,512]{3,2,1,0:T(8,128)(2,1)} %param.20), channel_id=1, source_target_pairs={{0,2},{2,4},{4,6},{6,8},{8,10},{10,12},{12,14},{14,16},{16,18},{18... | collective-permute-start | bytes 6291464 | tf_op jit(solution)/shard_map/ppermute | solution.py:88
  8.5 0.7 add_bitcast_fusion.1
  9.2 0.7 broadcast_in_dim.102
  9.9 11.5 %all-to-all-start = ((s32[128,1,64]{2,1,0:T(1,128)}), s32[128,1,64]{2,1,0:T(1,128)S(1)}, u32[]{:S(2)}, u32[]{:S(2)}) async-start(s32[128,1,64]{2,1,0:T(1,128)} %broadcast_in_dim.102), calls=%async_computation | async-start | bytes 131072 | tf_op jit(solution)/shard_map/all_to_all | solution.py:221
  21.3 0.7 broadcast_compare_fusion.1
  22.0 1.2 gather_fusion.2
  23.5 2.7 %fusion.33 = (bf16[1,64,16,512]{3,2,1,0:T(8,128)(2,1)}, bf16[1,64,16,512]{3,2,1,0:T(8,128)(2,1)S(1)}) fusion(bf16[2,64,16,512]{3,2,1,0:T(8,128)(2,1)} %param.20), kind=kLoop, calls=%fused_computation.140 | loop fusion | bytes 4194304 | tf_op jit(solution)/shard_map/slice | solution.py:143
  26.2 0.2 convolution_bitcast_fusion
  26.4 0.2 convolution_bitcast_fusion.1
  26.6 0.2 convolution_bitcast_fusion.2
  26.9 0.2 convolution_bitcast_fusion.3
  27.1 0.6 gather_fusion.3
  27.9 0.1 and.80
  28.1 0.1 add.100
  28.4 0.1 fusion.36
  28.6 1.6 %copy.58 = bf16[1,32,128,128]{2,3,1,0:T(8,128)(2,1)S(1)} copy(bf16[1,32,128,128]{3,2,1,0:T(8,128)(2,1)} %param.31) | data formatting | bytes 2097152 | tf_op args[14]
  30.3 0.6 gather_fusion
  31.0 0.1 and.74
  31.1 0.1 and.75
  31.4 0.1 add.97
  31.6 0.2 slice_reduce_fusion
  31.7 0.6 gather_fusion.1
  32.5 1.7 %fusion.34 = (bf16[1,64,16,512]{3,2,1,0:T(8,128)(2,1)S(1)}, bf16[1,64,16,512]{3,2,1,0:T(8,128)(2,1)S(1)}) fusion(bf16[2,64,16,512]{3,2,1,0:T(8,128)(2,1)} %collective-permute-done.1), kind=kLoop, calls=%fused_computation.141 | loop fusion | bytes 4194304 | tf_op jit(solution)/shard_map/slice | solution.py:112
  34.2 0.2 convolution_bitcast_fusion.4
  34.4 0.2 convolution_bitcast_fusion.5
  34.6 0.2 convolution_bitcast_fusion.6
  34.8 0.2 convolution_bitcast_fusion.7
  35.1 0.2 select_reduce_fusion
  35.3 0.4 fusion.12
  35.7 0.3 divide_convert_fusion
  36.0 0.3 copy-done.2
  36.3 0.2 convolution_bitcast_fusion.11
  36.5 0.2 convolution_bitcast_fusion.10
  36.6 0.2 convolution_bitcast_fusion.9
  36.8 0.2 convolution_bitcast_fusion.8
  37.0 0.2 convolution_bitcast_fusion.15
  37.1 0.2 convolution_bitcast_fusion.14
  37.3 0.2 convolution_bitcast_fusion.13
  37.5 0.2 convolution_bitcast_fusion.12
  37.8 6.4 %collective-permute-start.2 = (bf16[2,4096]{1,0:T(2,128)(2,1)S(1)}, bf16[2,4096]{1,0:T(2,128)(2,1)S(1)}, u32[]{:S(2)}, u32[]{:S(2)}) collective-permute-start(bf16[2,4096]{1,0:T(2,128)(2,1)S(1)} %get-tuple-element.22), channel_id=1, source_target_pairs={{0,1},{1,0},{2,3},{3,2},{4,5},{5,4},{6,7},{7,6},{8,9},{9,8},{10,11... | collective-permute-start | bytes 49160 | tf_op jit(solution)/shard_map/ppermute | solution.py:209
  44.4 0.9 collective-permute-done.2
  45.3 0.2 multiply_reduce_fusion.4
  45.5 0.1 multiply_convert_fusion.2
  45.6 2.0 %convolution_convert_fusion = bf16[4096,256]{1,0:T(8,128)(2,1)} fusion(s32[4096]{0:T(1024)S(1)} %eq.80, bf16[8,8,2,128]{3,2,1,0:T(2,128)(2,1)S(1)} %bitcast.246), kind=kOutput, calls=%fused_computation.6 | convolution fusion | flops 135528448 | bytes 2146304 | tf_op jit(solution)/shard_map/dot_general | solution.py:235
  47.6 45.7 %shard_map.163 = bf16[128,32,256]{2,1,0:T(8,128)(2,1)} custom-call(bf16[128,32,256]{2,1,0:T(8,128)(2,1)} %bitcast.213), custom_call_target="tpu_custom_call" | custom-call | tf_op jit(solution)/shard_map/pallas_call | solution.py:71
  93.4 1.9 %fusion.32 = (bf16[128,32,128]{2,1,0:T(8,128)(2,1)S(1)}, bf16[128,32,128]{2,1,0:T(8,128)(2,1)S(1)}) fusion(bf16[128,32,256]{2,1,0:T(8,128)(2,1)} %shard_map.163), kind=kLoop, calls=%fused_computation.139 | loop fusion | bytes 4194304 | tf_op jit(solution)/shard_map/slice | solution.py:242
  95.3 0.7 multiply_reduce_fusion
  96.1 0.7 multiply_reduce_fusion.2
  96.8 0.5 copy-done.9
  97.3 0.7 multiply_reduce_fusion.1
  98.0 0.7 multiply_reduce_fusion.3
  98.8 0.7 fusion
  99.5 0.2 slice_bitcast_fusion.1
  99.7 0.2 copy.68
  99.9 0.2 copy.69
  100.2 1.7 %pad_maximum_fusion.x_ref = bf16[128,32,256]{2,1,0:T(8,128)(2,1)} fusion(bf16[128,32,128]{2,1,0:T(8,128)(2,1)S(1)} %bitcast.234, bf16[128,32,128]{2,1,0:T(8,128)(2,1)S(1)} %bitcast.232), kind=kLoop, calls=%fused_computation.7 | loop fusion | flops 4194304 | bytes 4194304 | tf_op jit(solution)/shard_map/concatenate | solution.py:253
  101.9 39.8 %shard_map.164 = bf16[128,32,256]{2,1,0:T(8,128)(2,1)} custom-call(bf16[128,32,256]{2,1,0:T(8,128)(2,1)} %pad_maximum_fusion.x_ref), custom_call_target="tpu_custom_call" | custom-call | tf_op jit(solution)/shard_map/pallas_call | solution.py:71
  141.7 1.9 %fusion.31 = (bf16[128,32,128]{2,1,0:T(8,128)(2,1)S(1)}, bf16[128,32,128]{2,1,0:T(8,128)(2,1)S(1)}) fusion(bf16[128,32,256]{2,1,0:T(8,128)(2,1)} %shard_map.164), kind=kLoop, calls=%fused_computation.138 | loop fusion | bytes 4194304 | tf_op jit(solution)/shard_map/slice | solution.py:260
  143.6 0.3 fusion.7
  143.9 0.3 fusion.6
  144.2 0.7 fusion.20
  (59 shorter events, 1.8 us)
Async XLA Ops:
  0.0 95.3 %copy-start = (bf16[1,32,128,128]{3,2,1,0:T(8,128)(2,1)S(1)}, bf16[1,32,128,128]{3,2,1,0:T(8,128)(2,1)}, u32[]{:S(2)}) copy-start(bf16[1,32,128,128]{3,2,1,0:T(8,128)(2,1)} %param.27) | copy-start | bytes 3145732
  1.6 28.7 %collective-permute-start = (s32[4,17]{1,0:T(4,128)S(1)}, s32[4,17]{1,0:T(4,128)S(1)}, u32[]{:S(2)}, u32[]{:S(2)}) collective-permute-start(s32[4,17]{1,0:T(4,128)S(1)} %pad_add_fusion), channel_id=1, source_target_pairs={{0,2},{2,4},{4,6},{6,8},{8,10},{10,12},{12,14},{14,16},{16,18},{18... | collective-permute-start | bytes 824 | tf_op jit(solution)/shard_map/ppermute | solution.py:88
  6.5 26.0 %collective-permute-start.1 = (bf16[2,64,16,512]{3,2,1,0:T(8,128)(2,1)}, bf16[2,64,16,512]{3,2,1,0:T(8,128)(2,1)}, u32[]{:S(2)}, u32[]{:S(2)}) collective-permute-start(bf16[2,64,16,512]{3,2,1,0:T(8,128)(2,1)} %param.20), channel_id=1, source_target_pairs={{0,2},{2,4},{4,6},{6,8},{8,10},{10,12},{12,14},{14,16},{16,18},{18... | collective-permute-start | bytes 6291464 | tf_op jit(solution)/shard_map/ppermute | solution.py:88
  9.9 34.3 %all-to-all-start = ((s32[128,1,64]{2,1,0:T(1,128)}), s32[128,1,64]{2,1,0:T(1,128)S(1)}, u32[]{:S(2)}, u32[]{:S(2)}) async-start(s32[128,1,64]{2,1,0:T(1,128)} %broadcast_in_dim.102), calls=%async_computation | async-start | bytes 131072 | tf_op jit(solution)/shard_map/all_to_all | solution.py:221
  23.5 2.7 %copy-start.4 = (bf16[4,4096]{1,0:T(4,128)(2,1)S(1)}, bf16[4,4096]{1,0:T(4,128)(2,1)}, u32[]{:S(2)}) copy-start(bf16[4,4096]{1,0:T(4,128)(2,1)} %param.17) | copy-start | bytes 98308
  23.5 3.6 %copy-start.1 = (s32[4]{0:T(128)S(1)}, s32[4]{0:T(128)}, u32[]{:S(2)}) copy-start(s32[4]{0:T(128)} %param.22) | copy-start | bytes 52
  26.2 2.0 %copy-start.6 = (bf16[4,512]{1,0:T(4,128)(2,1)S(1)}, bf16[4,512]{1,0:T(4,128)(2,1)}, u32[]{:S(2)}) copy-start(bf16[4,512]{1,0:T(4,128)(2,1)} %param.18) | copy-start | bytes 12292
  26.2 2.1 %copy-start.7 = (bf16[4,512]{1,0:T(4,128)(2,1)S(1)}, bf16[4,512]{1,0:T(4,128)(2,1)}, u32[]{:S(2)}) copy-start(bf16[4,512]{1,0:T(4,128)(2,1)} %param.19) | copy-start | bytes 12292
  26.2 2.1 %copy-start.8 = (f32[1,32]{1,0:T(1,128)S(1)}, f32[1,32]{1,0:T(1,128)}, u32[]{:S(2)}) copy-start(f32[1,32]{1,0:T(1,128)} %param.33) | copy-start | bytes 388
  35.1 1.2 copy-start.2
  36.0 9.3 %copy-start.3 = (bf16[2,8192]{1,0:T(2,128)(2,1)S(1)}, bf16[2,8192]{1,0:T(2,128)(2,1)}, u32[]{:S(2)}) copy-start(bf16[2,8192]{1,0:T(2,128)(2,1)} %param.24) | copy-start | bytes 98308
  36.0 9.5 %copy-start.5 = (f32[8192]{0:T(1024)S(1)}, f32[8192]{0:T(1024)}, u32[]{:S(2)}) copy-start(f32[8192]{0:T(1024)} %param.25) | copy-start | bytes 98308
  37.8 7.5 %collective-permute-start.2 = (bf16[2,4096]{1,0:T(2,128)(2,1)S(1)}, bf16[2,4096]{1,0:T(2,128)(2,1)S(1)}, u32[]{:S(2)}, u32[]{:S(2)}) collective-permute-start(bf16[2,4096]{1,0:T(2,128)(2,1)S(1)} %get-tuple-element.22), channel_id=1, source_target_pairs={{0,1},{1,0},{2,3},{3,2},{4,5},{5,4},{6,7},{7,6},{8,9},{9,8},{10,11... | collective-permute-start | bytes 49160 | tf_op jit(solution)/shard_map/ppermute | solution.py:209
  93.4 1.9 %copy-start.10 = (f32[1,32]{1,0:T(1,128)S(1)}, f32[1,32]{1,0:T(1,128)}, u32[]{:S(2)}) copy-start(f32[1,32]{1,0:T(1,128)} %param.30) | copy-start | bytes 388
  96.0 1.2 copy-start.9
  96.0 1.2 copy-start.11

commit v14 on v11

--- a/solution.py
+++ b/solution.py
@@ -71,8 +71,8 @@
     return pl.pallas_call(
         functools.partial(exchange_kernel, route, lanes),
         out_shape=jax.ShapeDtypeStruct(x.shape, x.dtype),
-        in_specs=[pl.BlockSpec(memory_space=pl.ANY)],
-        out_specs=pl.BlockSpec(memory_space=pl.ANY),
+        in_specs=[pl.BlockSpec(memory_space=pltpu.VMEM)],
+        out_specs=pl.BlockSpec(memory_space=pltpu.VMEM),
         scratch_shapes=[
             pltpu.SemaphoreType.DMA((ways,)),
             pltpu.SemaphoreType.DMA((ways,)),

time: 146 us -> 152 us (1.041)
  Pallas kernels: 86.5 us -> 92.4 us
    pallas_call x2, Pallas kernels: 86.5 us -> 92.4 us  [exchange(): pl.pallas_call(functools.partial(exchange_kernel, route, lanes), out_shap...]
  transfers between devices with their start and end apart: 4 -> 4, of which waited for: 1 -> 1; matrix products, arithmetic and copies ran while one was open for 12% -> 11% of each run, Pallas kernels for 0% -> 0%
where the time goes in v14:
time: 152 us
  Pallas kernels  92.4 us (61%)
  starting transfers between devices  24.7 us (16%)
  local copies, waits for them, and re-layouts  17.5 us (12%)
  matrix products  9.12 us (6%)
  other arithmetic  6.69 us (4%)
    pallas_call x2, Pallas kernels, exchange(): pl.pallas_call(functools.partial(exchange_kernel, route, lanes), out_shap...  92.4 us
    all_to_all x1, starting transfers between devices, per_device(): lax.all_to_all(jnp.broadcast_to(own_lists, (peers, own_lists.shape[1])),...  11.5 us
    ppermute x2, starting transfers between devices, shifted(): return lax.ppermute(block, axis, route)  6.85 us
    ppermute x1, starting transfers between devices, per_device(): arrived_half = lax.ppermute(theirs, 'head', [(0, 1), (1, 0)])  6.35 us
    unnamed x30, local copies, waits for them, and re-layouts  3.16 us
  transfers between devices with their start and end apart: 4, of which 1 were waited for; matrix products, arithmetic and copies ran while one was open for 11% of the time, Pallas kernels for 0%

profile of v14, /device:TPU:1, one launch (start us, length us, event | category | flops | bytes accessed | tf_op | source)
XLA Modules:
  0.0 151.8 jit_solution(9481225179946502542)
XLA Ops:
  0.0 0.8 copy.46
  0.8 0.8 pad_add_fusion
  1.6 4.9 %collective-permute-start = (s32[4,17]{1,0:T(4,128)S(1)}, s32[4,17]{1,0:T(4,128)S(1)}, u32[]{:S(2)}, u32[]{:S(2)}) collective-permute-start(s32[4,17]{1,0:T(4,128)S(1)} %pad_add_fusion), channel_id=1, source_target_pairs={{0,2},{2,4},{4,6},{6,8},{8,10},{10,12},{12,14},{14,16},{16,18},{18... | collective-permute-start | bytes 824 | tf_op jit(solution)/shard_map/ppermute | solution.py:88
  6.5 1.9 %collective-permute-start.1 = (bf16[2,64,16,512]{3,2,1,0:T(8,128)(2,1)}, bf16[2,64,16,512]{3,2,1,0:T(8,128)(2,1)}, u32[]{:S(2)}, u32[]{:S(2)}) collective-permute-start(bf16[2,64,16,512]{3,2,1,0:T(8,128)(2,1)} %param.20), channel_id=1, source_target_pairs={{0,2},{2,4},{4,6},{6,8},{8,10},{10,12},{12,14},{14,16},{16,18},{18... | collective-permute-start | bytes 6291464 | tf_op jit(solution)/shard_map/ppermute | solution.py:88
  8.5 0.7 add_bitcast_fusion.1
  9.2 0.7 broadcast_in_dim.102
  9.9 11.5 %all-to-all-start = ((s32[128,1,64]{2,1,0:T(1,128)}), s32[128,1,64]{2,1,0:T(1,128)S(1)}, u32[]{:S(2)}, u32[]{:S(2)}) async-start(s32[128,1,64]{2,1,0:T(1,128)} %broadcast_in_dim.102), calls=%async_computation | async-start | bytes 131072 | tf_op jit(solution)/shard_map/all_to_all | solution.py:221
  21.3 0.7 broadcast_compare_fusion.1
  22.0 1.2 gather_fusion.2
  23.5 2.7 %fusion.33 = (bf16[1,64,16,512]{3,2,1,0:T(8,128)(2,1)}, bf16[1,64,16,512]{3,2,1,0:T(8,128)(2,1)S(1)}) fusion(bf16[2,64,16,512]{3,2,1,0:T(8,128)(2,1)} %param.20), kind=kLoop, calls=%fused_computation.140 | loop fusion | bytes 4194304 | tf_op jit(solution)/shard_map/slice | solution.py:143
  26.2 0.2 convolution_bitcast_fusion
  26.4 0.2 convolution_bitcast_fusion.1
  26.6 0.2 convolution_bitcast_fusion.2
  26.9 0.2 convolution_bitcast_fusion.3
  27.1 0.6 gather_fusion.3
  27.9 0.1 and.80
  28.1 0.1 add.100
  28.4 0.1 fusion.36
  28.6 1.6 %copy.58 = bf16[1,32,128,128]{2,3,1,0:T(8,128)(2,1)S(1)} copy(bf16[1,32,128,128]{3,2,1,0:T(8,128)(2,1)} %param.31) | data formatting | bytes 2097152 | tf_op args[14]
  30.3 0.6 gather_fusion
  31.0 0.1 and.74
  31.1 0.1 and.75
  31.4 0.1 add.97
  31.6 0.2 slice_reduce_fusion
  31.7 0.6 gather_fusion.1
  32.5 1.7 %fusion.34 = (bf16[1,64,16,512]{3,2,1,0:T(8,128)(2,1)S(1)}, bf16[1,64,16,512]{3,2,1,0:T(8,128)(2,1)S(1)}) fusion(bf16[2,64,16,512]{3,2,1,0:T(8,128)(2,1)} %collective-permute-done.1), kind=kLoop, calls=%fused_computation.141 | loop fusion | bytes 4194304 | tf_op jit(solution)/shard_map/slice | solution.py:112
  34.2 0.2 convolution_bitcast_fusion.4
  34.4 0.2 convolution_bitcast_fusion.5
  34.6 0.2 convolution_bitcast_fusion.6
  34.8 0.2 convolution_bitcast_fusion.7
  35.1 0.2 select_reduce_fusion
  35.3 0.4 fusion.12
  35.7 0.3 divide_convert_fusion
  36.0 0.3 copy-done.2
  36.3 0.2 convolution_bitcast_fusion.11
  36.5 0.2 convolution_bitcast_fusion.10
  36.6 0.2 convolution_bitcast_fusion.9
  36.8 0.2 convolution_bitcast_fusion.8
  37.0 0.2 convolution_bitcast_fusion.15
  37.1 0.2 convolution_bitcast_fusion.14
  37.3 0.2 convolution_bitcast_fusion.13
  37.5 0.2 convolution_bitcast_fusion.12
  37.8 6.4 %collective-permute-start.2 = (bf16[2,4096]{1,0:T(2,128)(2,1)S(1)}, bf16[2,4096]{1,0:T(2,128)(2,1)S(1)}, u32[]{:S(2)}, u32[]{:S(2)}) collective-permute-start(bf16[2,4096]{1,0:T(2,128)(2,1)S(1)} %get-tuple-element.22), channel_id=1, source_target_pairs={{0,1},{1,0},{2,3},{3,2},{4,5},{5,4},{6,7},{7,6},{8,9},{9,8},{10,11... | collective-permute-start | bytes 49160 | tf_op jit(solution)/shard_map/ppermute | solution.py:209
  44.4 0.9 collective-permute-done.2
  45.3 0.2 multiply_reduce_fusion.4
  45.5 0.1 multiply_convert_fusion.2
  45.6 2.0 %convolution_convert_fusion = bf16[4096,256]{1,0:T(8,128)(2,1)} fusion(s32[4096]{0:T(1024)S(1)} %eq.80, bf16[8,8,2,128]{3,2,1,0:T(2,128)(2,1)S(1)} %bitcast.246), kind=kOutput, calls=%fused_computation.6 | convolution fusion | flops 135528448 | bytes 2146304 | tf_op jit(solution)/shard_map/dot_general | solution.py:235
  47.6 51.3 %shard_map.163 = bf16[128,32,256]{2,1,0:T(8,128)(2,1)} custom-call(bf16[128,32,256]{2,1,0:T(8,128)(2,1)} %bitcast.213), custom_call_target="tpu_custom_call" | custom-call | tf_op jit(solution)/shard_map/pallas_call | solution.py:71
  98.9 1.9 %fusion.32 = (bf16[128,32,128]{2,1,0:T(8,128)(2,1)S(1)}, bf16[128,32,128]{2,1,0:T(8,128)(2,1)S(1)}) fusion(bf16[128,32,256]{2,1,0:T(8,128)(2,1)} %shard_map.163), kind=kLoop, calls=%fused_computation.139 | loop fusion | bytes 4194304 | tf_op jit(solution)/shard_map/slice | solution.py:242
  100.8 0.7 multiply_reduce_fusion
  101.6 0.7 multiply_reduce_fusion.2
  102.3 0.5 copy-done.9
  102.8 0.7 multiply_reduce_fusion.1
  103.5 0.7 multiply_reduce_fusion.3
  104.3 0.7 fusion
  105.0 0.2 slice_bitcast_fusion.1
  105.2 0.2 copy.68
  105.5 0.2 copy.69
  105.7 1.7 %pad_maximum_fusion.x_ref = bf16[128,32,256]{2,1,0:T(8,128)(2,1)} fusion(bf16[128,32,128]{2,1,0:T(8,128)(2,1)S(1)} %bitcast.234, bf16[128,32,128]{2,1,0:T(8,128)(2,1)S(1)} %bitcast.232), kind=kLoop, calls=%fused_computation.7 | loop fusion | flops 4194304 | bytes 4194304 | tf_op jit(solution)/shard_map/concatenate | solution.py:253
  107.4 41.1 %shard_map.164 = bf16[128,32,256]{2,1,0:T(8,128)(2,1)} custom-call(bf16[128,32,256]{2,1,0:T(8,128)(2,1)} %pad_maximum_fusion.x_ref), custom_call_target="tpu_custom_call" | custom-call | tf_op jit(solution)/shard_map/pallas_call | solution.py:71
  148.5 1.9 %fusion.31 = (bf16[128,32,128]{2,1,0:T(8,128)(2,1)S(1)}, bf16[128,32,128]{2,1,0:T(8,128)(2,1)S(1)}) fusion(bf16[128,32,256]{2,1,0:T(8,128)(2,1)} %shard_map.164), kind=kLoop, calls=%fused_computation.138 | loop fusion | bytes 4194304 | tf_op jit(solution)/shard_map/slice | solution.py:260
  150.4 0.3 fusion.7
  150.7 0.3 fusion.6
  151.0 0.7 fusion.20
  (59 shorter events, 1.8 us)
Async XLA Ops:
  0.0 100.8 %copy-start = (bf16[1,32,128,128]{3,2,1,0:T(8,128)(2,1)S(1)}, bf16[1,32,128,128]{3,2,1,0:T(8,128)(2,1)}, u32[]{:S(2)}) copy-start(bf16[1,32,128,128]{3,2,1,0:T(8,128)(2,1)} %param.27) | copy-start | bytes 3145732
  1.6 28.7 %collective-permute-start = (s32[4,17]{1,0:T(4,128)S(1)}, s32[4,17]{1,0:T(4,128)S(1)}, u32[]{:S(2)}, u32[]{:S(2)}) collective-permute-start(s32[4,17]{1,0:T(4,128)S(1)} %pad_add_fusion), channel_id=1, source_target_pairs={{0,2},{2,4},{4,6},{6,8},{8,10},{10,12},{12,14},{14,16},{16,18},{18... | collective-permute-start | bytes 824 | tf_op jit(solution)/shard_map/ppermute | solution.py:88
  6.5 26.0 %collective-permute-start.1 = (bf16[2,64,16,512]{3,2,1,0:T(8,128)(2,1)}, bf16[2,64,16,512]{3,2,1,0:T(8,128)(2,1)}, u32[]{:S(2)}, u32[]{:S(2)}) collective-permute-start(bf16[2,64,16,512]{3,2,1,0:T(8,128)(2,1)} %param.20), channel_id=1, source_target_pairs={{0,2},{2,4},{4,6},{6,8},{8,10},{10,12},{12,14},{14,16},{16,18},{18... | collective-permute-start | bytes 6291464 | tf_op jit(solution)/shard_map/ppermute | solution.py:88
  9.9 34.3 %all-to-all-start = ((s32[128,1,64]{2,1,0:T(1,128)}), s32[128,1,64]{2,1,0:T(1,128)S(1)}, u32[]{:S(2)}, u32[]{:S(2)}) async-start(s32[128,1,64]{2,1,0:T(1,128)} %broadcast_in_dim.102), calls=%async_computation | async-start | bytes 131072 | tf_op jit(solution)/shard_map/all_to_all | solution.py:221
  23.5 2.7 %copy-start.4 = (bf16[4,4096]{1,0:T(4,128)(2,1)S(1)}, bf16[4,4096]{1,0:T(4,128)(2,1)}, u32[]{:S(2)}) copy-start(bf16[4,4096]{1,0:T(4,128)(2,1)} %param.17) | copy-start | bytes 98308
  23.5 3.6 %copy-start.1 = (s32[4]{0:T(128)S(1)}, s32[4]{0:T(128)}, u32[]{:S(2)}) copy-start(s32[4]{0:T(128)} %param.22) | copy-start | bytes 52
  26.2 2.0 %copy-start.6 = (bf16[4,512]{1,0:T(4,128)(2,1)S(1)}, bf16[4,512]{1,0:T(4,128)(2,1)}, u32[]{:S(2)}) copy-start(bf16[4,512]{1,0:T(4,128)(2,1)} %param.18) | copy-start | bytes 12292
  26.2 2.1 %copy-start.7 = (bf16[4,512]{1,0:T(4,128)(2,1)S(1)}, bf16[4,512]{1,0:T(4,128)(2,1)}, u32[]{:S(2)}) copy-start(bf16[4,512]{1,0:T(4,128)(2,1)} %param.19) | copy-start | bytes 12292
  26.2 2.1 %copy-start.8 = (f32[1,32]{1,0:T(1,128)S(1)}, f32[1,32]{1,0:T(1,128)}, u32[]{:S(2)}) copy-start(f32[1,32]{1,0:T(1,128)} %param.33) | copy-start | bytes 388
  35.1 1.2 copy-start.2
  36.0 9.3 %copy-start.3 = (bf16[2,8192]{1,0:T(2,128)(2,1)S(1)}, bf16[2,8192]{1,0:T(2,128)(2,1)}, u32[]{:S(2)}) copy-start(bf16[2,8192]{1,0:T(2,128)(2,1)} %param.24) | copy-start | bytes 98308
  36.0 9.5 %copy-start.5 = (f32[8192]{0:T(1024)S(1)}, f32[8192]{0:T(1024)}, u32[]{:S(2)}) copy-start(f32[8192]{0:T(1024)} %param.25) | copy-start | bytes 98308
  37.8 7.5 %collective-permute-start.2 = (bf16[2,4096]{1,0:T(2,128)(2,1)S(1)}, bf16[2,4096]{1,0:T(2,128)(2,1)S(1)}, u32[]{:S(2)}, u32[]{:S(2)}) collective-permute-start(bf16[2,4096]{1,0:T(2,128)(2,1)S(1)} %get-tuple-element.22), channel_id=1, source_target_pairs={{0,1},{1,0},{2,3},{3,2},{4,5},{5,4},{6,7},{7,6},{8,9},{9,8},{10,11... | collective-permute-start | bytes 49160 | tf_op jit(solution)/shard_map/ppermute | solution.py:209
  98.9 1.9 %copy-start.10 = (f32[1,32]{1,0:T(1,128)S(1)}, f32[1,32]{1,0:T(1,128)}, u32[]{:S(2)}) copy-start(f32[1,32]{1,0:T(1,128)} %param.30) | copy-start | bytes 388
  101.6 1.2 copy-start.9
  101.6 1.2 copy-start.11

commit v15 on v11

--- a/solution.py
+++ b/solution.py
@@ -217,7 +217,9 @@
         middle * lax.rsqrt(jnp.mean(middle * middle, axis=-1, keepdims=True) + 1e-05) * norm_gain
     ).astype(jnp.bfloat16)
     peers = lax.axis_size("wide")
-    own_lists = jnp.concatenate([gate_up_keep, down_keep], axis=1)
+    own_lists, normed = lax.optimization_barrier(
+        (jnp.concatenate([gate_up_keep, down_keep], axis=1), normed)
+    )
     keep_lists = lax.all_to_all(
         jnp.broadcast_to(own_lists, (peers, own_lists.shape[1])),
         "wide",

time: 146 us -> 161 us (1.10)
  waiting for transfers between devices: 0.89 us -> 24.2 us
  Pallas kernels: 86.5 us -> 78.2 us
  starting transfers between devices: 24.7 us -> 26.7 us
    ppermute x2, waiting for transfers between devices: 0.01 us -> 14.2 us  [shifted(): return lax.ppermute(block, axis, route)]
    all_to_all x1, waiting for transfers between devices: 0.01 us -> 8.99 us  [per_device(): lax.all_to_all(jnp.broadcast_to(own_lists, (peers, own_lists.shape[1])),...]
    pallas_call x2, Pallas kernels: 86.5 us -> 78.2 us  [exchange(): pl.pallas_call(functools.partial(exchange_kernel, route, lanes), out_shap...]
    all_to_all x1, starting transfers between devices: 11.5 us -> 13.6 us  [per_device(): lax.all_to_all(jnp.broadcast_to(own_lists, (peers, own_lists.shape[1])),...]
  transfers between devices with their start and end apart: 4 -> 4, of which waited for: 1 -> 3; matrix products, arithmetic and copies ran while one was open for 12% -> 6% of each run, Pallas kernels for 0% -> 0%
where the time goes in v15:
time: 161 us
  Pallas kernels  78.2 us (49%)
  starting transfers between devices  26.7 us (17%)
  waiting for transfers between devices  24.2 us (15%)
  local copies, waits for them, and re-layouts  15.9 us (10%)
  matrix products  9.15 us (6%)
  other arithmetic  6.01 us (4%)
    pallas_call x2, Pallas kernels, exchange(): pl.pallas_call(functools.partial(exchange_kernel, route, lanes), out_shap...  78.2 us
    ppermute x2, waiting for transfers between devices, shifted(): return lax.ppermute(block, axis, route)  14.2 us
    all_to_all x1, starting transfers between devices, per_device(): lax.all_to_all(jnp.broadcast_to(own_lists, (peers, own_lists.shape[1])),...  13.6 us
    all_to_all x1, waiting for transfers between devices, per_device(): lax.all_to_all(jnp.broadcast_to(own_lists, (peers, own_lists.shape[1])),...  8.99 us
    ppermute x2, starting transfers between devices, shifted(): return lax.ppermute(block, axis, route)  6.85 us
    ppermute x1, starting transfers between devices, per_device(): arrived_half = lax.ppermute(theirs, 'head', [(0, 1), (1, 0)])  6.27 us
  transfers between devices with their start and end apart: 4, of which 3 were waited for; matrix products, arithmetic and copies ran while one was open for 6% of the time, Pallas kernels for 0%

profile of v15, /device:TPU:1, one launch (start us, length us, event | category | flops | bytes accessed | tf_op | source)
XLA Modules:
  0.0 160.7 jit_solution(7057094239288018048)
XLA Ops:
  0.0 0.8 copy.46
  0.8 0.8 pad_add_fusion
  1.6 4.9 %collective-permute-start = (s32[4,17]{1,0:T(4,128)S(1)}, s32[4,17]{1,0:T(4,128)S(1)}, u32[]{:S(2)}, u32[]{:S(2)}) collective-permute-start(s32[4,17]{1,0:T(4,128)S(1)} %pad_add_fusion), channel_id=1, source_target_pairs={{0,2},{2,4},{4,6},{6,8},{8,10},{10,12},{12,14},{14,16},{16,18},{18... | collective-permute-start | bytes 824 | tf_op jit(solution)/shard_map/ppermute | solution.py:88
  6.5 1.9 %collective-permute-start.1 = (bf16[2,64,16,512]{3,2,1,0:T(8,128)(2,1)}, bf16[2,64,16,512]{3,2,1,0:T(8,128)(2,1)}, u32[]{:S(2)}, u32[]{:S(2)}) collective-permute-start(bf16[2,64,16,512]{3,2,1,0:T(8,128)(2,1)} %param.20), channel_id=1, source_target_pairs={{0,2},{2,4},{4,6},{6,8},{8,10},{10,12},{12,14},{14,16},{16,18},{18... | collective-permute-start | bytes 6291464 | tf_op jit(solution)/shard_map/ppermute | solution.py:88
  8.5 0.7 broadcast_compare_fusion.1
  9.2 1.2 gather_fusion.2
  10.4 1.3 gather_fusion.3
  11.7 1.7 %fusion.33 = (bf16[1,64,16,512]{3,2,1,0:T(8,128)(2,1)S(1)}, bf16[1,64,16,512]{3,2,1,0:T(8,128)(2,1)S(1)}) fusion(bf16[2,64,16,512]{3,2,1,0:T(8,128)(2,1)} %param.20), kind=kLoop, calls=%fused_computation.140 | loop fusion | bytes 4194304 | tf_op jit(solution)/shard_map/slice | solution.py:143
  13.5 0.2 convolution_bitcast_fusion
  13.6 0.2 convolution_bitcast_fusion.1
  13.8 0.2 convolution_bitcast_fusion.2
  14.0 0.2 convolution_bitcast_fusion.3
  14.2 0.1 fusion.23
  14.5 0.1 and.80
  14.9 0.1 fusion.36
  15.0 0.1 add.99
  15.1 0.1 add.100
  15.3 0.6 gather_fusion
  16.2 0.1 and.75
  16.5 0.1 add.97
  16.6 0.2 slice_reduce_fusion
  16.8 0.6 gather_fusion.1
  17.6 14.2 %collective-permute-done.1 = bf16[2,64,16,512]{3,2,1,0:T(8,128)(2,1)} collective-permute-done((bf16[2,64,16,512]{3,2,1,0:T(8,128)(2,1)}, bf16[2,64,16,512]{3,2,1,0:T(8,128)(2,1)}, u32[]{:S(2)}, u32[]{:S(2)}) %collective-permute-start.1) | collective-permute-done | bytes 2097184 | tf_op jit(solution)/shard_map/ppermute | solution.py:88
  31.7 1.7 %fusion.34 = (bf16[1,64,16,512]{3,2,1,0:T(8,128)(2,1)S(1)}, bf16[1,64,16,512]{3,2,1,0:T(8,128)(2,1)S(1)}) fusion(bf16[2,64,16,512]{3,2,1,0:T(8,128)(2,1)} %collective-permute-done.1), kind=kLoop, calls=%fused_computation.141 | loop fusion | bytes 4194304 | tf_op jit(solution)/shard_map/slice | solution.py:112
  33.4 0.2 convolution_bitcast_fusion.4
  33.6 0.2 convolution_bitcast_fusion.5
  33.8 0.2 convolution_bitcast_fusion.6
  34.0 0.2 convolution_bitcast_fusion.7
  34.3 0.2 select_reduce_fusion
  34.5 0.4 fusion.12
  34.9 0.3 divide_convert_fusion
  35.3 0.2 convolution_bitcast_fusion.11
  35.4 0.2 convolution_bitcast_fusion.10
  35.6 0.2 convolution_bitcast_fusion.9
  35.8 0.2 convolution_bitcast_fusion.8
  35.9 0.2 convolution_bitcast_fusion.15
  36.1 0.2 convolution_bitcast_fusion.14
  36.2 0.2 convolution_bitcast_fusion.13
  36.4 0.2 convolution_bitcast_fusion.12
  36.7 6.3 %collective-permute-start.2 = (bf16[2,4096]{1,0:T(2,128)(2,1)S(1)}, bf16[2,4096]{1,0:T(2,128)(2,1)S(1)}, u32[]{:S(2)}, u32[]{:S(2)}) collective-permute-start(bf16[2,4096]{1,0:T(2,128)(2,1)S(1)} %get-tuple-element.26), channel_id=1, source_target_pairs={{0,1},{1,0},{2,3},{3,2},{4,5},{5,4},{6,7},{7,6},{8,9},{9,8},{10,11... | collective-permute-start | bytes 49160 | tf_op jit(solution)/shard_map/ppermute | solution.py:209
  43.1 1.0 collective-permute-done.2
  44.2 0.2 multiply_reduce_fusion.4
  44.5 0.7 broadcast_in_dim.102
  45.1 13.6 %all-to-all-start = ((s32[128,1,64]{2,1,0:T(1,128)}), s32[128,1,64]{2,1,0:T(1,128)S(1)}, u32[]{:S(2)}, u32[]{:S(2)}) async-start(s32[128,1,64]{2,1,0:T(1,128)} %broadcast_in_dim.102), calls=%async_computation | async-start | bytes 131072 | tf_op jit(solution)/shard_map/all_to_all | solution.py:223
  58.8 0.7 copy.58
  59.5 9.0 %all-to-all-done = s32[128,1,64]{2,1,0:T(1,128)S(1)} async-done(((s32[128,1,64]{2,1,0:T(1,128)}), s32[128,1,64]{2,1,0:T(1,128)S(1)}, u32[]{:S(2)}, u32[]{:S(2)}) %all-to-all-start) | async-done | bytes 32800 | tf_op jit(solution)/shard_map/all_to_all | solution.py:223
  68.7 2.0 %convolution_convert_fusion = bf16[4096,256]{1,0:T(8,128)(2,1)} fusion(s32[4096]{0:T(1024)S(1)} %eq.80, bf16[8,8,2,128]{3,2,1,0:T(2,128)(2,1)S(1)} %bitcast.245), kind=kOutput, calls=%fused_computation.6 | convolution fusion | flops 135528448 | bytes 2146304 | tf_op jit(solution)/shard_map/dot_general | solution.py:237
  70.7 39.8 %shard_map.163 = bf16[128,32,256]{2,1,0:T(8,128)(2,1)} custom-call(bf16[128,32,256]{2,1,0:T(8,128)(2,1)} %bitcast.212), custom_call_target="tpu_custom_call" | custom-call | tf_op jit(solution)/shard_map/pallas_call | solution.py:71
  110.5 1.9 %fusion.32 = (bf16[128,32,128]{2,1,0:T(8,128)(2,1)S(1)}, bf16[128,32,128]{2,1,0:T(8,128)(2,1)S(1)}) fusion(bf16[128,32,256]{2,1,0:T(8,128)(2,1)} %shard_map.163), kind=kLoop, calls=%fused_computation.139 | loop fusion | bytes 4194304 | tf_op jit(solution)/shard_map/slice | solution.py:244
  112.5 0.7 multiply_reduce_fusion
  113.2 0.7 multiply_reduce_fusion.2
  113.9 0.5 copy-done.8
  114.4 0.7 multiply_reduce_fusion.1
  115.1 0.7 multiply_reduce_fusion.3
  115.9 0.7 fusion
  116.6 0.2 slice_bitcast_fusion.1
  116.8 0.2 copy.68
  117.1 0.2 copy.69
  117.3 1.7 %pad_maximum_fusion.x_ref = bf16[128,32,256]{2,1,0:T(8,128)(2,1)} fusion(bf16[128,32,128]{2,1,0:T(8,128)(2,1)S(1)} %bitcast.233, bf16[128,32,128]{2,1,0:T(8,128)(2,1)S(1)} %bitcast.232), kind=kLoop, calls=%fused_computation.7 | loop fusion | flops 4194304 | bytes 4194304 | tf_op jit(solution)/shard_map/concatenate | solution.py:255
  119.0 38.4 %shard_map.164 = bf16[128,32,256]{2,1,0:T(8,128)(2,1)} custom-call(bf16[128,32,256]{2,1,0:T(8,128)(2,1)} %pad_maximum_fusion.x_ref), custom_call_target="tpu_custom_call" | custom-call | tf_op jit(solution)/shard_map/pallas_call | solution.py:71
  157.4 1.9 %fusion.31 = (bf16[128,32,128]{2,1,0:T(8,128)(2,1)S(1)}, bf16[128,32,128]{2,1,0:T(8,128)(2,1)S(1)}) fusion(bf16[128,32,256]{2,1,0:T(8,128)(2,1)} %shard_map.164), kind=kLoop, calls=%fused_computation.138 | loop fusion | bytes 4194304 | tf_op jit(solution)/shard_map/slice | solution.py:262
  159.4 0.3 fusion.7
  159.7 0.3 fusion.6
  160.0 0.7 fusion.20
  (61 shorter events, 1.9 us)
Async XLA Ops:
  0.0 112.4 %copy-start = (bf16[1,32,128,128]{3,2,1,0:T(8,128)(2,1)S(1)}, bf16[1,32,128,128]{3,2,1,0:T(8,128)(2,1)}, u32[]{:S(2)}) copy-start(bf16[1,32,128,128]{3,2,1,0:T(8,128)(2,1)} %param.27) | copy-start | bytes 3145732
  1.6 13.7 %collective-permute-start = (s32[4,17]{1,0:T(4,128)S(1)}, s32[4,17]{1,0:T(4,128)S(1)}, u32[]{:S(2)}, u32[]{:S(2)}) collective-permute-start(s32[4,17]{1,0:T(4,128)S(1)} %pad_add_fusion), channel_id=1, source_target_pairs={{0,2},{2,4},{4,6},{6,8},{8,10},{10,12},{12,14},{14,16},{16,18},{18... | collective-permute-start | bytes 824 | tf_op jit(solution)/shard_map/ppermute | solution.py:88
  6.5 25.2 %collective-permute-start.1 = (bf16[2,64,16,512]{3,2,1,0:T(8,128)(2,1)}, bf16[2,64,16,512]{3,2,1,0:T(8,128)(2,1)}, u32[]{:S(2)}, u32[]{:S(2)}) collective-permute-start(bf16[2,64,16,512]{3,2,1,0:T(8,128)(2,1)} %param.20), channel_id=1, source_target_pairs={{0,2},{2,4},{4,6},{6,8},{8,10},{10,12},{12,14},{14,16},{16,18},{18... | collective-permute-start | bytes 6291464 | tf_op jit(solution)/shard_map/ppermute | solution.py:88
  11.7 1.7 %copy-start.3 = (bf16[4,4096]{1,0:T(4,128)(2,1)S(1)}, bf16[4,4096]{1,0:T(4,128)(2,1)}, u32[]{:S(2)}) copy-start(bf16[4,4096]{1,0:T(4,128)(2,1)} %param.17) | copy-start | bytes 98308
  11.7 3.0 %copy-start.5 = (bf16[4,512]{1,0:T(4,128)(2,1)S(1)}, bf16[4,512]{1,0:T(4,128)(2,1)}, u32[]{:S(2)}) copy-start(bf16[4,512]{1,0:T(4,128)(2,1)} %param.18) | copy-start | bytes 12292
  13.4 1.4 copy-start.6
  34.9 8.2 %copy-start.9 = (s32[1,32]{1,0:T(1,128)S(1)}, s32[1,32]{1,0:T(1,128)}, u32[]{:S(2)}) copy-start(s32[1,32]{1,0:T(1,128)} %param.32) | copy-start | bytes 388
  34.9 8.1 %copy-start.10 = (s32[1,32]{1,0:T(1,128)S(1)}, s32[1,32]{1,0:T(1,128)}, u32[]{:S(2)}) copy-start(s32[1,32]{1,0:T(1,128)} %param.28) | copy-start | bytes 388
  34.9 9.3 %copy-start.2 = (bf16[2,8192]{1,0:T(2,128)(2,1)S(1)}, bf16[2,8192]{1,0:T(2,128)(2,1)}, u32[]{:S(2)}) copy-start(bf16[2,8192]{1,0:T(2,128)(2,1)} %param.24) | copy-start | bytes 98308
  34.9 9.5 %copy-start.4 = (f32[8192]{0:T(1024)S(1)}, f32[8192]{0:T(1024)}, u32[]{:S(2)}) copy-start(f32[8192]{0:T(1024)} %param.25) | copy-start | bytes 98308
  35.2 23.5 %copy-start.7 = (f32[1,32]{1,0:T(1,128)S(1)}, f32[1,32]{1,0:T(1,128)}, u32[]{:S(2)}) copy-start(f32[1,32]{1,0:T(1,128)} %param.33) | copy-start | bytes 388
  35.2 23.6 %copy-start.1 = (bf16[1,32,128,128]{3,2,1,0:T(8,128)(2,1)S(1)}, bf16[1,32,128,128]{3,2,1,0:T(8,128)(2,1)}, u32[]{:S(2)}) copy-start(bf16[1,32,128,128]{3,2,1,0:T(8,128)(2,1)} %param.31) | copy-start | bytes 3145732
  36.7 7.4 %collective-permute-start.2 = (bf16[2,4096]{1,0:T(2,128)(2,1)S(1)}, bf16[2,4096]{1,0:T(2,128)(2,1)S(1)}, u32[]{:S(2)}, u32[]{:S(2)}) collective-permute-start(bf16[2,4096]{1,0:T(2,128)(2,1)S(1)} %get-tuple-element.26), channel_id=1, source_target_pairs={{0,1},{1,0},{2,3},{3,2},{4,5},{5,4},{6,7},{7,6},{8,9},{9,8},{10,11... | collective-permute-start | bytes 49160 | tf_op jit(solution)/shard_map/ppermute | solution.py:209
  45.1 23.4 %all-to-all-start = ((s32[128,1,64]{2,1,0:T(1,128)}), s32[128,1,64]{2,1,0:T(1,128)S(1)}, u32[]{:S(2)}, u32[]{:S(2)}) async-start(s32[128,1,64]{2,1,0:T(1,128)} %broadcast_in_dim.102), calls=%async_computation | async-start | bytes 131072 | tf_op jit(solution)/shard_map/all_to_all | solution.py:223
  110.5 1.9 %copy-start.11 = (f32[1,32]{1,0:T(1,128)S(1)}, f32[1,32]{1,0:T(1,128)}, u32[]{:S(2)}) copy-start(f32[1,32]{1,0:T(1,128)} %param.30) | copy-start | bytes 388
  113.2 1.2 copy-start.8
  113.2 1.2 copy-start.12

commit v16 on v11

--- a/solution.py
+++ b/solution.py
@@ -40,7 +40,9 @@
     for way in range(ways):
 
         def send(step, carry, way=way):
-            peer = lax.rem(me + step * ways + way, n)
+            turn = step * ways + way
+            hop = (turn % 2) * ((turn + 1) // 2) + (1 - turn % 2) * (n - turn // 2)
+            peer = lax.rem(me + hop, n)
             pltpu.make_async_remote_copy(
                 src_ref=x_ref.at[peer],
                 dst_ref=y_ref.at[me],

time: 146 us -> 146 us (level); the launches traced: 146 us -> 144 us
  Pallas kernels: 86.5 us -> 84.4 us
    pallas_call x2, Pallas kernels: 86.5 us -> 84.4 us  [exchange(): pl.pallas_call(functools.partial(exchange_kernel, route, lanes), out_shap...]
where the time goes in v16:
time: 146 us; the launch traced here: 144 us
  Pallas kernels  84.4 us (58%)
  starting transfers between devices  24.7 us (17%)
  local copies, waits for them, and re-layouts  17.5 us (12%)
  matrix products  9.13 us (6%)
  other arithmetic  6.69 us (5%)
    pallas_call x2, Pallas kernels, exchange(): pl.pallas_call(functools.partial(exchange_kernel, route, lanes), out_shap...  84.4 us
    all_to_all x1, starting transfers between devices, per_device(): lax.all_to_all(jnp.broadcast_to(own_lists, (peers, own_lists.shape[1])),...  11.5 us
    ppermute x2, starting transfers between devices, shifted(): return lax.ppermute(block, axis, route)  6.85 us
    ppermute x1, starting transfers between devices, per_device(): arrived_half = lax.ppermute(theirs, 'head', [(0, 1), (1, 0)])  6.35 us
    unnamed x30, local copies, waits for them, and re-layouts  3.15 us
  transfers between devices with their start and end apart: 4, of which 1 were waited for; matrix products, arithmetic and copies ran while one was open for 12% of the time, Pallas kernels for 0%

profile of v16, /device:TPU:1, one launch (start us, length us, event | category | flops | bytes accessed | tf_op | source)
XLA Modules:
  0.0 143.7 jit_solution(1429957046010785487)
XLA Ops:
  0.0 0.8 copy.46
  0.8 0.8 pad_add_fusion
  1.6 4.9 %collective-permute-start = (s32[4,17]{1,0:T(4,128)S(1)}, s32[4,17]{1,0:T(4,128)S(1)}, u32[]{:S(2)}, u32[]{:S(2)}) collective-permute-start(s32[4,17]{1,0:T(4,128)S(1)} %pad_add_fusion), channel_id=1, source_target_pairs={{0,2},{2,4},{4,6},{6,8},{8,10},{10,12},{12,14},{14,16},{16,18},{18... | collective-permute-start | bytes 824 | tf_op jit(solution)/shard_map/ppermute | solution.py:90
  6.5 1.9 %collective-permute-start.1 = (bf16[2,64,16,512]{3,2,1,0:T(8,128)(2,1)}, bf16[2,64,16,512]{3,2,1,0:T(8,128)(2,1)}, u32[]{:S(2)}, u32[]{:S(2)}) collective-permute-start(bf16[2,64,16,512]{3,2,1,0:T(8,128)(2,1)} %param.20), channel_id=1, source_target_pairs={{0,2},{2,4},{4,6},{6,8},{8,10},{10,12},{12,14},{14,16},{16,18},{18... | collective-permute-start | bytes 6291464 | tf_op jit(solution)/shard_map/ppermute | solution.py:90
  8.5 0.7 add_bitcast_fusion.1
  9.2 0.7 broadcast_in_dim.102
  9.9 11.5 %all-to-all-start = ((s32[128,1,64]{2,1,0:T(1,128)}), s32[128,1,64]{2,1,0:T(1,128)S(1)}, u32[]{:S(2)}, u32[]{:S(2)}) async-start(s32[128,1,64]{2,1,0:T(1,128)} %broadcast_in_dim.102), calls=%async_computation | async-start | bytes 131072 | tf_op jit(solution)/shard_map/all_to_all | solution.py:223
  21.3 0.7 broadcast_compare_fusion.1
  22.0 1.2 gather_fusion.2
  23.5 2.7 %fusion.33 = (bf16[1,64,16,512]{3,2,1,0:T(8,128)(2,1)}, bf16[1,64,16,512]{3,2,1,0:T(8,128)(2,1)S(1)}) fusion(bf16[2,64,16,512]{3,2,1,0:T(8,128)(2,1)} %param.20), kind=kLoop, calls=%fused_computation.140 | loop fusion | bytes 4194304 | tf_op jit(solution)/shard_map/slice | solution.py:145
  26.2 0.2 convolution_bitcast_fusion
  26.4 0.2 convolution_bitcast_fusion.1
  26.6 0.2 convolution_bitcast_fusion.2
  26.9 0.2 convolution_bitcast_fusion.3
  27.1 0.6 gather_fusion.3
  27.9 0.1 and.80
  28.1 0.1 add.100
  28.4 0.1 fusion.36
  28.6 1.6 %copy.58 = bf16[1,32,128,128]{2,3,1,0:T(8,128)(2,1)S(1)} copy(bf16[1,32,128,128]{3,2,1,0:T(8,128)(2,1)} %param.31) | data formatting | bytes 2097152 | tf_op args[14]
  30.3 0.6 gather_fusion
  31.0 0.1 and.74
  31.1 0.1 and.75
  31.4 0.1 add.97
  31.6 0.2 slice_reduce_fusion
  31.7 0.6 gather_fusion.1
  32.5 1.7 %fusion.34 = (bf16[1,64,16,512]{3,2,1,0:T(8,128)(2,1)S(1)}, bf16[1,64,16,512]{3,2,1,0:T(8,128)(2,1)S(1)}) fusion(bf16[2,64,16,512]{3,2,1,0:T(8,128)(2,1)} %collective-permute-done.1), kind=kLoop, calls=%fused_computation.141 | loop fusion | bytes 4194304 | tf_op jit(solution)/shard_map/slice | solution.py:114
  34.2 0.2 convolution_bitcast_fusion.4
  34.4 0.2 convolution_bitcast_fusion.5
  34.6 0.2 convolution_bitcast_fusion.6
  34.8 0.2 convolution_bitcast_fusion.7
  35.1 0.2 select_reduce_fusion
  35.3 0.4 fusion.12
  35.7 0.3 divide_convert_fusion
  36.0 0.3 copy-done.2
  36.3 0.2 convolution_bitcast_fusion.11
  36.5 0.2 convolution_bitcast_fusion.10
  36.6 0.2 convolution_bitcast_fusion.9
  36.8 0.2 convolution_bitcast_fusion.8
  37.0 0.2 convolution_bitcast_fusion.15
  37.1 0.2 convolution_bitcast_fusion.14
  37.3 0.2 convolution_bitcast_fusion.13
  37.5 0.2 convolution_bitcast_fusion.12
  37.8 6.4 %collective-permute-start.2 = (bf16[2,4096]{1,0:T(2,128)(2,1)S(1)}, bf16[2,4096]{1,0:T(2,128)(2,1)S(1)}, u32[]{:S(2)}, u32[]{:S(2)}) collective-permute-start(bf16[2,4096]{1,0:T(2,128)(2,1)S(1)} %get-tuple-element.22), channel_id=1, source_target_pairs={{0,1},{1,0},{2,3},{3,2},{4,5},{5,4},{6,7},{7,6},{8,9},{9,8},{10,11... | collective-permute-start | bytes 49160 | tf_op jit(solution)/shard_map/ppermute | solution.py:211
  44.4 0.9 collective-permute-done.2
  45.3 0.2 multiply_reduce_fusion.4
  45.5 0.1 multiply_convert_fusion.2
  45.6 2.0 %convolution_convert_fusion = bf16[4096,256]{1,0:T(8,128)(2,1)} fusion(s32[4096]{0:T(1024)S(1)} %eq.80, bf16[8,8,2,128]{3,2,1,0:T(2,128)(2,1)S(1)} %bitcast.246), kind=kOutput, calls=%fused_computation.6 | convolution fusion | flops 135528448 | bytes 2146304 | tf_op jit(solution)/shard_map/dot_general | solution.py:237
  47.6 48.9 %shard_map.163 = bf16[128,32,256]{2,1,0:T(8,128)(2,1)} custom-call(bf16[128,32,256]{2,1,0:T(8,128)(2,1)} %bitcast.213), custom_call_target="tpu_custom_call" | custom-call | tf_op jit(solution)/shard_map/pallas_call | solution.py:73
  96.5 1.9 %fusion.32 = (bf16[128,32,128]{2,1,0:T(8,128)(2,1)S(1)}, bf16[128,32,128]{2,1,0:T(8,128)(2,1)S(1)}) fusion(bf16[128,32,256]{2,1,0:T(8,128)(2,1)} %shard_map.163), kind=kLoop, calls=%fused_computation.139 | loop fusion | bytes 4194304 | tf_op jit(solution)/shard_map/slice | solution.py:244
  98.5 0.7 multiply_reduce_fusion
  99.2 0.7 multiply_reduce_fusion.2
  99.9 0.5 copy-done.9
  100.4 0.7 multiply_reduce_fusion.1
  101.1 0.7 multiply_reduce_fusion.3
  101.9 0.7 fusion
  102.6 0.2 slice_bitcast_fusion.1
  102.8 0.2 copy.68
  103.1 0.2 copy.69
  103.3 1.7 %pad_maximum_fusion.x_ref = bf16[128,32,256]{2,1,0:T(8,128)(2,1)} fusion(bf16[128,32,128]{2,1,0:T(8,128)(2,1)S(1)} %bitcast.234, bf16[128,32,128]{2,1,0:T(8,128)(2,1)S(1)} %bitcast.232), kind=kLoop, calls=%fused_computation.7 | loop fusion | flops 4194304 | bytes 4194304 | tf_op jit(solution)/shard_map/concatenate | solution.py:255
  105.0 35.5 %shard_map.164 = bf16[128,32,256]{2,1,0:T(8,128)(2,1)} custom-call(bf16[128,32,256]{2,1,0:T(8,128)(2,1)} %pad_maximum_fusion.x_ref), custom_call_target="tpu_custom_call" | custom-call | tf_op jit(solution)/shard_map/pallas_call | solution.py:73
  140.5 1.9 %fusion.31 = (bf16[128,32,128]{2,1,0:T(8,128)(2,1)S(1)}, bf16[128,32,128]{2,1,0:T(8,128)(2,1)S(1)}) fusion(bf16[128,32,256]{2,1,0:T(8,128)(2,1)} %shard_map.164), kind=kLoop, calls=%fused_computation.138 | loop fusion | bytes 4194304 | tf_op jit(solution)/shard_map/slice | solution.py:262
  142.4 0.3 fusion.7
  142.7 0.3 fusion.6
  143.0 0.7 fusion.20
  (59 shorter events, 1.8 us)
Async XLA Ops:
  0.0 98.4 %copy-start = (bf16[1,32,128,128]{3,2,1,0:T(8,128)(2,1)S(1)}, bf16[1,32,128,128]{3,2,1,0:T(8,128)(2,1)}, u32[]{:S(2)}) copy-start(bf16[1,32,128,128]{3,2,1,0:T(8,128)(2,1)} %param.27) | copy-start | bytes 3145732
  1.6 28.7 %collective-permute-start = (s32[4,17]{1,0:T(4,128)S(1)}, s32[4,17]{1,0:T(4,128)S(1)}, u32[]{:S(2)}, u32[]{:S(2)}) collective-permute-start(s32[4,17]{1,0:T(4,128)S(1)} %pad_add_fusion), channel_id=1, source_target_pairs={{0,2},{2,4},{4,6},{6,8},{8,10},{10,12},{12,14},{14,16},{16,18},{18... | collective-permute-start | bytes 824 | tf_op jit(solution)/shard_map/ppermute | solution.py:90
  6.5 26.0 %collective-permute-start.1 = (bf16[2,64,16,512]{3,2,1,0:T(8,128)(2,1)}, bf16[2,64,16,512]{3,2,1,0:T(8,128)(2,1)}, u32[]{:S(2)}, u32[]{:S(2)}) collective-permute-start(bf16[2,64,16,512]{3,2,1,0:T(8,128)(2,1)} %param.20), channel_id=1, source_target_pairs={{0,2},{2,4},{4,6},{6,8},{8,10},{10,12},{12,14},{14,16},{16,18},{18... | collective-permute-start | bytes 6291464 | tf_op jit(solution)/shard_map/ppermute | solution.py:90
  9.9 34.3 %all-to-all-start = ((s32[128,1,64]{2,1,0:T(1,128)}), s32[128,1,64]{2,1,0:T(1,128)S(1)}, u32[]{:S(2)}, u32[]{:S(2)}) async-start(s32[128,1,64]{2,1,0:T(1,128)} %broadcast_in_dim.102), calls=%async_computation | async-start | bytes 131072 | tf_op jit(solution)/shard_map/all_to_all | solution.py:223
  23.5 2.7 %copy-start.4 = (bf16[4,4096]{1,0:T(4,128)(2,1)S(1)}, bf16[4,4096]{1,0:T(4,128)(2,1)}, u32[]{:S(2)}) copy-start(bf16[4,4096]{1,0:T(4,128)(2,1)} %param.17) | copy-start | bytes 98308
  23.5 3.6 %copy-start.1 = (s32[4]{0:T(128)S(1)}, s32[4]{0:T(128)}, u32[]{:S(2)}) copy-start(s32[4]{0:T(128)} %param.22) | copy-start | bytes 52
  26.2 2.0 %copy-start.6 = (bf16[4,512]{1,0:T(4,128)(2,1)S(1)}, bf16[4,512]{1,0:T(4,128)(2,1)}, u32[]{:S(2)}) copy-start(bf16[4,512]{1,0:T(4,128)(2,1)} %param.18) | copy-start | bytes 12292
  26.2 2.1 %copy-start.7 = (bf16[4,512]{1,0:T(4,128)(2,1)S(1)}, bf16[4,512]{1,0:T(4,128)(2,1)}, u32[]{:S(2)}) copy-start(bf16[4,512]{1,0:T(4,128)(2,1)} %param.19) | copy-start | bytes 12292
  26.2 2.1 %copy-start.8 = (f32[1,32]{1,0:T(1,128)S(1)}, f32[1,32]{1,0:T(1,128)}, u32[]{:S(2)}) copy-start(f32[1,32]{1,0:T(1,128)} %param.33) | copy-start | bytes 388
  35.1 1.2 copy-start.2
  36.0 9.3 %copy-start.3 = (bf16[2,8192]{1,0:T(2,128)(2,1)S(1)}, bf16[2,8192]{1,0:T(2,128)(2,1)}, u32[]{:S(2)}) copy-start(bf16[2,8192]{1,0:T(2,128)(2,1)} %param.24) | copy-start | bytes 98308
  36.0 9.5 %copy-start.5 = (f32[8192]{0:T(1024)S(1)}, f32[8192]{0:T(1024)}, u32[]{:S(2)}) copy-start(f32[8192]{0:T(1024)} %param.25) | copy-start | bytes 98308
  37.8 7.5 %collective-permute-start.2 = (bf16[2,4096]{1,0:T(2,128)(2,1)S(1)}, bf16[2,4096]{1,0:T(2,128)(2,1)S(1)}, u32[]{:S(2)}, u32[]{:S(2)}) collective-permute-start(bf16[2,4096]{1,0:T(2,128)(2,1)S(1)} %get-tuple-element.22), channel_id=1, source_target_pairs={{0,1},{1,0},{2,3},{3,2},{4,5},{5,4},{6,7},{7,6},{8,9},{9,8},{10,11... | collective-permute-start | bytes 49160 | tf_op jit(solution)/shard_map/ppermute | solution.py:211
  96.5 1.9 %copy-start.10 = (f32[1,32]{1,0:T(1,128)S(1)}, f32[1,32]{1,0:T(1,128)}, u32[]{:S(2)}) copy-start(f32[1,32]{1,0:T(1,128)} %param.30) | copy-start | bytes 388
  99.2 1.2 copy-start.9
  99.2 1.2 copy-start.11

commit v17 on v16

--- a/solution.py
+++ b/solution.py
@@ -69,7 +69,7 @@
     local.wait()
 
 
-def exchange(x, route, lanes, ways=8):
+def exchange(x, route, lanes, ways=16):
     return pl.pallas_call(
         functools.partial(exchange_kernel, route, lanes),
         out_shape=jax.ShapeDtypeStruct(x.shape, x.dtype),

time: 146 us -> 146 us (level)
  no operation moved by 1% of the time
where the time goes in v17:
time: 146 us; the launch traced here: 145 us
  Pallas kernels  85.7 us (59%)
  starting transfers between devices  24.7 us (17%)
  local copies, waits for them, and re-layouts  17.5 us (12%)
  matrix products  9.12 us (6%)
  other arithmetic  6.69 us (5%)
    pallas_call x2, Pallas kernels, exchange(): pl.pallas_call(functools.partial(exchange_kernel, route, lanes), out_shap...  85.7 us
    all_to_all x1, starting transfers between devices, per_device(): lax.all_to_all(jnp.broadcast_to(own_lists, (peers, own_lists.shape[1])),...  11.5 us
    ppermute x2, starting transfers between devices, shifted(): return lax.ppermute(block, axis, route)  6.85 us
    ppermute x1, starting transfers between devices, per_device(): arrived_half = lax.ppermute(theirs, 'head', [(0, 1), (1, 0)])  6.35 us
    unnamed x30, local copies, waits for them, and re-layouts  3.16 us
  transfers between devices with their start and end apart: 4, of which 1 were waited for; matrix products, arithmetic and copies ran while one was open for 12% of the time, Pallas kernels for 0%

profile of v17, /device:TPU:1, one launch (start us, length us, event | category | flops | bytes accessed | tf_op | source)
XLA Modules:
  0.0 145.1 jit_solution(1052407935648458013)
XLA Ops:
  0.0 0.8 copy.46
  0.8 0.8 pad_add_fusion
  1.6 4.9 %collective-permute-start = (s32[4,17]{1,0:T(4,128)S(1)}, s32[4,17]{1,0:T(4,128)S(1)}, u32[]{:S(2)}, u32[]{:S(2)}) collective-permute-start(s32[4,17]{1,0:T(4,128)S(1)} %pad_add_fusion), channel_id=1, source_target_pairs={{0,2},{2,4},{4,6},{6,8},{8,10},{10,12},{12,14},{14,16},{16,18},{18... | collective-permute-start | bytes 824 | tf_op jit(solution)/shard_map/ppermute | solution.py:90
  6.5 1.9 %collective-permute-start.1 = (bf16[2,64,16,512]{3,2,1,0:T(8,128)(2,1)}, bf16[2,64,16,512]{3,2,1,0:T(8,128)(2,1)}, u32[]{:S(2)}, u32[]{:S(2)}) collective-permute-start(bf16[2,64,16,512]{3,2,1,0:T(8,128)(2,1)} %param.20), channel_id=1, source_target_pairs={{0,2},{2,4},{4,6},{6,8},{8,10},{10,12},{12,14},{14,16},{16,18},{18... | collective-permute-start | bytes 6291464 | tf_op jit(solution)/shard_map/ppermute | solution.py:90
  8.5 0.7 add_bitcast_fusion.1
  9.2 0.7 broadcast_in_dim.102
  9.9 11.5 %all-to-all-start = ((s32[128,1,64]{2,1,0:T(1,128)}), s32[128,1,64]{2,1,0:T(1,128)S(1)}, u32[]{:S(2)}, u32[]{:S(2)}) async-start(s32[128,1,64]{2,1,0:T(1,128)} %broadcast_in_dim.102), calls=%async_computation | async-start | bytes 131072 | tf_op jit(solution)/shard_map/all_to_all | solution.py:223
  21.3 0.7 broadcast_compare_fusion.1
  22.0 1.2 gather_fusion.2
  23.5 2.7 %fusion.33 = (bf16[1,64,16,512]{3,2,1,0:T(8,128)(2,1)}, bf16[1,64,16,512]{3,2,1,0:T(8,128)(2,1)S(1)}) fusion(bf16[2,64,16,512]{3,2,1,0:T(8,128)(2,1)} %param.20), kind=kLoop, calls=%fused_computation.140 | loop fusion | bytes 4194304 | tf_op jit(solution)/shard_map/slice | solution.py:145
  26.2 0.2 convolution_bitcast_fusion
  26.4 0.2 convolution_bitcast_fusion.1
  26.6 0.2 convolution_bitcast_fusion.2
  26.9 0.2 convolution_bitcast_fusion.3
  27.1 0.6 gather_fusion.3
  27.9 0.1 and.80
  28.1 0.1 add.100
  28.4 0.1 fusion.36
  28.6 1.6 %copy.58 = bf16[1,32,128,128]{2,3,1,0:T(8,128)(2,1)S(1)} copy(bf16[1,32,128,128]{3,2,1,0:T(8,128)(2,1)} %param.31) | data formatting | bytes 2097152 | tf_op args[14]
  30.3 0.6 gather_fusion
  31.0 0.1 and.74
  31.1 0.1 and.75
  31.4 0.1 add.97
  31.6 0.2 slice_reduce_fusion
  31.7 0.6 gather_fusion.1
  32.5 1.7 %fusion.34 = (bf16[1,64,16,512]{3,2,1,0:T(8,128)(2,1)S(1)}, bf16[1,64,16,512]{3,2,1,0:T(8,128)(2,1)S(1)}) fusion(bf16[2,64,16,512]{3,2,1,0:T(8,128)(2,1)} %collective-permute-done.1), kind=kLoop, calls=%fused_computation.141 | loop fusion | bytes 4194304 | tf_op jit(solution)/shard_map/slice | solution.py:114
  34.2 0.2 convolution_bitcast_fusion.4
  34.4 0.2 convolution_bitcast_fusion.5
  34.6 0.2 convolution_bitcast_fusion.6
  34.8 0.2 convolution_bitcast_fusion.7
  35.1 0.2 select_reduce_fusion
  35.3 0.4 fusion.12
  35.7 0.3 divide_convert_fusion
  36.0 0.3 copy-done.2
  36.3 0.2 convolution_bitcast_fusion.11
  36.5 0.2 convolution_bitcast_fusion.10
  36.6 0.2 convolution_bitcast_fusion.9
  36.8 0.2 convolution_bitcast_fusion.8
  37.0 0.2 convolution_bitcast_fusion.15
  37.1 0.2 convolution_bitcast_fusion.14
  37.3 0.2 convolution_bitcast_fusion.13
  37.5 0.2 convolution_bitcast_fusion.12
  37.8 6.4 %collective-permute-start.2 = (bf16[2,4096]{1,0:T(2,128)(2,1)S(1)}, bf16[2,4096]{1,0:T(2,128)(2,1)S(1)}, u32[]{:S(2)}, u32[]{:S(2)}) collective-permute-start(bf16[2,4096]{1,0:T(2,128)(2,1)S(1)} %get-tuple-element.22), channel_id=1, source_target_pairs={{0,1},{1,0},{2,3},{3,2},{4,5},{5,4},{6,7},{7,6},{8,9},{9,8},{10,11... | collective-permute-start | bytes 49160 | tf_op jit(solution)/shard_map/ppermute | solution.py:211
  44.4 0.9 collective-permute-done.2
  45.3 0.2 multiply_reduce_fusion.4
  45.5 0.1 multiply_convert_fusion.2
  45.6 2.0 %convolution_convert_fusion = bf16[4096,256]{1,0:T(8,128)(2,1)} fusion(s32[4096]{0:T(1024)S(1)} %eq.80, bf16[8,8,2,128]{3,2,1,0:T(2,128)(2,1)S(1)} %bitcast.246), kind=kOutput, calls=%fused_computation.6 | convolution fusion | flops 135528448 | bytes 2146304 | tf_op jit(solution)/shard_map/dot_general | solution.py:237
  47.6 47.7 %shard_map.163 = bf16[128,32,256]{2,1,0:T(8,128)(2,1)} custom-call(bf16[128,32,256]{2,1,0:T(8,128)(2,1)} %bitcast.213), custom_call_target="tpu_custom_call" | custom-call | tf_op jit(solution)/shard_map/pallas_call | solution.py:73
  95.3 1.9 %fusion.32 = (bf16[128,32,128]{2,1,0:T(8,128)(2,1)S(1)}, bf16[128,32,128]{2,1,0:T(8,128)(2,1)S(1)}) fusion(bf16[128,32,256]{2,1,0:T(8,128)(2,1)} %shard_map.163), kind=kLoop, calls=%fused_computation.139 | loop fusion | bytes 4194304 | tf_op jit(solution)/shard_map/slice | solution.py:244
  97.3 0.7 multiply_reduce_fusion
  98.0 0.7 multiply_reduce_fusion.2
  98.7 0.5 copy-done.9
  99.2 0.7 multiply_reduce_fusion.1
  99.9 0.7 multiply_reduce_fusion.3
  100.7 0.7 fusion
  101.4 0.2 slice_bitcast_fusion.1
  101.6 0.2 copy.68
  101.9 0.2 copy.69
  102.1 1.7 %pad_maximum_fusion.x_ref = bf16[128,32,256]{2,1,0:T(8,128)(2,1)} fusion(bf16[128,32,128]{2,1,0:T(8,128)(2,1)S(1)} %bitcast.234, bf16[128,32,128]{2,1,0:T(8,128)(2,1)S(1)} %bitcast.232), kind=kLoop, calls=%fused_computation.7 | loop fusion | flops 4194304 | bytes 4194304 | tf_op jit(solution)/shard_map/concatenate | solution.py:255
  103.8 38.1 %shard_map.164 = bf16[128,32,256]{2,1,0:T(8,128)(2,1)} custom-call(bf16[128,32,256]{2,1,0:T(8,128)(2,1)} %pad_maximum_fusion.x_ref), custom_call_target="tpu_custom_call" | custom-call | tf_op jit(solution)/shard_map/pallas_call | solution.py:73
  141.9 1.9 %fusion.31 = (bf16[128,32,128]{2,1,0:T(8,128)(2,1)S(1)}, bf16[128,32,128]{2,1,0:T(8,128)(2,1)S(1)}) fusion(bf16[128,32,256]{2,1,0:T(8,128)(2,1)} %shard_map.164), kind=kLoop, calls=%fused_computation.138 | loop fusion | bytes 4194304 | tf_op jit(solution)/shard_map/slice | solution.py:262
  143.8 0.3 fusion.7
  144.1 0.3 fusion.6
  144.4 0.7 fusion.20
  (59 shorter events, 1.8 us)
Async XLA Ops:
  0.0 97.2 %copy-start = (bf16[1,32,128,128]{3,2,1,0:T(8,128)(2,1)S(1)}, bf16[1,32,128,128]{3,2,1,0:T(8,128)(2,1)}, u32[]{:S(2)}) copy-start(bf16[1,32,128,128]{3,2,1,0:T(8,128)(2,1)} %param.27) | copy-start | bytes 3145732
  1.6 28.7 %collective-permute-start = (s32[4,17]{1,0:T(4,128)S(1)}, s32[4,17]{1,0:T(4,128)S(1)}, u32[]{:S(2)}, u32[]{:S(2)}) collective-permute-start(s32[4,17]{1,0:T(4,128)S(1)} %pad_add_fusion), channel_id=1, source_target_pairs={{0,2},{2,4},{4,6},{6,8},{8,10},{10,12},{12,14},{14,16},{16,18},{18... | collective-permute-start | bytes 824 | tf_op jit(solution)/shard_map/ppermute | solution.py:90
  6.5 26.0 %collective-permute-start.1 = (bf16[2,64,16,512]{3,2,1,0:T(8,128)(2,1)}, bf16[2,64,16,512]{3,2,1,0:T(8,128)(2,1)}, u32[]{:S(2)}, u32[]{:S(2)}) collective-permute-start(bf16[2,64,16,512]{3,2,1,0:T(8,128)(2,1)} %param.20), channel_id=1, source_target_pairs={{0,2},{2,4},{4,6},{6,8},{8,10},{10,12},{12,14},{14,16},{16,18},{18... | collective-permute-start | bytes 6291464 | tf_op jit(solution)/shard_map/ppermute | solution.py:90
  9.9 34.3 %all-to-all-start = ((s32[128,1,64]{2,1,0:T(1,128)}), s32[128,1,64]{2,1,0:T(1,128)S(1)}, u32[]{:S(2)}, u32[]{:S(2)}) async-start(s32[128,1,64]{2,1,0:T(1,128)} %broadcast_in_dim.102), calls=%async_computation | async-start | bytes 131072 | tf_op jit(solution)/shard_map/all_to_all | solution.py:223
  23.5 2.7 %copy-start.4 = (bf16[4,4096]{1,0:T(4,128)(2,1)S(1)}, bf16[4,4096]{1,0:T(4,128)(2,1)}, u32[]{:S(2)}) copy-start(bf16[4,4096]{1,0:T(4,128)(2,1)} %param.17) | copy-start | bytes 98308
  23.5 3.6 %copy-start.1 = (s32[4]{0:T(128)S(1)}, s32[4]{0:T(128)}, u32[]{:S(2)}) copy-start(s32[4]{0:T(128)} %param.22) | copy-start | bytes 52
  26.2 2.0 %copy-start.6 = (bf16[4,512]{1,0:T(4,128)(2,1)S(1)}, bf16[4,512]{1,0:T(4,128)(2,1)}, u32[]{:S(2)}) copy-start(bf16[4,512]{1,0:T(4,128)(2,1)} %param.18) | copy-start | bytes 12292
  26.2 2.1 %copy-start.7 = (bf16[4,512]{1,0:T(4,128)(2,1)S(1)}, bf16[4,512]{1,0:T(4,128)(2,1)}, u32[]{:S(2)}) copy-start(bf16[4,512]{1,0:T(4,128)(2,1)} %param.19) | copy-start | bytes 12292
  26.2 2.1 %copy-start.8 = (f32[1,32]{1,0:T(1,128)S(1)}, f32[1,32]{1,0:T(1,128)}, u32[]{:S(2)}) copy-start(f32[1,32]{1,0:T(1,128)} %param.33) | copy-start | bytes 388
  35.1 1.2 copy-start.2
  36.0 9.3 %copy-start.3 = (bf16[2,8192]{1,0:T(2,128)(2,1)S(1)}, bf16[2,8192]{1,0:T(2,128)(2,1)}, u32[]{:S(2)}) copy-start(bf16[2,8192]{1,0:T(2,128)(2,1)} %param.24) | copy-start | bytes 98308
  36.0 9.5 %copy-start.5 = (f32[8192]{0:T(1024)S(1)}, f32[8192]{0:T(1024)}, u32[]{:S(2)}) copy-start(f32[8192]{0:T(1024)} %param.25) | copy-start | bytes 98308
  37.8 7.5 %collective-permute-start.2 = (bf16[2,4096]{1,0:T(2,128)(2,1)S(1)}, bf16[2,4096]{1,0:T(2,128)(2,1)S(1)}, u32[]{:S(2)}, u32[]{:S(2)}) collective-permute-start(bf16[2,4096]{1,0:T(2,128)(2,1)S(1)} %get-tuple-element.22), channel_id=1, source_target_pairs={{0,1},{1,0},{2,3},{3,2},{4,5},{5,4},{6,7},{7,6},{8,9},{9,8},{10,11... | collective-permute-start | bytes 49160 | tf_op jit(solution)/shard_map/ppermute | solution.py:211
  95.3 1.9 %copy-start.10 = (f32[1,32]{1,0:T(1,128)S(1)}, f32[1,32]{1,0:T(1,128)}, u32[]{:S(2)}) copy-start(f32[1,32]{1,0:T(1,128)} %param.30) | copy-start | bytes 388
  98.0 1.2 copy-start.9
  98.0 1.2 copy-start.11

commit v18 on v16

--- a/solution.py
+++ b/solution.py
@@ -233,20 +233,21 @@
     rows = normed.shape[0]
     blocks = jnp.arange(feature_blocks, dtype=jnp.int32)
     choose = (in_keep.reshape(peers * keep, 1) == blocks[None, :]).astype(jnp.bfloat16)
-    by_block = jnp.swapaxes(normed.reshape(rows, feature_blocks, BLK), 0, 1)
-    outgoing = jnp.dot(
-        choose, by_block.reshape(feature_blocks, rows * BLK), preferred_element_type=jnp.float32
-    ).astype(jnp.bfloat16)
-    picked = exchange(outgoing.reshape(peers, keep, rows * BLK), gather_route, Z_LANES)
-    hidden = jnp.concatenate(
+    normed_blocks = normed.reshape(rows, feature_blocks, BLK)
+    outgoing = jnp.stack(
         [
-            hidden_units(
-                picked[:, :, r * BLK : (r + 1) * BLK], gate_blocks, up_blocks, gate_scale, up_scale
-            )
+            jnp.dot(choose, normed_blocks[r], preferred_element_type=jnp.float32)
+            .astype(jnp.bfloat16)
+            .reshape(peers, keep, BLK)
             for r in range(rows)
         ],
-        axis=0,
-    )
+        axis=1,
+    ).reshape(peers, rows * keep, BLK)
+    picked = exchange(outgoing, gather_route, Z_LANES)
+    hidden = hidden_units(
+        picked.reshape(peers * rows, keep, BLK), gate_blocks, up_blocks, gate_scale, up_scale
+    )
+    hidden = jnp.swapaxes(hidden.reshape(peers, rows, BLK), 0, 1).reshape(peers * rows, BLK)
     down_flat = jnp.swapaxes(down_blocks[0], 0, 1).reshape(BLK, keep * BLK)
     down_part = jnp.dot(hidden, down_flat, preferred_element_type=jnp.float32)
     column_scale = jnp.repeat(down_scale[0], BLK)

time: 146 us -> 149 us (1.021)
  matrix products: 9.13 us -> 13 us
  local copies, waits for them, and re-layouts: 17.5 us -> 15.3 us
  other arithmetic: 6.69 us -> 8.33 us
    dot_general x1 -> x2, matrix products: 2.04 us -> 4.46 us  [per_device(): jnp.dot(choose, normed_blocks[r], preferred_element_type=jnp.float32)]
    slice x1, local copies, waits for them, and re-layouts: 1.91 us -> 0.18 us  [per_device(): normed_blocks[r]]
    dot_general x2 -> x1, matrix products: 1.45 us -> 3 us  [hidden_units(): jnp.einsum('skd,kdf->ksf', picked, gate_blocks[0], preferred_element_type...]
    another operation x0 -> x1, other arithmetic: none -> 1.54 us  [per_device(): jnp.stack([jnp.dot(choose, normed_blocks[r], preferred_element_type=jnp.f...]
    unnamed x30 -> x32, local copies, waits for them, and re-layouts: 3.15 us -> 2.66 us
where the time goes in v18:
time: 149 us; the launch traced here: 147 us
  Pallas kernels  84.4 us (57%)
  starting transfers between devices  24.7 us (17%)
  local copies, waits for them, and re-layouts  15.3 us (10%)
  matrix products  13 us (9%)
  other arithmetic  8.33 us (6%)
    pallas_call x2, Pallas kernels, exchange(): pl.pallas_call(functools.partial(exchange_kernel, route, lanes), out_shap...  84.4 us
    all_to_all x1, starting transfers between devices, per_device(): lax.all_to_all(jnp.broadcast_to(own_lists, (peers, own_lists.shape[1])),...  11.5 us
    ppermute x2, starting transfers between devices, shifted(): return lax.ppermute(block, axis, route)  6.85 us
    ppermute x1, starting transfers between devices, per_device(): arrived_half = lax.ppermute(theirs, 'head', [(0, 1), (1, 0)])  6.35 us
    dot_general x2, matrix products, per_device(): jnp.dot(choose, normed_blocks[r], preferred_element_type=jnp.float32)  4.46 us
    dot_general x1, matrix products, hidden_units(): jnp.einsum('skd,kdf->ksf', picked, gate_blocks[0], preferred_element_type...  3 us
  transfers between devices with their start and end apart: 4, of which 1 were waited for; matrix products, arithmetic and copies ran while one was open for 12% of the time, Pallas kernels for 0%

profile of v18, /device:TPU:1, one launch (start us, length us, event | category | flops | bytes accessed | tf_op | source)
XLA Modules:
  0.0 147.0 jit_solution(15565663340230935462)
XLA Ops:
  0.0 0.8 copy.62
  0.8 0.8 pad_add_fusion
  1.6 4.9 %collective-permute-start = (s32[4,17]{1,0:T(4,128)S(1)}, s32[4,17]{1,0:T(4,128)S(1)}, u32[]{:S(2)}, u32[]{:S(2)}) collective-permute-start(s32[4,17]{1,0:T(4,128)S(1)} %pad_add_fusion), channel_id=1, source_target_pairs={{0,2},{2,4},{4,6},{6,8},{8,10},{10,12},{12,14},{14,16},{16,18},{18... | collective-permute-start | bytes 824 | tf_op jit(solution)/shard_map/ppermute | solution.py:90
  6.5 1.9 %collective-permute-start.1 = (bf16[2,64,16,512]{3,2,1,0:T(8,128)(2,1)}, bf16[2,64,16,512]{3,2,1,0:T(8,128)(2,1)}, u32[]{:S(2)}, u32[]{:S(2)}) collective-permute-start(bf16[2,64,16,512]{3,2,1,0:T(8,128)(2,1)} %param.20), channel_id=1, source_target_pairs={{0,2},{2,4},{4,6},{6,8},{8,10},{10,12},{12,14},{14,16},{16,18},{18... | collective-permute-start | bytes 6291464 | tf_op jit(solution)/shard_map/ppermute | solution.py:90
  8.5 0.7 add_bitcast_fusion.1
  9.2 0.7 broadcast_in_dim.102
  9.9 11.5 %all-to-all-start = ((s32[128,1,64]{2,1,0:T(1,128)}), s32[128,1,64]{2,1,0:T(1,128)S(1)}, u32[]{:S(2)}, u32[]{:S(2)}) async-start(s32[128,1,64]{2,1,0:T(1,128)} %broadcast_in_dim.102), calls=%async_computation | async-start | bytes 131072 | tf_op jit(solution)/shard_map/all_to_all | solution.py:223
  21.3 0.7 broadcast_compare_fusion.1
  22.0 1.2 gather_fusion.2
  23.5 2.7 %fusion.28 = (bf16[1,64,16,512]{3,2,1,0:T(8,128)(2,1)}, bf16[1,64,16,512]{3,2,1,0:T(8,128)(2,1)S(1)}) fusion(bf16[2,64,16,512]{3,2,1,0:T(8,128)(2,1)} %param.20), kind=kLoop, calls=%fused_computation.136 | loop fusion | bytes 4194304 | tf_op jit(solution)/shard_map/slice | solution.py:145
  26.2 0.2 convolution_bitcast_fusion
  26.4 0.2 convolution_bitcast_fusion.1
  26.6 0.2 convolution_bitcast_fusion.2
  26.9 0.2 convolution_bitcast_fusion.3
  27.1 0.6 gather_fusion.3
  27.9 0.1 and.80
  28.1 0.1 add.98
  28.4 0.1 fusion.31
  28.6 1.6 %copy.74 = bf16[1,32,128,128]{2,3,1,0:T(8,128)(2,1)S(1)} copy(bf16[1,32,128,128]{3,2,1,0:T(8,128)(2,1)} %param.31) | data formatting | bytes 2097152 | tf_op args[14]
  30.3 0.6 gather_fusion
  31.0 0.1 and.74
  31.1 0.1 and.75
  31.4 0.1 add.95
  31.6 0.2 slice_reduce_fusion.2
  31.7 0.6 gather_fusion.1
  32.5 1.7 %fusion.29 = (bf16[1,64,16,512]{3,2,1,0:T(8,128)(2,1)S(1)}, bf16[1,64,16,512]{3,2,1,0:T(8,128)(2,1)S(1)}) fusion(bf16[2,64,16,512]{3,2,1,0:T(8,128)(2,1)} %collective-permute-done.1), kind=kLoop, calls=%fused_computation.137 | loop fusion | bytes 4194304 | tf_op jit(solution)/shard_map/slice | solution.py:114
  34.2 0.2 convolution_bitcast_fusion.4
  34.4 0.2 convolution_bitcast_fusion.5
  34.6 0.2 convolution_bitcast_fusion.6
  34.8 0.2 convolution_bitcast_fusion.7
  35.1 0.2 select_reduce_fusion
  35.3 0.4 fusion.9
  35.7 0.3 divide_convert_fusion
  36.0 0.3 copy-done.2
  36.3 0.2 convolution_bitcast_fusion.11
  36.5 0.2 convolution_bitcast_fusion.10
  36.6 0.2 convolution_bitcast_fusion.9
  36.8 0.2 convolution_bitcast_fusion.8
  37.0 0.2 convolution_bitcast_fusion.15
  37.1 0.2 convolution_bitcast_fusion.14
  37.3 0.2 convolution_bitcast_fusion.13
  37.5 0.2 convolution_bitcast_fusion.12
  37.8 6.4 %collective-permute-start.2 = (bf16[2,4096]{1,0:T(2,128)(2,1)S(1)}, bf16[2,4096]{1,0:T(2,128)(2,1)S(1)}, u32[]{:S(2)}, u32[]{:S(2)}) collective-permute-start(bf16[2,4096]{1,0:T(2,128)(2,1)S(1)} %get-tuple-element.22), channel_id=1, source_target_pairs={{0,1},{1,0},{2,3},{3,2},{4,5},{5,4},{6,7},{7,6},{8,9},{9,8},{10,11... | collective-permute-start | bytes 49160 | tf_op jit(solution)/shard_map/ppermute | solution.py:211
  44.4 0.9 collective-permute-done.2
  45.3 0.2 multiply_reduce_fusion.2
  45.5 0.1 multiply_convert_fusion
  45.6 0.2 slice_reduce_fusion.1
  45.8 2.2 %convolution_convert_fusion.1 = bf16[4096,128]{1,0:T(8,128)(2,1)S(1)} fusion(s32[4096]{0:T(1024)S(1)} %eq.80, bf16[8192]{0:T(1024)(128)(2,1)S(1)} %get-tuple-element.5), kind=kOutput, calls=%fused_computation.7 | convolution fusion | flops 67895296 | bytes 1081344 | tf_op jit(solution)/shard_map/dot_general | solution.py:239
  48.0 2.2 %convolution_convert_fusion = bf16[4096,128]{1,0:T(8,128)(2,1)S(1)} fusion(s32[4096]{0:T(1024)S(1)} %eq.80, bf16[8192]{0:T(1024)(128)(2,1)S(1)} %get-tuple-element.6), kind=kOutput, calls=%fused_computation.6 | convolution fusion | flops 67895296 | bytes 1081344 | tf_op jit(solution)/shard_map/dot_general | solution.py:239
  50.2 1.5 %pad_maximum_fusion = bf16[128,2,32,128]{3,2,1,0:T(8,128)(2,1)} fusion(bf16[128,1,32,128]{3,2,1,0:T(8,128)(2,1)S(1)} %bitcast.242, bf16[128,1,32,128]{3,2,1,0:T(8,128)(2,1)S(1)} %bitcast.239), kind=kLoop, calls=%fused_computation.10 | loop fusion | flops 1048576 | bytes 4194304 | tf_op jit(solution)/shard_map/stack | solution.py:237
  51.8 48.9 %shard_map.163 = bf16[128,64,128]{2,1,0:T(8,128)(2,1)} custom-call(bf16[128,64,128]{2,1,0:T(8,128)(2,1)} %bitcast.221), custom_call_target="tpu_custom_call" | custom-call | tf_op jit(solution)/shard_map/pallas_call | solution.py:73
  100.7 3.0 %multiply_reduce_fusion.1 = f32[256,128]{1,0:T(8,128)S(1)} fusion(f32[32]{0:T(128)S(1)} %bitcast.266, bf16[256,32,128]{2,1,0:T(8,128)(2,1)} %bitcast.245, bf16[1,32,128,128]{3,2,1,0:T(8,128)(2,1)S(1)} %copy-done), kind=kOutput, calls=%fused_computation.9 | convolution fusion | flops 270499840 | bytes 3276928 | tf_op jit(solution)/shard_map/skd,kdf->ksf/dot_general | solution.py:163
  103.8 1.3 multiply_reduce_fusion
  105.0 0.1 fusion.17
  105.2 0.7 fusion
  105.9 0.2 slice_bitcast_fusion.1
  106.1 0.2 copy.84
  106.4 0.2 copy.83
  106.6 1.7 %pad_maximum_fusion.1.x_ref = bf16[128,32,256]{2,1,0:T(8,128)(2,1)} fusion(bf16[128,32,128]{2,1,0:T(8,128)(2,1)S(1)} %bitcast.241, bf16[128,32,128]{2,1,0:T(8,128)(2,1)S(1)} %bitcast.244), kind=kLoop, calls=%fused_computation.11 | loop fusion | flops 4194304 | bytes 4194304 | tf_op jit(solution)/shard_map/concatenate | solution.py:256
  108.3 35.5 %shard_map.164 = bf16[128,32,256]{2,1,0:T(8,128)(2,1)} custom-call(bf16[128,32,256]{2,1,0:T(8,128)(2,1)} %pad_maximum_fusion.1.x_ref), custom_call_target="tpu_custom_call" | custom-call | tf_op jit(solution)/shard_map/pallas_call | solution.py:73
  143.8 1.9 %fusion.27 = (bf16[128,32,128]{2,1,0:T(8,128)(2,1)S(1)}, bf16[128,32,128]{2,1,0:T(8,128)(2,1)S(1)}) fusion(bf16[128,32,256]{2,1,0:T(8,128)(2,1)} %shard_map.164), kind=kLoop, calls=%fused_computation.135 | loop fusion | bytes 4194304 | tf_op jit(solution)/shard_map/slice | solution.py:263
  145.7 0.3 fusion.8
  146.0 0.3 fusion.7
  146.3 0.7 fusion.16
  (62 shorter events, 1.8 us)
Async XLA Ops:
  0.0 100.7 %copy-start = (bf16[1,32,128,128]{3,2,1,0:T(8,128)(2,1)S(1)}, bf16[1,32,128,128]{3,2,1,0:T(8,128)(2,1)}, u32[]{:S(2)}) copy-start(bf16[1,32,128,128]{3,2,1,0:T(8,128)(2,1)} %param.26) | copy-start | bytes 3145732
  1.6 28.7 %collective-permute-start = (s32[4,17]{1,0:T(4,128)S(1)}, s32[4,17]{1,0:T(4,128)S(1)}, u32[]{:S(2)}, u32[]{:S(2)}) collective-permute-start(s32[4,17]{1,0:T(4,128)S(1)} %pad_add_fusion), channel_id=1, source_target_pairs={{0,2},{2,4},{4,6},{6,8},{8,10},{10,12},{12,14},{14,16},{16,18},{18... | collective-permute-start | bytes 824 | tf_op jit(solution)/shard_map/ppermute | solution.py:90
  6.5 26.0 %collective-permute-start.1 = (bf16[2,64,16,512]{3,2,1,0:T(8,128)(2,1)}, bf16[2,64,16,512]{3,2,1,0:T(8,128)(2,1)}, u32[]{:S(2)}, u32[]{:S(2)}) collective-permute-start(bf16[2,64,16,512]{3,2,1,0:T(8,128)(2,1)} %param.20), channel_id=1, source_target_pairs={{0,2},{2,4},{4,6},{6,8},{8,10},{10,12},{12,14},{14,16},{16,18},{18... | collective-permute-start | bytes 6291464 | tf_op jit(solution)/shard_map/ppermute | solution.py:90
  9.9 34.3 %all-to-all-start = ((s32[128,1,64]{2,1,0:T(1,128)}), s32[128,1,64]{2,1,0:T(1,128)S(1)}, u32[]{:S(2)}, u32[]{:S(2)}) async-start(s32[128,1,64]{2,1,0:T(1,128)} %broadcast_in_dim.102), calls=%async_computation | async-start | bytes 131072 | tf_op jit(solution)/shard_map/all_to_all | solution.py:223
  23.5 2.7 %copy-start.5 = (bf16[4,4096]{1,0:T(4,128)(2,1)S(1)}, bf16[4,4096]{1,0:T(4,128)(2,1)}, u32[]{:S(2)}) copy-start(bf16[4,4096]{1,0:T(4,128)(2,1)} %param.17) | copy-start | bytes 98308
  23.5 3.6 %copy-start.1 = (s32[4]{0:T(128)S(1)}, s32[4]{0:T(128)}, u32[]{:S(2)}) copy-start(s32[4]{0:T(128)} %param.22) | copy-start | bytes 52
  26.2 2.0 %copy-start.7 = (bf16[4,512]{1,0:T(4,128)(2,1)S(1)}, bf16[4,512]{1,0:T(4,128)(2,1)}, u32[]{:S(2)}) copy-start(bf16[4,512]{1,0:T(4,128)(2,1)} %param.18) | copy-start | bytes 12292
  26.2 2.1 %copy-start.8 = (bf16[4,512]{1,0:T(4,128)(2,1)S(1)}, bf16[4,512]{1,0:T(4,128)(2,1)}, u32[]{:S(2)}) copy-start(bf16[4,512]{1,0:T(4,128)(2,1)} %param.19) | copy-start | bytes 12292
  26.2 2.1 %copy-start.9 = (f32[1,32]{1,0:T(1,128)S(1)}, f32[1,32]{1,0:T(1,128)}, u32[]{:S(2)}) copy-start(f32[1,32]{1,0:T(1,128)} %param.33) | copy-start | bytes 388
  35.1 1.2 copy-start.2
  36.0 9.3 %copy-start.4 = (bf16[2,8192]{1,0:T(2,128)(2,1)S(1)}, bf16[2,8192]{1,0:T(2,128)(2,1)}, u32[]{:S(2)}) copy-start(bf16[2,8192]{1,0:T(2,128)(2,1)} %param.24) | copy-start | bytes 98308
  36.0 9.5 %copy-start.6 = (f32[8192]{0:T(1024)S(1)}, f32[8192]{0:T(1024)}, u32[]{:S(2)}) copy-start(f32[8192]{0:T(1024)} %param.25) | copy-start | bytes 98308
  37.8 7.5 %collective-permute-start.2 = (bf16[2,4096]{1,0:T(2,128)(2,1)S(1)}, bf16[2,4096]{1,0:T(2,128)(2,1)S(1)}, u32[]{:S(2)}, u32[]{:S(2)}) collective-permute-start(bf16[2,4096]{1,0:T(2,128)(2,1)S(1)} %get-tuple-element.22), channel_id=1, source_target_pairs={{0,1},{1,0},{2,3},{3,2},{4,5},{5,4},{6,7},{7,6},{8,9},{9,8},{10,11... | collective-permute-start | bytes 49160 | tf_op jit(solution)/shard_map/ppermute | solution.py:211
  51.8 48.9 %copy-start.11 = (f32[1,32]{1,0:T(1,128)S(1)}, f32[1,32]{1,0:T(1,128)}, u32[]{:S(2)}) copy-start(f32[1,32]{1,0:T(1,128)} %param.29) | copy-start | bytes 388
  100.7 3.0 %copy-start.3 = (bf16[128,64,128]{2,1,0:T(8,128)(2,1)S(1)}, bf16[128,64,128]{2,1,0:T(8,128)(2,1)}, u32[]{:S(2)}) copy-start(bf16[128,64,128]{2,1,0:T(8,128)(2,1)} %shard_map.163) | copy-start | bytes 6291460
  100.7 3.0 %copy-start.10 = (bf16[1,32,128,128]{3,2,1,0:T(8,128)(2,1)S(1)}, bf16[1,32,128,128]{3,2,1,0:T(8,128)(2,1)}, u32[]{:S(2)}) copy-start(bf16[1,32,128,128]{3,2,1,0:T(8,128)(2,1)} %param.27) | copy-start | bytes 3145732
  100.7 3.0 %copy-start.12 = (f32[1,32]{1,0:T(1,128)S(1)}, f32[1,32]{1,0:T(1,128)}, u32[]{:S(2)}) copy-start(f32[1,32]{1,0:T(1,128)} %param.30) | copy-start | bytes 388
